TPU v7x, 512 devices: a whole 4x8x8 slice. The times are simulated.
512 devices in a mesh: bx: 16 (over z_hi, x, core), by: 32 (over z_lo, y).
Axes of the slice: x: 4, y: 8, z: 8 (z_hi: 2, z_lo: 4; z = z_hi * 4 + z_lo), core: 2. Of those that a mesh axis runs over, the one named last changes fastest.
Arguments:
- sources: bfloat16 [32, 16, 32, 1024], P(None, 'bx', 'by'), may hold values from -6 to 6
- near_blocks: bfloat16 [16, 32, 8, 9, 128, 128], P('bx', 'by'), may hold values from -0.1875 to 0.1875
- near_index: int32 [16, 32, 8, 9], P('bx', 'by'), may hold values from 0 to 7
- far_project: bfloat16 [16, 32, 1024, 128], P('bx', 'by'), may hold values from -0.1875 to 0.1875
- far_mixing: bfloat16 [16, 32, 9, 2, 128, 128], P('bx', 'by'), may hold values from -0.375 to 0.375
- far_expand: bfloat16 [16, 32, 128, 1024], P('bx', 'by'), may hold values from -0.5 to 0.5
Outputs:
- response: float32 [32, 16, 32, 1024], P(None, 'bx', 'by')
Inputs may be any that keep to these rules, and one draw needn't show every extreme that they name: `near_index`: entry k of a block row's list names a block of the box at neighbour position k.
All inputs are finite; a program needn't handle non-finite values.
Results may differ from a plain program's by a relative error of at most 0.012.
Values may be sent and summed in bfloat16 or wider, within the bound.
No kernel may reach another device: no remote copies, remote signals or barrier semaphores. Data moves between devices by JAX's collectives and lax.ppermute only.
A program may use at most 64 MiB of HBM per device.

v0:
```python
import jax
import jax.numpy as jnp
from jax import lax
from jax.sharding import PartitionSpec as P


def with_halo(block, sides, width):
    for axis, dim in sides:
        count = lax.axis_size(axis)
        forward = [(i, i + 1) for i in range(count - 1)]
        backward = [(target, source) for source, target in forward]
        low = lax.ppermute(
            lax.slice_in_dim(block, block.shape[dim] - width, None, axis=dim), axis, forward
        )
        high = lax.ppermute(lax.slice_in_dim(block, 0, width, axis=dim), axis, backward)
        block = jnp.concatenate([low, block, high], axis=dim)
    return block


def swapped(array, axis, apart):
    return lax.ppermute(array, axis, [(i, i ^ 1 << apart) for i in range(lax.axis_size(axis))])


def near_field(sources, near_blocks, near_index):
    excite = sources.shape[0]
    blocks = near_blocks.shape[2]
    positions = near_blocks.shape[3]
    block_len = near_blocks.shape[4]
    beside_all = with_halo(sources, (("bx", 1), ("by", 2)), 1)
    source_blocks = beside_all.reshape(excite, positions, blocks, block_len)
    onehot = (
        near_index[0, 0][:, :, None] == jnp.arange(blocks, dtype=jnp.int32)[None, None, :]
    ).astype(jnp.bfloat16)
    picked = jnp.einsum(
        "rkb,ckbj->rkcj", onehot, source_blocks, preferred_element_type=jnp.float32
    ).astype(jnp.bfloat16)
    near_sum = jnp.einsum(
        "rkij,rkcj->cri", near_blocks[0, 0], picked, preferred_element_type=jnp.float32
    )
    return near_sum.reshape(excite, 1, 1, blocks * block_len)


def mix_level(coeffs, partner, mixing):
    own_term = jnp.dot(coeffs, mixing[0], preferred_element_type=jnp.float32)
    other_term = jnp.dot(partner, mixing[1], preferred_element_type=jnp.float32)
    return (own_term + other_term).astype(jnp.bfloat16)


def far_field(sources, far_project, far_mixing, far_expand):
    excite = sources.shape[0]
    unknowns = sources.shape[3]
    coeffs = jnp.dot(
        sources[:, 0, 0], far_project[0, 0], preferred_element_type=jnp.float32
    ).astype(jnp.bfloat16)
    levels_first = lax.axis_size("bx").bit_length() - 1
    levels_second = lax.axis_size("by").bit_length() - 1
    for level_num in range(levels_first):
        partner = swapped(coeffs, "bx", level_num)
        coeffs = mix_level(coeffs, partner, far_mixing[0, 0, level_num])
    for level_num in range(levels_second):
        partner = swapped(coeffs, "by", level_num)
        coeffs = mix_level(coeffs, partner, far_mixing[0, 0, levels_first + level_num])
    far_sum = jnp.dot(coeffs, far_expand[0, 0], preferred_element_type=jnp.float32)
    return far_sum.reshape(excite, 1, 1, unknowns)


def per_device(sources, near_blocks, near_index, far_project, far_mixing, far_expand):
    near_part = near_field(sources, near_blocks, near_index)
    far_part = far_field(sources, far_project, far_mixing, far_expand)
    return near_part + far_part


def solution(mesh):
    placed = (
        P(None, "bx", "by", None),
        P("bx", "by", None, None, None, None),
        P("bx", "by", None, None),
        P("bx", "by", None, None),
        P("bx", "by", None, None, None, None),
        P("bx", "by", None, None),
    )
    return jax.shard_map(
        per_device, mesh=mesh, in_specs=placed, out_specs=P(None, "bx", "by", None), check_vma=False
    )
```

profile of v0, /device:TPU:62, one launch (start us, length us, event | category | flops | bytes accessed | tf_op | source)
XLA Modules:
  0.0 91.2 jit_solution(14612568294518254306)
XLA Ops:
  0.0 0.0 copy-start
  0.0 2.3 %collective-permute-start.1 = (bf16[32,1,1,1024]{3,0,2,1:T(8,128)(2,1)}, bf16[32,1,1,1024]{3,0,2,1:T(8,128)(2,1)S(1)}, u32[]{:S(2)}, u32[]{:S(2)}) collective-permute-start(bf16[32,1,1,1024]{3,0,2,1:T(8,128)(2,1)} %param.6), channel_id=1, source_target_pairs={{32,0},{64,32},{96,64},{128,96},{160,128},{192,160},{224,192},{256... | collective-permute-start | bytes 196616 | tf_op jit(solution)/shard_map/ppermute | solution.py:15
  2.3 2.2 %collective-permute-start = (bf16[32,1,1,1024]{3,0,2,1:T(8,128)(2,1)}, bf16[32,1,1,1024]{3,0,2,1:T(8,128)(2,1)S(1)}, u32[]{:S(2)}, u32[]{:S(2)}) collective-permute-start(bf16[32,1,1,1024]{3,0,2,1:T(8,128)(2,1)} %param.6), channel_id=1, source_target_pairs={{0,32},{32,64},{64,96},{96,128},{128,160},{160,192},{192,224},{224... | collective-permute-start | bytes 196616 | tf_op jit(solution)/shard_map/ppermute | solution.py:12
  4.5 1.2 %convolution_convert_fusion = bf16[32,128]{1,0:T(8,128)(2,1)S(1)} fusion(bf16[1,1,1024,128]{3,2,1,0:T(8,128)(2,1)} %param.9, bf16[32,1,1,1024]{3,0,2,1:T(8,128)(2,1)} %param.6), kind=kOutput, calls=%fused_computation.24 | convolution fusion | flops 8392704 | bytes 335872 | tf_op jit(solution)/shard_map/dot_general | solution.py:52
  5.6 10.4 %collective-permute-start.4 = (bf16[32,128]{1,0:T(8,128)(2,1)S(1)}, bf16[32,128]{1,0:T(8,128)(2,1)S(1)}, u32[]{:S(2)}, u32[]{:S(2)}) collective-permute-start(bf16[32,128]{1,0:T(8,128)(2,1)S(1)} %convolution_convert_fusion), channel_id=1, source_target_pairs={{0,32},{32,0},{64,96},{96,64},{128,160},{160,128},{192,224},{224,1... | collective-permute-start | bytes 24584 | tf_op jit(solution)/shard_map/ppermute | solution.py:21
  16.1 0.9 fusion.49
  17.0 0.8 fusion.20
  17.8 0.0 collective-permute-done.4
  17.8 0.9 fusion.6
  18.7 1.9 %collective-permute-start.5 = (bf16[32,128]{1,0:T(8,128)(2,1)S(1)}, bf16[32,128]{1,0:T(8,128)(2,1)S(1)}, u32[]{:S(2)}, u32[]{:S(2)}) collective-permute-start(bf16[32,128]{1,0:T(8,128)(2,1)S(1)} %fusion.6), channel_id=1, source_target_pairs={{0,64},{32,96},{64,0},{96,32},{128,192},{160,224},{192,128},{224,1... | collective-permute-start | bytes 24584 | tf_op jit(solution)/shard_map/ppermute | solution.py:21
  20.6 0.9 fusion.46
  21.5 2.7 %collective-permute-done.5 = bf16[32,128]{1,0:T(8,128)(2,1)S(1)} collective-permute-done((bf16[32,128]{1,0:T(8,128)(2,1)S(1)}, bf16[32,128]{1,0:T(8,128)(2,1)S(1)}, u32[]{:S(2)}, u32[]{:S(2)}) %collective-permute-start.5) | collective-permute-done | bytes 8224 | tf_op jit(solution)/shard_map/ppermute | solution.py:21
  24.2 0.9 fusion.7
  25.1 1.9 %collective-permute-start.6 = (bf16[32,128]{1,0:T(8,128)(2,1)S(1)}, bf16[32,128]{1,0:T(8,128)(2,1)S(1)}, u32[]{:S(2)}, u32[]{:S(2)}) collective-permute-start(bf16[32,128]{1,0:T(8,128)(2,1)S(1)} %fusion.7), channel_id=1, source_target_pairs={{0,128},{32,160},{64,192},{96,224},{128,0},{160,32},{192,64},{224,... | collective-permute-start | bytes 24584 | tf_op jit(solution)/shard_map/ppermute | solution.py:21
  27.0 0.9 fusion.43
  27.9 4.2 %collective-permute-done.6 = bf16[32,128]{1,0:T(8,128)(2,1)S(1)} collective-permute-done((bf16[32,128]{1,0:T(8,128)(2,1)S(1)}, bf16[32,128]{1,0:T(8,128)(2,1)S(1)}, u32[]{:S(2)}, u32[]{:S(2)}) %collective-permute-start.6) | collective-permute-done | bytes 8224 | tf_op jit(solution)/shard_map/ppermute | solution.py:21
  32.1 0.9 fusion.8
  33.0 2.4 %collective-permute-start.7 = (bf16[32,128]{1,0:T(8,128)(2,1)S(1)}, bf16[32,128]{1,0:T(8,128)(2,1)S(1)}, u32[]{:S(2)}, u32[]{:S(2)}) collective-permute-start(bf16[32,128]{1,0:T(8,128)(2,1)S(1)} %fusion.8), channel_id=1, source_target_pairs={{0,256},{32,288},{64,320},{96,352},{128,384},{160,416},{192,448},{... | collective-permute-start | bytes 24584 | tf_op jit(solution)/shard_map/ppermute | solution.py:21
  35.4 0.9 fusion.40
  36.3 6.2 %collective-permute-done.7 = bf16[32,128]{1,0:T(8,128)(2,1)S(1)} collective-permute-done((bf16[32,128]{1,0:T(8,128)(2,1)S(1)}, bf16[32,128]{1,0:T(8,128)(2,1)S(1)}, u32[]{:S(2)}, u32[]{:S(2)}) %collective-permute-start.7) | collective-permute-done | bytes 8224 | tf_op jit(solution)/shard_map/ppermute | solution.py:21
  42.5 0.9 fusion.9
  43.4 3.3 %collective-permute-start.8 = (bf16[32,128]{1,0:T(8,128)(2,1)S(1)}, bf16[32,128]{1,0:T(8,128)(2,1)S(1)}, u32[]{:S(2)}, u32[]{:S(2)}) collective-permute-start(bf16[32,128]{1,0:T(8,128)(2,1)S(1)} %fusion.9), channel_id=1, source_target_pairs={{0,1},{1,0},{2,3},{3,2},{4,5},{5,4},{6,7},{7,6},{8,9},{9,8},{10,11... | collective-permute-start | bytes 24584 | tf_op jit(solution)/shard_map/ppermute | solution.py:21
  46.6 0.9 fusion.37
  47.5 1.4 %collective-permute-done.8 = bf16[32,128]{1,0:T(8,128)(2,1)S(1)} collective-permute-done((bf16[32,128]{1,0:T(8,128)(2,1)S(1)}, bf16[32,128]{1,0:T(8,128)(2,1)S(1)}, u32[]{:S(2)}, u32[]{:S(2)}) %collective-permute-start.8) | collective-permute-done | bytes 8224 | tf_op jit(solution)/shard_map/ppermute | solution.py:21
  48.9 0.9 fusion.10
  49.8 4.0 %collective-permute-start.9 = (bf16[32,128]{1,0:T(8,128)(2,1)S(1)}, bf16[32,128]{1,0:T(8,128)(2,1)S(1)}, u32[]{:S(2)}, u32[]{:S(2)}) collective-permute-start(bf16[32,128]{1,0:T(8,128)(2,1)S(1)} %fusion.10), channel_id=1, source_target_pairs={{0,2},{1,3},{2,0},{3,1},{4,6},{5,7},{6,4},{7,5},{8,10},{9,11},{10,... | collective-permute-start | bytes 24584 | tf_op jit(solution)/shard_map/ppermute | solution.py:21
  53.8 0.9 fusion.34
  54.7 1.5 %collective-permute-done.9 = bf16[32,128]{1,0:T(8,128)(2,1)S(1)} collective-permute-done((bf16[32,128]{1,0:T(8,128)(2,1)S(1)}, bf16[32,128]{1,0:T(8,128)(2,1)S(1)}, u32[]{:S(2)}, u32[]{:S(2)}) %collective-permute-start.9) | collective-permute-done | bytes 8224 | tf_op jit(solution)/shard_map/ppermute | solution.py:21
  56.2 0.9 fusion.11
  57.1 4.7 %collective-permute-start.10 = (bf16[32,128]{1,0:T(8,128)(2,1)S(1)}, bf16[32,128]{1,0:T(8,128)(2,1)S(1)}, u32[]{:S(2)}, u32[]{:S(2)}) collective-permute-start(bf16[32,128]{1,0:T(8,128)(2,1)S(1)} %fusion.11), channel_id=1, source_target_pairs={{0,4},{1,5},{2,6},{3,7},{4,0},{5,1},{6,2},{7,3},{8,12},{9,13},{10,... | collective-permute-start | bytes 24584 | tf_op jit(solution)/shard_map/ppermute | solution.py:21
  61.8 0.9 fusion.31
  62.7 3.8 %collective-permute-done.10 = bf16[32,128]{1,0:T(8,128)(2,1)S(1)} collective-permute-done((bf16[32,128]{1,0:T(8,128)(2,1)S(1)}, bf16[32,128]{1,0:T(8,128)(2,1)S(1)}, u32[]{:S(2)}, u32[]{:S(2)}) %collective-permute-start.10) | collective-permute-done | bytes 8224 | tf_op jit(solution)/shard_map/ppermute | solution.py:21
  66.6 0.9 fusion.12
  67.4 0.9 fusion.28
  68.3 3.4 %collective-permute-start.11 = (bf16[32,128]{1,0:T(8,128)(2,1)S(1)}, bf16[32,128]{1,0:T(8,128)(2,1)S(1)}, u32[]{:S(2)}, u32[]{:S(2)}) collective-permute-start(bf16[32,128]{1,0:T(8,128)(2,1)S(1)} %fusion.12), channel_id=1, source_target_pairs={{0,8},{1,9},{2,10},{3,11},{4,12},{5,13},{6,14},{7,15},{8,0},{9,1},... | collective-permute-start | bytes 24584 | tf_op jit(solution)/shard_map/ppermute | solution.py:21
  71.7 0.0 collective-permute-done
  71.7 0.8 constant_dynamic-update-slice_fusion.1
  72.6 0.0 collective-permute-done.1
  72.6 3.3 %collective-permute-start.3 = (bf16[32,3,1,1024]{3,0,2,1:T(8,128)(2,1)S(1)}, bf16[32,3,1,1024]{3,0,2,1:T(8,128)(2,1)S(1)}, u32[]{:S(2)}, u32[]{:S(2)}) collective-permute-start(bf16[32,3,1,1024]{3,0,2,1:T(8,128)(2,1)S(1)} %constant_dynamic-update-slice_fusion), channel_id=1, source_target_pairs={{1,0},{2,1},{3,2},{4,3},{5,4},{6,5},{7,6},{8,7},{9,8},{10,9},{11,1... | collective-permute-start | bytes 589832 | tf_op jit(solution)/shard_map/ppermute | solution.py:15
  75.9 4.7 %collective-permute-start.2 = (bf16[32,3,1,1024]{3,0,2,1:T(8,128)(2,1)S(1)}, bf16[32,3,1,1024]{3,0,2,1:T(8,128)(2,1)S(1)}, u32[]{:S(2)}, u32[]{:S(2)}) collective-permute-start(bf16[32,3,1,1024]{3,0,2,1:T(8,128)(2,1)S(1)} %constant_dynamic-update-slice_fusion), channel_id=1, source_target_pairs={{0,1},{1,2},{2,3},{3,4},{4,5},{5,6},{6,7},{7,8},{8,9},{9,10},{10,1... | collective-permute-start | bytes 589832 | tf_op jit(solution)/shard_map/ppermute | solution.py:12
  80.6 0.0 collective-permute-done.11
  80.6 0.9 fusion.13
  81.5 5.5 %collective-permute-start.12 = (bf16[32,128]{1,0:T(8,128)(2,1)S(1)}, bf16[32,128]{1,0:T(8,128)(2,1)S(1)}, u32[]{:S(2)}, u32[]{:S(2)}) collective-permute-start(bf16[32,128]{1,0:T(8,128)(2,1)S(1)} %fusion.13), channel_id=1, source_target_pairs={{0,16},{1,17},{2,18},{3,19},{4,20},{5,21},{6,22},{7,23},{8,24},{9,... | collective-permute-start | bytes 24584 | tf_op jit(solution)/shard_map/ppermute | solution.py:21
  87.0 0.9 fusion.25
  87.9 0.0 collective-permute-done.3
  87.9 0.0 collective-permute-done.2
  87.9 0.1 pad_maximum_fusion
  88.0 0.1 copy.14
  88.1 0.0 copy-start.1
  88.1 0.3 fusion.21
  88.4 0.0 copy-done
  88.4 0.9 fusion.2
  89.3 0.0 collective-permute-done.12
  89.3 0.0 copy-done.1
  89.3 1.0 %fusion.5 = f32[32,1,1,1024]{3,0,2,1:T(8,128)S(1)} fusion(f32[32,128]{1,0:T(8,128)S(1)} %fusion.25, bf16[32,128]{1,0:T(8,128)(2,1)S(1)} %collective-permute-done.12, bf16[1,1,128,1024]{3,2,1,0:T(8,128)(2,1)S(1)} %copy-done.1, f32[8,4,8,128]{3,2,1,0:T(8,128)S(1)} %fusion.2, bf16[1,1,9,2,128,128]{5,4,3,2,1,0:T(8,128)(2,1)} %param.10), kind=kOutput, calls=%fused_computation.5 | convolution fusion | flops 9478144 | bytes 581632 | tf_op jit(solution)/shard_map/dot_general | solution.py:63
  90.4 0.8 copy.9
  (2 shorter events, 0.0 us)
Async XLA Ops:
  0.0 88.4 %copy-start = (bf16[1,1,8,9,128,128]{5,4,3,2,1,0:T(8,128)(2,1)S(1)}, bf16[1,1,8,9,128,128]{5,4,3,2,1,0:T(8,128)(2,1)}, u32[]{:S(2)}) copy-start(bf16[1,1,8,9,128,128]{5,4,3,2,1,0:T(8,128)(2,1)} %param.7) | copy-start | bytes 7077892
  0.0 72.6 %collective-permute-start.1 = (bf16[32,1,1,1024]{3,0,2,1:T(8,128)(2,1)}, bf16[32,1,1,1024]{3,0,2,1:T(8,128)(2,1)S(1)}, u32[]{:S(2)}, u32[]{:S(2)}) collective-permute-start(bf16[32,1,1,1024]{3,0,2,1:T(8,128)(2,1)} %param.6), channel_id=1, source_target_pairs={{32,0},{64,32},{96,64},{128,96},{160,128},{192,160},{224,192},{256... | collective-permute-start | bytes 196616 | tf_op jit(solution)/shard_map/ppermute | solution.py:15
  2.3 69.4 %collective-permute-start = (bf16[32,1,1,1024]{3,0,2,1:T(8,128)(2,1)}, bf16[32,1,1,1024]{3,0,2,1:T(8,128)(2,1)S(1)}, u32[]{:S(2)}, u32[]{:S(2)}) collective-permute-start(bf16[32,1,1,1024]{3,0,2,1:T(8,128)(2,1)} %param.6), channel_id=1, source_target_pairs={{0,32},{32,64},{64,96},{96,128},{128,160},{160,192},{192,224},{224... | collective-permute-start | bytes 196616 | tf_op jit(solution)/shard_map/ppermute | solution.py:12
  5.6 12.1 %collective-permute-start.4 = (bf16[32,128]{1,0:T(8,128)(2,1)S(1)}, bf16[32,128]{1,0:T(8,128)(2,1)S(1)}, u32[]{:S(2)}, u32[]{:S(2)}) collective-permute-start(bf16[32,128]{1,0:T(8,128)(2,1)S(1)} %convolution_convert_fusion), channel_id=1, source_target_pairs={{0,32},{32,0},{64,96},{96,64},{128,160},{160,128},{192,224},{224,1... | collective-permute-start | bytes 24584 | tf_op jit(solution)/shard_map/ppermute | solution.py:21
  18.7 5.5 %collective-permute-start.5 = (bf16[32,128]{1,0:T(8,128)(2,1)S(1)}, bf16[32,128]{1,0:T(8,128)(2,1)S(1)}, u32[]{:S(2)}, u32[]{:S(2)}) collective-permute-start(bf16[32,128]{1,0:T(8,128)(2,1)S(1)} %fusion.6), channel_id=1, source_target_pairs={{0,64},{32,96},{64,0},{96,32},{128,192},{160,224},{192,128},{224,1... | collective-permute-start | bytes 24584 | tf_op jit(solution)/shard_map/ppermute | solution.py:21
  25.1 7.0 %collective-permute-start.6 = (bf16[32,128]{1,0:T(8,128)(2,1)S(1)}, bf16[32,128]{1,0:T(8,128)(2,1)S(1)}, u32[]{:S(2)}, u32[]{:S(2)}) collective-permute-start(bf16[32,128]{1,0:T(8,128)(2,1)S(1)} %fusion.7), channel_id=1, source_target_pairs={{0,128},{32,160},{64,192},{96,224},{128,0},{160,32},{192,64},{224,... | collective-permute-start | bytes 24584 | tf_op jit(solution)/shard_map/ppermute | solution.py:21
  33.0 9.5 %collective-permute-start.7 = (bf16[32,128]{1,0:T(8,128)(2,1)S(1)}, bf16[32,128]{1,0:T(8,128)(2,1)S(1)}, u32[]{:S(2)}, u32[]{:S(2)}) collective-permute-start(bf16[32,128]{1,0:T(8,128)(2,1)S(1)} %fusion.8), channel_id=1, source_target_pairs={{0,256},{32,288},{64,320},{96,352},{128,384},{160,416},{192,448},{... | collective-permute-start | bytes 24584 | tf_op jit(solution)/shard_map/ppermute | solution.py:21
  43.4 5.5 %collective-permute-start.8 = (bf16[32,128]{1,0:T(8,128)(2,1)S(1)}, bf16[32,128]{1,0:T(8,128)(2,1)S(1)}, u32[]{:S(2)}, u32[]{:S(2)}) collective-permute-start(bf16[32,128]{1,0:T(8,128)(2,1)S(1)} %fusion.9), channel_id=1, source_target_pairs={{0,1},{1,0},{2,3},{3,2},{4,5},{5,4},{6,7},{7,6},{8,9},{9,8},{10,11... | collective-permute-start | bytes 24584 | tf_op jit(solution)/shard_map/ppermute | solution.py:21
  49.8 6.4 %collective-permute-start.9 = (bf16[32,128]{1,0:T(8,128)(2,1)S(1)}, bf16[32,128]{1,0:T(8,128)(2,1)S(1)}, u32[]{:S(2)}, u32[]{:S(2)}) collective-permute-start(bf16[32,128]{1,0:T(8,128)(2,1)S(1)} %fusion.10), channel_id=1, source_target_pairs={{0,2},{1,3},{2,0},{3,1},{4,6},{5,7},{6,4},{7,5},{8,10},{9,11},{10,... | collective-permute-start | bytes 24584 | tf_op jit(solution)/shard_map/ppermute | solution.py:21
  57.1 9.4 %collective-permute-start.10 = (bf16[32,128]{1,0:T(8,128)(2,1)S(1)}, bf16[32,128]{1,0:T(8,128)(2,1)S(1)}, u32[]{:S(2)}, u32[]{:S(2)}) collective-permute-start(bf16[32,128]{1,0:T(8,128)(2,1)S(1)} %fusion.11), channel_id=1, source_target_pairs={{0,4},{1,5},{2,6},{3,7},{4,0},{5,1},{6,2},{7,3},{8,12},{9,13},{10,... | collective-permute-start | bytes 24584 | tf_op jit(solution)/shard_map/ppermute | solution.py:21
  68.3 12.2 %collective-permute-start.11 = (bf16[32,128]{1,0:T(8,128)(2,1)S(1)}, bf16[32,128]{1,0:T(8,128)(2,1)S(1)}, u32[]{:S(2)}, u32[]{:S(2)}) collective-permute-start(bf16[32,128]{1,0:T(8,128)(2,1)S(1)} %fusion.12), channel_id=1, source_target_pairs={{0,8},{1,9},{2,10},{3,11},{4,12},{5,13},{6,14},{7,15},{8,0},{9,1},... | collective-permute-start | bytes 24584 | tf_op jit(solution)/shard_map/ppermute | solution.py:21
  72.6 15.3 %collective-permute-start.3 = (bf16[32,3,1,1024]{3,0,2,1:T(8,128)(2,1)S(1)}, bf16[32,3,1,1024]{3,0,2,1:T(8,128)(2,1)S(1)}, u32[]{:S(2)}, u32[]{:S(2)}) collective-permute-start(bf16[32,3,1,1024]{3,0,2,1:T(8,128)(2,1)S(1)} %constant_dynamic-update-slice_fusion), channel_id=1, source_target_pairs={{1,0},{2,1},{3,2},{4,3},{5,4},{6,5},{7,6},{8,7},{9,8},{10,9},{11,1... | collective-permute-start | bytes 589832 | tf_op jit(solution)/shard_map/ppermute | solution.py:15
  75.9 12.0 %collective-permute-start.2 = (bf16[32,3,1,1024]{3,0,2,1:T(8,128)(2,1)S(1)}, bf16[32,3,1,1024]{3,0,2,1:T(8,128)(2,1)S(1)}, u32[]{:S(2)}, u32[]{:S(2)}) collective-permute-start(bf16[32,3,1,1024]{3,0,2,1:T(8,128)(2,1)S(1)} %constant_dynamic-update-slice_fusion), channel_id=1, source_target_pairs={{0,1},{1,2},{2,3},{3,4},{4,5},{5,6},{6,7},{7,8},{8,9},{9,10},{10,1... | collective-permute-start | bytes 589832 | tf_op jit(solution)/shard_map/ppermute | solution.py:12
  81.5 7.8 %collective-permute-start.12 = (bf16[32,128]{1,0:T(8,128)(2,1)S(1)}, bf16[32,128]{1,0:T(8,128)(2,1)S(1)}, u32[]{:S(2)}, u32[]{:S(2)}) collective-permute-start(bf16[32,128]{1,0:T(8,128)(2,1)S(1)} %fusion.13), channel_id=1, source_target_pairs={{0,16},{1,17},{2,18},{3,19},{4,20},{5,21},{6,22},{7,23},{8,24},{9,... | collective-permute-start | bytes 24584 | tf_op jit(solution)/shard_map/ppermute | solution.py:21
  88.1 1.3 %copy-start.1 = (bf16[1,1,128,1024]{3,2,1,0:T(8,128)(2,1)S(1)}, bf16[1,1,128,1024]{3,2,1,0:T(8,128)(2,1)}, u32[]{:S(2)}) copy-start(bf16[1,1,128,1024]{3,2,1,0:T(8,128)(2,1)} %param.11) | copy-start | bytes 786436
where the time goes:
time: 92.9 us; the launch traced here: 91.2 us
  starting transfers between devices  50 us (54%)
  waiting for transfers between devices  19.9 us (21%)
  matrix products  18.5 us (20%)
  local copies, waits for them, and re-layouts  1.76 us (2%)
    ppermute x9, starting transfers between devices, swapped(): lax.ppermute(array, axis, [(i, i ^ 1 << apart) for i in range(lax.axis_si...  37.6 us
    ppermute x9, waiting for transfers between devices, swapped(): lax.ppermute(array, axis, [(i, i ^ 1 << apart) for i in range(lax.axis_si...  19.9 us
    dot_general x9, matrix products, mix_level(): own_term = jnp.dot(coeffs, mixing[0], preferred_element_type=jnp.float32)  7.98 us
    dot_general x8, matrix products, mix_level(): other_term = jnp.dot(partner, mixing[1], preferred_element_type=jnp.float32)  7.09 us
    ppermute x2, starting transfers between devices, with_halo(): lax.ppermute(lax.slice_in_dim(block, block.shape[dim] - width, None, axis...  6.85 us
    ppermute x2, starting transfers between devices, with_halo(): lax.ppermute(lax.slice_in_dim(block, 0, width, axis=dim), axis, backward)  5.55 us
  transfers between devices with their start and end apart: 13, of which 6 were waited for; matrix products, arithmetic and copies ran while one was open for 21% of the time, Pallas kernels for 0%

commit v1 on v0

--- a/solution.py
+++ b/solution.py
@@ -15,10 +15,6 @@
         high = lax.ppermute(lax.slice_in_dim(block, 0, width, axis=dim), axis, backward)
         block = jnp.concatenate([low, block, high], axis=dim)
     return block
-
-
-def swapped(array, axis, apart):
-    return lax.ppermute(array, axis, [(i, i ^ 1 << apart) for i in range(lax.axis_size(axis))])
 
 
 def near_field(sources, near_blocks, near_index):
@@ -40,26 +36,30 @@
     return near_sum.reshape(excite, 1, 1, blocks * block_len)
 
 
-def mix_level(coeffs, partner, mixing):
-    own_term = jnp.dot(coeffs, mixing[0], preferred_element_type=jnp.float32)
-    other_term = jnp.dot(partner, mixing[1], preferred_element_type=jnp.float32)
-    return (own_term + other_term).astype(jnp.bfloat16)
+def pair_gather(coeffs, axis, apart):
+    count = lax.axis_size(axis)
+    pairs = [[i, i ^ 1 << apart] for i in range(count) if not i >> apart & 1]
+    return lax.all_gather(coeffs, axis, axis_index_groups=pairs)
 
 
 def far_field(sources, far_project, far_mixing, far_expand):
     excite = sources.shape[0]
     unknowns = sources.shape[3]
+    levels = [("bx", n) for n in range(lax.axis_size("bx").bit_length() - 1)]
+    levels += [("by", n) for n in range(lax.axis_size("by").bit_length() - 1)]
+    upper = jnp.stack([lax.axis_index(axis) >> n & 1 for axis, n in levels])
+    mixing = far_mixing[0, 0]
+    mixing = lax.optimization_barrier(
+        jnp.where(upper[:, None, None, None] == 1, mixing[:, ::-1], mixing)
+    )
     coeffs = jnp.dot(
         sources[:, 0, 0], far_project[0, 0], preferred_element_type=jnp.float32
     ).astype(jnp.bfloat16)
-    levels_first = lax.axis_size("bx").bit_length() - 1
-    levels_second = lax.axis_size("by").bit_length() - 1
-    for level_num in range(levels_first):
-        partner = swapped(coeffs, "bx", level_num)
-        coeffs = mix_level(coeffs, partner, far_mixing[0, 0, level_num])
-    for level_num in range(levels_second):
-        partner = swapped(coeffs, "by", level_num)
-        coeffs = mix_level(coeffs, partner, far_mixing[0, 0, levels_first + level_num])
+    for level_num, (axis, apart) in enumerate(levels):
+        both = pair_gather(coeffs, axis, apart)
+        coeffs = jnp.einsum(
+            "bcr,brq->cq", both, mixing[level_num], preferred_element_type=jnp.float32
+        ).astype(jnp.bfloat16)
     far_sum = jnp.dot(coeffs, far_expand[0, 0], preferred_element_type=jnp.float32)
     return far_sum.reshape(excite, 1, 1, unknowns)
 

time: 92.9 us -> 82.2 us (0.88)
  the two profiles are of different devices: /device:TPU:62 before, /device:TPU:70 now
where the time goes in v1:
time: 82.2 us; the launch traced here: 81.9 us
  blocking collectives  55.8 us (68%)
  starting transfers between devices  11.9 us (14%)
  waiting for transfers between devices  7.65 us (9%)
  matrix products  3.68 us (4%)
  other arithmetic  1.63 us (2%)
  local copies, waits for them, and re-layouts  1.02 us (1%)
    all_gather x9, blocking collectives, pair_gather(): return lax.all_gather(coeffs, axis, axis_index_groups=pairs)  55.8 us
    ppermute x2, starting transfers between devices, with_halo(): lax.ppermute(lax.slice_in_dim(block, 0, width, axis=dim), axis, backward)  7.86 us
    ppermute x2, waiting for transfers between devices, with_halo(): lax.ppermute(lax.slice_in_dim(block, block.shape[dim] - width, None, axis...  6.51 us
    ppermute x2, starting transfers between devices, with_halo(): lax.ppermute(lax.slice_in_dim(block, block.shape[dim] - width, None, axis...  4.07 us
  transfers between devices with their start and end apart: 4, of which 2 were waited for; matrix products, arithmetic and copies ran while one was open for 5% of the time, Pallas kernels for 0%

profile of v1, /device:TPU:70, one launch (start us, length us, event | category | flops | bytes accessed | tf_op | source)
XLA Modules:
  0.0 81.9 jit_solution(11553004973818654180)
XLA Ops:
  0.0 0.0 copy-start
  0.0 0.0 copy-start.2
  0.0 0.0 copy-start.3
  0.0 2.3 %collective-permute-start.1 = (bf16[32,1,1,1024]{3,0,2,1:T(8,128)(2,1)}, bf16[32,1,1,1024]{3,0,2,1:T(8,128)(2,1)S(1)}, u32[]{:S(2)}, u32[]{:S(2)}) collective-permute-start(bf16[32,1,1,1024]{3,0,2,1:T(8,128)(2,1)} %param.6), channel_id=1, source_target_pairs={{32,0},{64,32},{96,64},{128,96},{160,128},{192,160},{224,192},{256... | collective-permute-start | bytes 196616 | tf_op jit(solution)/shard_map/ppermute | solution.py:15
  2.3 2.2 %collective-permute-start = (bf16[32,1,1,1024]{3,0,2,1:T(8,128)(2,1)}, bf16[32,1,1,1024]{3,0,2,1:T(8,128)(2,1)S(1)}, u32[]{:S(2)}, u32[]{:S(2)}) collective-permute-start(bf16[32,1,1,1024]{3,0,2,1:T(8,128)(2,1)} %param.6), channel_id=1, source_target_pairs={{0,32},{32,64},{64,96},{96,128},{128,160},{160,192},{192,224},{224... | collective-permute-start | bytes 196616 | tf_op jit(solution)/shard_map/ppermute | solution.py:12
  4.5 0.1 stack.39
  4.6 1.2 %convolution_convert_fusion = bf16[32,128]{1,0:T(8,128)(2,1)S(1)} fusion(bf16[1,1,1024,128]{3,2,1,0:T(8,128)(2,1)} %param.9, bf16[32,1,1,1024]{3,0,2,1:T(8,128)(2,1)} %param.6), kind=kOutput, calls=%fused_computation.24 | convolution fusion | flops 8392704 | bytes 335872 | tf_op jit(solution)/shard_map/dot_general | solution.py:55
  5.8 9.1 %all-gather = bf16[64,128]{1,0:T(8,128)(2,1)S(1)} all-gather(bf16[32,128]{1,0:T(8,128)(2,1)S(1)} %convolution_convert_fusion), channel_id=2, replica_groups={{0,32},{64,96},{128,160},{192,224},{256,288},{320,352},{384,416},{448,4..., dimensions={0}, use_global_device_ids=true | all-gather | bytes 24576 | tf_op jit(solution)/shard_map/all_gather | solution.py:42
  14.9 1.5 %reverse_select_fusion = bf16[9,2,128,128]{3,2,1,0:T(8,128)(2,1)S(1)} fusion(bf16[9,2,128,128]{3,2,1,0:T(8,128)(2,1)} %bitcast.134, pred[9]{0:T(512)(128)(4,1)S(1)} %broadcast_compare_fusion), kind=kLoop, calls=%fused_computation.25 | loop fusion | flops 294912 | bytes 1179657 | tf_op jit(solution)/shard_map/jit(_where)/select_n | solution.py:53
  16.4 0.1 fusion.6
  16.5 4.4 %all-gather.1 = bf16[64,128]{1,0:T(8,128)(2,1)S(1)} all-gather(bf16[32,128]{1,0:T(8,128)(2,1)S(1)} %fusion.6), channel_id=3, replica_groups={{0,64},{32,96},{128,192},{160,224},{256,320},{288,352},{384,448},{416,4..., dimensions={0}, use_global_device_ids=true | all-gather | bytes 24576 | tf_op jit(solution)/shard_map/all_gather | solution.py:42
  20.8 0.1 fusion.7
  21.0 5.9 %all-gather.2 = bf16[64,128]{1,0:T(8,128)(2,1)S(1)} all-gather(bf16[32,128]{1,0:T(8,128)(2,1)S(1)} %fusion.7), channel_id=4, replica_groups={{0,128},{32,160},{64,192},{96,224},{256,384},{288,416},{320,448},{352,4..., dimensions={0}, use_global_device_ids=true | all-gather | bytes 24576 | tf_op jit(solution)/shard_map/all_gather | solution.py:42
  26.8 0.1 fusion.8
  27.0 8.3 %all-gather.3 = bf16[64,128]{1,0:T(8,128)(2,1)S(1)} all-gather(bf16[32,128]{1,0:T(8,128)(2,1)S(1)} %fusion.8), channel_id=5, replica_groups={{0,256},{32,288},{64,320},{96,352},{128,384},{160,416},{192,448},{224,4..., dimensions={0}, use_global_device_ids=true | all-gather | bytes 24576 | tf_op jit(solution)/shard_map/all_gather | solution.py:42
  35.2 0.1 fusion.9
  35.4 4.4 %all-gather.4 = bf16[64,128]{1,0:T(8,128)(2,1)S(1)} all-gather(bf16[32,128]{1,0:T(8,128)(2,1)S(1)} %fusion.9), channel_id=6, replica_groups={{0,1},{2,3},{4,5},{6,7},{8,9},{10,11},{12,13},{14,15},{16,17},{18,19},{..., dimensions={0}, use_global_device_ids=true | all-gather | bytes 24576 | tf_op jit(solution)/shard_map/all_gather | solution.py:42
  39.7 0.1 fusion.10
  39.8 5.3 %all-gather.5 = bf16[64,128]{1,0:T(8,128)(2,1)S(1)} all-gather(bf16[32,128]{1,0:T(8,128)(2,1)S(1)} %fusion.10), channel_id=7, replica_groups={{0,2},{1,3},{4,6},{5,7},{8,10},{9,11},{12,14},{13,15},{16,18},{17,19},{..., dimensions={0}, use_global_device_ids=true | all-gather | bytes 24576 | tf_op jit(solution)/shard_map/all_gather | solution.py:42
  45.1 0.1 fusion.11
  45.2 8.3 %all-gather.6 = bf16[64,128]{1,0:T(8,128)(2,1)S(1)} all-gather(bf16[32,128]{1,0:T(8,128)(2,1)S(1)} %fusion.11), channel_id=8, replica_groups={{0,4},{1,5},{2,6},{3,7},{8,12},{9,13},{10,14},{11,15},{16,20},{17,21},{..., dimensions={0}, use_global_device_ids=true | all-gather | bytes 24576 | tf_op jit(solution)/shard_map/all_gather | solution.py:42
  53.5 0.1 fusion.12
  53.6 4.4 %all-gather.7 = bf16[64,128]{1,0:T(8,128)(2,1)S(1)} all-gather(bf16[32,128]{1,0:T(8,128)(2,1)S(1)} %fusion.12), channel_id=9, replica_groups={{0,8},{1,9},{2,10},{3,11},{4,12},{5,13},{6,14},{7,15},{16,24},{17,25},{..., dimensions={0}, use_global_device_ids=true | all-gather | bytes 24576 | tf_op jit(solution)/shard_map/all_gather | solution.py:42
  58.0 0.1 fusion.13
  58.1 5.9 %all-gather.8 = bf16[64,128]{1,0:T(8,128)(2,1)S(1)} all-gather(bf16[32,128]{1,0:T(8,128)(2,1)S(1)} %fusion.13), channel_id=10, replica_groups={{0,16},{1,17},{2,18},{3,19},{4,20},{5,21},{6,22},{7,23},{8,24},{9,25},{..., dimensions={0}, use_global_device_ids=true | all-gather | bytes 24576 | tf_op jit(solution)/shard_map/all_gather | solution.py:42
  64.0 0.0 collective-permute-done
  64.1 0.0 copy-done.2
  64.1 0.0 collective-permute-done.1
  64.1 5.6 %collective-permute-start.3 = (bf16[32,3,1,1024]{3,0,2,1:T(8,128)(2,1)S(1)}, bf16[32,3,1,1024]{3,0,2,1:T(8,128)(2,1)S(1)}, u32[]{:S(2)}, u32[]{:S(2)}) collective-permute-start(bf16[32,3,1,1024]{3,0,2,1:T(8,128)(2,1)S(1)} %constant_dynamic-update-slice_fusion), channel_id=1, source_target_pairs={{1,0},{2,1},{3,2},{4,3},{5,4},{6,5},{7,6},{8,7},{9,8},{10,9},{11,1... | collective-permute-start | bytes 589832 | tf_op jit(solution)/shard_map/ppermute | solution.py:15
  69.7 1.9 %collective-permute-start.2 = (bf16[32,3,1,1024]{3,0,2,1:T(8,128)(2,1)S(1)}, bf16[32,3,1,1024]{3,0,2,1:T(8,128)(2,1)S(1)}, u32[]{:S(2)}, u32[]{:S(2)}) collective-permute-start(bf16[32,3,1,1024]{3,0,2,1:T(8,128)(2,1)S(1)} %constant_dynamic-update-slice_fusion), channel_id=1, source_target_pairs={{0,1},{1,2},{2,3},{3,4},{4,5},{5,6},{6,7},{7,8},{8,9},{9,10},{10,1... | collective-permute-start | bytes 589832 | tf_op jit(solution)/shard_map/ppermute | solution.py:12
  71.6 0.0 copy-done.3
  71.6 0.1 fusion.20
  71.7 1.1 %collective-permute-done.3 = bf16[32,3,1,1024]{3,0,2,1:T(8,128)(2,1)S(1)} collective-permute-done((bf16[32,3,1,1024]{3,0,2,1:T(8,128)(2,1)S(1)}, bf16[32,3,1,1024]{3,0,2,1:T(8,128)(2,1)S(1)}, u32[]{:S(2)}, u32[]{:S(2)}) %collective-permute-start.3) | collective-permute-done | bytes 196640 | tf_op jit(solution)/shard_map/ppermute | solution.py:15
  72.8 6.5 %collective-permute-done.2 = bf16[32,3,1,1024]{3,0,2,1:T(8,128)(2,1)S(1)} collective-permute-done((bf16[32,3,1,1024]{3,0,2,1:T(8,128)(2,1)S(1)}, bf16[32,3,1,1024]{3,0,2,1:T(8,128)(2,1)S(1)}, u32[]{:S(2)}, u32[]{:S(2)}) %collective-permute-start.2) | collective-permute-done | bytes 196640 | tf_op jit(solution)/shard_map/ppermute | solution.py:12
  79.3 0.1 pad_maximum_fusion
  79.4 0.1 copy.14
  79.5 0.0 copy-start.1
  79.5 0.3 fusion.21
  79.8 0.0 copy-done
  79.8 0.9 %fusion.2 = f32[8,4,8,128]{3,2,1,0:T(8,128)S(1)} fusion(bf16[1,1,8,9,128,128]{5,4,3,2,1,0:T(8,128)(2,1)S(1)} %copy-done, bf16[9,32,128,8]{2,3,1,0:T(8,128)(2,1)S(1)} %fusion.21), kind=kOutput, calls=%fused_computation.3 | convolution fusion | flops 75497472 | bytes 3080192 | tf_op jit(solution)/shard_map/rkij,rkcj->cri/dot_general | solution.py:33
  80.7 0.0 copy-done.1
  80.7 0.3 fusion.5
  81.1 0.8 copy.9
  (4 shorter events, 0.0 us)
Async XLA Ops:
  0.0 79.8 %copy-start = (bf16[1,1,8,9,128,128]{5,4,3,2,1,0:T(8,128)(2,1)S(1)}, bf16[1,1,8,9,128,128]{5,4,3,2,1,0:T(8,128)(2,1)}, u32[]{:S(2)}) copy-start(bf16[1,1,8,9,128,128]{5,4,3,2,1,0:T(8,128)(2,1)} %param.7) | copy-start | bytes 7077892
  0.0 64.1 %copy-start.2 = (bf16[32,1,1,1024]{3,0,2,1:T(8,128)(2,1)S(1)}, bf16[32,1,1,1024]{3,0,2,1:T(8,128)(2,1)}, u32[]{:S(2)}) copy-start(bf16[32,1,1,1024]{3,0,2,1:T(8,128)(2,1)} %param.6) | copy-start | bytes 196612
  0.0 71.6 %copy-start.3 = (s32[1,1,8,9]{3,2,1,0:T(8,128)S(1)}, s32[1,1,8,9]{3,2,1,0:T(8,128)}, u32[]{:S(2)}) copy-start(s32[1,1,8,9]{3,2,1,0:T(8,128)} %param.8) | copy-start | bytes 868
  0.0 64.1 %collective-permute-start.1 = (bf16[32,1,1,1024]{3,0,2,1:T(8,128)(2,1)}, bf16[32,1,1,1024]{3,0,2,1:T(8,128)(2,1)S(1)}, u32[]{:S(2)}, u32[]{:S(2)}) collective-permute-start(bf16[32,1,1,1024]{3,0,2,1:T(8,128)(2,1)} %param.6), channel_id=1, source_target_pairs={{32,0},{64,32},{96,64},{128,96},{160,128},{192,160},{224,192},{256... | collective-permute-start | bytes 196616 | tf_op jit(solution)/shard_map/ppermute | solution.py:15
  2.3 61.7 %collective-permute-start = (bf16[32,1,1,1024]{3,0,2,1:T(8,128)(2,1)}, bf16[32,1,1,1024]{3,0,2,1:T(8,128)(2,1)S(1)}, u32[]{:S(2)}, u32[]{:S(2)}) collective-permute-start(bf16[32,1,1,1024]{3,0,2,1:T(8,128)(2,1)} %param.6), channel_id=1, source_target_pairs={{0,32},{32,64},{64,96},{96,128},{128,160},{160,192},{192,224},{224... | collective-permute-start | bytes 196616 | tf_op jit(solution)/shard_map/ppermute | solution.py:12
  64.1 8.7 %collective-permute-start.3 = (bf16[32,3,1,1024]{3,0,2,1:T(8,128)(2,1)S(1)}, bf16[32,3,1,1024]{3,0,2,1:T(8,128)(2,1)S(1)}, u32[]{:S(2)}, u32[]{:S(2)}) collective-permute-start(bf16[32,3,1,1024]{3,0,2,1:T(8,128)(2,1)S(1)} %constant_dynamic-update-slice_fusion), channel_id=1, source_target_pairs={{1,0},{2,1},{3,2},{4,3},{5,4},{6,5},{7,6},{8,7},{9,8},{10,9},{11,1... | collective-permute-start | bytes 589832 | tf_op jit(solution)/shard_map/ppermute | solution.py:15
  69.7 9.7 %collective-permute-start.2 = (bf16[32,3,1,1024]{3,0,2,1:T(8,128)(2,1)S(1)}, bf16[32,3,1,1024]{3,0,2,1:T(8,128)(2,1)S(1)}, u32[]{:S(2)}, u32[]{:S(2)}) collective-permute-start(bf16[32,3,1,1024]{3,0,2,1:T(8,128)(2,1)S(1)} %constant_dynamic-update-slice_fusion), channel_id=1, source_target_pairs={{0,1},{1,2},{2,3},{3,4},{4,5},{5,6},{6,7},{7,8},{8,9},{9,10},{10,1... | collective-permute-start | bytes 589832 | tf_op jit(solution)/shard_map/ppermute | solution.py:12
  79.5 1.2 %copy-start.1 = (bf16[1,1,128,1024]{3,2,1,0:T(8,128)(2,1)S(1)}, bf16[1,1,128,1024]{3,2,1,0:T(8,128)(2,1)}, u32[]{:S(2)}) copy-start(bf16[1,1,128,1024]{3,2,1,0:T(8,128)(2,1)} %param.11) | copy-start | bytes 786436

commit v2 on v1

v2 whole, which is shorter than its diff:
```python
import functools

import jax
import jax.numpy as jnp
from jax import lax
from jax.experimental import pallas as pl
from jax.experimental.pallas import tpu as pltpu
from jax.sharding import PartitionSpec as P

BOTH = ("bx", "by")


def pair_gather(values, axis, apart):
    count = lax.axis_size(axis)
    pairs = [[i, i ^ 1 << apart] for i in range(count) if not i >> apart & 1]
    return lax.all_gather(values, axis, axis_index_groups=pairs)


def handed(values, source):
    pairs = [(i, i ^ 1) for i in range(lax.axis_size("bx")) if i & 1 == source]
    return lax.ppermute(values, "bx", pairs)


def sent_on(values, step_x, step_y):
    count_x, count_y = lax.axis_size("bx"), lax.axis_size("by")
    moves = []
    for x in range(0, count_x, 2):
        for y in range(count_y):
            to_x, to_y = x + step_x, y + step_y
            if 0 <= to_x < count_x and 0 <= to_y < count_y:
                moves.append((x * count_y + y, to_x * count_y + to_y))
    return lax.ppermute(values, BOTH, moves)


def surroundings(sources):
    below, above = sent_on(sources, 0, 1), sent_on(sources, 0, -1)
    column = jnp.stack([below, sources, above], axis=1)
    before, after = sent_on(column[1], 2, 0), sent_on(column[0], -2, 0)
    return jnp.concatenate([before[None], column, after[None]])


def near_field(around, near_blocks, near_index):
    positions, excite, unknowns = around.shape
    blocks, block_len = near_blocks.shape[0], near_blocks.shape[2]
    source_blocks = around.reshape(positions, excite, blocks, block_len)
    onehot = (
        near_index[:, :, None] == jnp.arange(blocks, dtype=near_index.dtype)[None, None, :]
    ).astype(jnp.bfloat16)
    picked = jnp.einsum(
        "rkb,kcbj->rkcj", onehot, source_blocks, preferred_element_type=jnp.float32
    ).astype(jnp.bfloat16)
    near_sum = jnp.einsum(
        "rkij,rkcj->cri", near_blocks, picked, preferred_element_type=jnp.float32
    )
    return near_sum.reshape(excite, unknowns)


def order_levels(levels, theirs_hbm, own_hbm, ordered, sems):
    copies = []
    for box, blocks in enumerate((theirs_hbm, own_hbm)):
        for at, (axis, apart) in enumerate(levels):
            upper = lax.axis_index(axis) >> apart & 1
            for member in range(2):
                copy = pltpu.make_async_copy(
                    blocks.at[at + 1, member ^ upper],
                    ordered.at[box, at, member],
                    sems.at[box, at, member],
                )
                copy.start()
                copies.append(copy)
    for copy in copies:
        copy.wait()


def butterfly(coeffs, theirs, own):
    levels = [("bx", n) for n in range(1, lax.axis_size("bx").bit_length() - 1)]
    levels += [("by", n) for n in range(lax.axis_size("by").bit_length() - 1)]
    count, rank = len(levels), own.shape[-1]
    ordered = pl.pallas_call(
        functools.partial(order_levels, levels),
        out_shape=jax.ShapeDtypeStruct((2, count, 2, rank, rank), own.dtype),
        in_specs=[pl.BlockSpec(memory_space=pl.ANY)] * 2,
        out_specs=pl.BlockSpec(memory_space=pltpu.VMEM),
        scratch_shapes=[pltpu.SemaphoreType.DMA((2, count, 2))],
    )(theirs, own)
    first = jnp.stack([theirs[0], own[0][::-1]])
    coeffs = jnp.einsum(
        "gcr,bgrq->bcq", coeffs, first, preferred_element_type=jnp.float32
    ).astype(jnp.bfloat16)
    for at, (axis, apart) in enumerate(levels):
        both = pair_gather(coeffs, axis, apart)
        coeffs = jnp.einsum(
            "gbcr,bgrq->bcq", both, ordered[:, at], preferred_element_type=jnp.float32
        ).astype(jnp.bfloat16)
    return coeffs


def per_device(sources, near_blocks, near_index, far_project, far_mixing, far_expand):
    own_sources, own_blocks, own_index = sources[:, 0, 0], near_blocks[0, 0], near_index[0, 0]
    own_mixing = far_mixing[0, 0]
    excite, unknowns = own_sources.shape
    rank = far_project.shape[3]
    core = lax.axis_index("bx") & 1
    their_mixing = handed(own_mixing, 0)
    their_blocks = handed(own_blocks, 1)
    coeffs = jnp.dot(
        own_sources, far_project[0, 0], preferred_element_type=jnp.float32
    ).astype(jnp.bfloat16)
    rows, positions = own_index.shape
    index_values = jnp.pad(
        own_index.astype(jnp.bfloat16), ((0, excite - rows), (0, 128 - positions))
    )
    shared = pair_gather(
        jnp.concatenate([own_sources, coeffs, index_values], axis=1), "bx", 0
    )

    def near_fields():
        around = surroundings(shared[:, :, :unknowns])
        their_index = shared[1, :rows, unknowns + rank : unknowns + rank + positions]
        mine = near_field(
            around[:3].reshape(-1, excite, unknowns), own_blocks, own_index
        )
        theirs = near_field(
            around[1:].reshape(-1, excite, unknowns), their_blocks, their_index.astype(jnp.int32)
        )
        return mine, theirs, jnp.zeros((excite, rank), jnp.bfloat16)

    def butterflies():
        final = butterfly(shared[:, :, unknowns : unknowns + rank], their_mixing, own_mixing)
        given = jnp.pad(final[0].astype(jnp.float32), ((0, 0), (0, unknowns - rank)))
        return given, given, final[1]

    mine, given, final = lax.cond(core == 0, near_fields, butterflies)
    taken = pair_gather(given, "bx", 0)
    near_part = jnp.where(core == 0, mine, taken[0])
    final = jnp.where(core == 0, taken[1, :, :rank].astype(jnp.bfloat16), final)
    far_part = jnp.dot(final, far_expand[0, 0], preferred_element_type=jnp.float32)
    return (near_part + far_part)[:, None, None]


def solution(mesh):
    placed = (
        P(None, "bx", "by", None),
        P("bx", "by", None, None, None, None),
        P("bx", "by", None, None),
        P("bx", "by", None, None),
        P("bx", "by", None, None, None, None),
        P("bx", "by", None, None),
    )
    return jax.shard_map(
        per_device, mesh=mesh, in_specs=placed, out_specs=P(None, "bx", "by", None), check_vma=False
    )
```

time: 82.2 us -> 63 us (0.77)
  the two profiles are of different devices: /device:TPU:70 before, /device:TPU:1 now
where the time goes in v2:
time: 63 us; the launch traced here: 62.6 us
  blocking collectives  42 us (67%)
  starting transfers between devices  10.3 us (16%)
  local copies, waits for them, and re-layouts  3.09 us (5%)
  Pallas kernels  2.96 us (5%)
  matrix products  2.51 us (4%)
  other arithmetic  1.57 us (2%)
    all_gather x10, blocking collectives, pair_gather(): return lax.all_gather(values, axis, axis_index_groups=pairs)  42 us
    ppermute x2, starting transfers between devices, handed(): return lax.ppermute(values, 'bx', pairs)  10.3 us
    pallas_call x1, Pallas kernels, butterfly(): pl.pallas_call(functools.partial(order_levels, levels), out_shape=jax.Sha...  2.96 us
    squeeze x1, local copies, waits for them, and re-layouts, butterfly(): ordered[:, at]  1.4 us
  transfers between devices with their start and end apart: 2, of which 0 were waited for; matrix products, arithmetic and copies ran while one was open for 4% of the time, Pallas kernels for 0%

profile of v2, /device:TPU:1, one launch (start us, length us, event | category | flops | bytes accessed | tf_op | source)
XLA Modules:
  0.0 62.6 jit_solution(13808123620179328740)
XLA Ops:
  0.0 0.0 copy-start
  0.0 9.0 %collective-permute-start.5 = (bf16[8,9,128,128]{3,2,1,0:T(8,128)(2,1)}, bf16[8,9,128,128]{3,2,1,0:T(8,128)(2,1)S(1)}, u32[]{:S(2)}, u32[]{:S(2)}) collective-permute-start(bf16[8,9,128,128]{3,2,1,0:T(8,128)(2,1)} %bitcast.178), channel_id=1, source_target_pairs={{32,0},{96,64},{160,128},{224,192},{288,256},{352,320},{416,384},{... | collective-permute-start | bytes 7077896 | tf_op jit(solution)/shard_map/ppermute | solution.py:21
  9.0 1.3 %collective-permute-start.4 = (bf16[9,2,128,128]{3,2,1,0:T(8,128)(2,1)}, bf16[9,2,128,128]{3,2,1,0:T(8,128)(2,1)S(1)}, u32[]{:S(2)}, u32[]{:S(2)}) collective-permute-start(bf16[9,2,128,128]{3,2,1,0:T(8,128)(2,1)} %bitcast.184), channel_id=1, source_target_pairs={{0,32},{64,96},{128,160},{192,224},{256,288},{320,352},{384,416},{... | collective-permute-start | bytes 1769480 | tf_op jit(solution)/shard_map/ppermute | solution.py:21
  10.3 0.7 %convert_bitcast_fusion = bf16[8,9]{1,0:T(8,128)(2,1)S(1)} fusion(s32[1,1,8,9]{3,2,1,0:T(8,128)} %param.10), kind=kLoop, calls=%fused_computation.84 | loop fusion | flops 72 | bytes 432 | tf_op jit(solution)/shard_map/convert_element_type | solution.py:111
  11.0 1.1 %convolution_convert_fusion.2 = bf16[32,128]{1,0:T(8,128)(2,1)S(1)} fusion(bf16[1,1,1024,128]{3,2,1,0:T(8,128)(2,1)} %param.11, bf16[32,1,1,1024]{3,0,2,1:T(8,128)(2,1)} %param.8), kind=kOutput, calls=%fused_computation.71 | convolution fusion | flops 8392704 | bytes 335872 | tf_op jit(solution)/shard_map/dot_general | solution.py:106
  12.2 0.8 %fusion.42 = bf16[32,1280]{1,0:T(8,128)(2,1)S(1)} fusion(bf16[8,9]{1,0:T(8,128)(2,1)S(1)} %convert_bitcast_fusion, bf16[32,128]{1,0:T(8,128)(2,1)S(1)} %convolution_convert_fusion.2, bf16[32,1024]{1,0:T(8,128)(2,1)} %bitcast.192), kind=kLoop, calls=%fused_computation.80 | loop fusion | flops 327680 | bytes 155792 | tf_op jit(solution)/shard_map/concatenate | solution.py:114
  13.0 2.7 %all-gather.8 = bf16[64,1280]{1,0:T(8,128)(2,1)S(1)} all-gather(bf16[32,1280]{1,0:T(8,128)(2,1)S(1)} %fusion.42), channel_id=10, replica_groups={{0,32},{64,96},{128,160},{192,224},{256,288},{320,352},{384,416},{448,4..., dimensions={0}, use_global_device_ids=true | all-gather | bytes 245760 | tf_op jit(solution)/shard_map/all_gather | solution.py:16
  15.7 0.0 collective-permute-done.4
  15.7 0.0 collective-permute-done.5
  15.7 43.8 %conditional.1 = (f32[32,1024]{1,0:T(8,128)S(1)}, f32[32,1024]{1,0:T(8,128)S(1)}, bf16[32,128]{1,0:T(8,128)(2,1)S(1)}) conditional(s32[]{:T(128)} %convert_element_type.78, (bf16[9,2,128,128]{3,2,1,0:T(8,128)(2,1)S(1)}, bf16[9,2,128,128]{3,2,1,0:T(8,128)(2,1)}, bf16[2,32,1280]{2,1,0:T(8,128)(2,1)S(1)}) %tuple.31, (bf16[2,32,1280]{2,1,0:T(8,128)(2,1)S(1)}, ...), branch_computations={%region_0.1_spmd, %region_1.2_spmd} | conditional | flops 163185856 | bytes 48638336 | solution.py:133
  15.7 3.0 %branch_0_fun.1 = bf16[2,8,2,128,128]{4,3,2,1,0:T(8,128)(2,1)} custom-call(bf16[9,2,128,128]{3,2,1,0:T(8,128)(2,1)S(1)} %get-tuple-element.19.theirs_hbm, bf16[9,2,128,128]{3,2,1,0:T(8,128)(2,1)} %get-tuple-element.20.own_hbm), custom_call_target="tpu_custom_call" | custom-call | tf_op jit(solution)/shard_map/cond/branch_0_fun/pallas_call | solution.py:79
  18.7 1.4 %slice_bitcast_fusion = (bf16[2,2,128,128]{3,2,1,0:T(8,128)(2,1)S(1)}, bf16[2,2,128,128]{3,2,1,0:T(8,128)(2,1)S(1)}, bf16[2,2,128,128]{3,2,1,0:T(8,128)(2,1)S(1)...) fusion(bf16[2,8,2,128,128]{4,3,2,1,0:T(8,128)(2,1)} %branch_0_fun.1), kind=kLoop, calls=%fused_computation.19 | loop fusion | bytes 2097152 | tf_op jit(solution)/shard_map/cond/branch_0_fun/squeeze | solution.py:93
  20.1 0.8 %slice_bitcast_fusion.8 = bf16[2,128,128]{2,1,0:T(8,128)(2,1)S(1)} fusion(bf16[9,2,128,128]{3,2,1,0:T(8,128)(2,1)} %get-tuple-element.20.own_hbm), kind=kLoop, calls=%fused_computation.40 | loop fusion | bytes 131072 | tf_op jit(solution)/shard_map/cond/branch_0_fun/squeeze | solution.py:86
  21.0 0.1 fusion.9
  21.1 3.3 %all-gather = bf16[4,32,128]{2,1,0:T(8,128)(2,1)S(1)} all-gather(bf16[2,32,128]{2,1,0:T(8,128)(2,1)S(1)} %fusion.9), channel_id=2, replica_groups={{0,64},{32,96},{128,192},{160,224},{256,320},{288,352},{384,448},{416,4..., dimensions={0}, use_global_device_ids=true | all-gather | bytes 49152 | tf_op jit(solution)/shard_map/cond/branch_0_fun/all_gather | solution.py:16
  24.4 0.1 fusion
  24.5 4.9 %all-gather.1 = bf16[4,32,128]{2,1,0:T(8,128)(2,1)S(1)} all-gather(bf16[2,32,128]{2,1,0:T(8,128)(2,1)S(1)} %fusion), channel_id=3, replica_groups={{0,128},{32,160},{64,192},{96,224},{256,384},{288,416},{320,448},{352,4..., dimensions={0}, use_global_device_ids=true | all-gather | bytes 49152 | tf_op jit(solution)/shard_map/cond/branch_0_fun/all_gather | solution.py:16
  29.5 0.1 fusion.1
  29.6 7.2 %all-gather.2 = bf16[4,32,128]{2,1,0:T(8,128)(2,1)S(1)} all-gather(bf16[2,32,128]{2,1,0:T(8,128)(2,1)S(1)} %fusion.1), channel_id=4, replica_groups={{0,256},{32,288},{64,320},{96,352},{128,384},{160,416},{192,448},{224,4..., dimensions={0}, use_global_device_ids=true | all-gather | bytes 49152 | tf_op jit(solution)/shard_map/cond/branch_0_fun/all_gather | solution.py:16
  36.8 0.1 fusion.2
  36.9 3.3 %all-gather.3 = bf16[4,32,128]{2,1,0:T(8,128)(2,1)S(1)} all-gather(bf16[2,32,128]{2,1,0:T(8,128)(2,1)S(1)} %fusion.2), channel_id=5, replica_groups={{0,1},{2,3},{4,5},{6,7},{8,9},{10,11},{12,13},{14,15},{16,17},{18,19},{..., dimensions={0}, use_global_device_ids=true | all-gather | bytes 49152 | tf_op jit(solution)/shard_map/cond/branch_0_fun/all_gather | solution.py:16
  40.1 0.1 fusion.3
  40.3 4.2 %all-gather.4 = bf16[4,32,128]{2,1,0:T(8,128)(2,1)S(1)} all-gather(bf16[2,32,128]{2,1,0:T(8,128)(2,1)S(1)} %fusion.3), channel_id=6, replica_groups={{0,2},{1,3},{4,6},{5,7},{8,10},{9,11},{12,14},{13,15},{16,18},{17,19},{..., dimensions={0}, use_global_device_ids=true | all-gather | bytes 49152 | tf_op jit(solution)/shard_map/cond/branch_0_fun/all_gather | solution.py:16
  44.4 0.1 fusion.4
  44.6 7.2 %all-gather.5 = bf16[4,32,128]{2,1,0:T(8,128)(2,1)S(1)} all-gather(bf16[2,32,128]{2,1,0:T(8,128)(2,1)S(1)} %fusion.4), channel_id=7, replica_groups={{0,4},{1,5},{2,6},{3,7},{8,12},{9,13},{10,14},{11,15},{16,20},{17,21},{..., dimensions={0}, use_global_device_ids=true | all-gather | bytes 49152 | tf_op jit(solution)/shard_map/cond/branch_0_fun/all_gather | solution.py:16
  51.7 0.1 fusion.5
  51.9 3.3 %all-gather.6 = bf16[4,32,128]{2,1,0:T(8,128)(2,1)S(1)} all-gather(bf16[2,32,128]{2,1,0:T(8,128)(2,1)S(1)} %fusion.5), channel_id=8, replica_groups={{0,8},{1,9},{2,10},{3,11},{4,12},{5,13},{6,14},{7,15},{16,24},{17,25},{..., dimensions={0}, use_global_device_ids=true | all-gather | bytes 49152 | tf_op jit(solution)/shard_map/cond/branch_0_fun/all_gather | solution.py:16
  55.1 0.1 fusion.6
  55.3 4.2 %all-gather.7 = bf16[4,32,128]{2,1,0:T(8,128)(2,1)S(1)} all-gather(bf16[2,32,128]{2,1,0:T(8,128)(2,1)S(1)} %fusion.6), channel_id=9, replica_groups={{0,16},{1,17},{2,18},{3,19},{4,20},{5,21},{6,22},{7,23},{8,24},{9,25},{..., dimensions={0}, use_global_device_ids=true | all-gather | bytes 49152 | tf_op jit(solution)/shard_map/cond/branch_0_fun/all_gather | solution.py:16
  59.4 0.1 fusion.7
  59.6 2.0 %all-gather.9 = f32[64,1024]{1,0:T(8,128)S(1)} all-gather(f32[32,1024]{1,0:T(8,128)S(1)} %get-tuple-element.30), channel_id=11, replica_groups={{0,32},{64,96},{128,160},{192,224},{256,288},{320,352},{384,416},{448,4..., dimensions={0}, use_global_device_ids=true | all-gather | bytes 393216 | tf_op jit(solution)/shard_map/all_gather | solution.py:16
  61.6 0.0 copy-done
  61.6 0.2 fusion.41
  61.8 0.8 %copy.51 = f32[32,1,1,1024]{3,2,1,0:T(1,128)} copy(f32[32,1,1,1024]{3,0,2,1:T(8,128)S(1)} %fusion.41) | data formatting | bytes 262144 | tf_op jit(solution)/shard_map/broadcast_in_dim | solution.py:138
  (6 shorter events, 0.1 us)
Async XLA Ops:
  0.0 61.6 %copy-start = (bf16[1,1,128,1024]{3,2,1,0:T(8,128)(2,1)S(1)}, bf16[1,1,128,1024]{3,2,1,0:T(8,128)(2,1)}, u32[]{:S(2)}) copy-start(bf16[1,1,128,1024]{3,2,1,0:T(8,128)(2,1)} %param.13) | copy-start | bytes 786436
  0.0 15.7 %collective-permute-start.5 = (bf16[8,9,128,128]{3,2,1,0:T(8,128)(2,1)}, bf16[8,9,128,128]{3,2,1,0:T(8,128)(2,1)S(1)}, u32[]{:S(2)}, u32[]{:S(2)}) collective-permute-start(bf16[8,9,128,128]{3,2,1,0:T(8,128)(2,1)} %bitcast.178), channel_id=1, source_target_pairs={{32,0},{96,64},{160,128},{224,192},{288,256},{352,320},{416,384},{... | collective-permute-start | bytes 7077896 | tf_op jit(solution)/shard_map/ppermute | solution.py:21
  9.0 6.7 %collective-permute-start.4 = (bf16[9,2,128,128]{3,2,1,0:T(8,128)(2,1)}, bf16[9,2,128,128]{3,2,1,0:T(8,128)(2,1)S(1)}, u32[]{:S(2)}, u32[]{:S(2)}) collective-permute-start(bf16[9,2,128,128]{3,2,1,0:T(8,128)(2,1)} %bitcast.184), channel_id=1, source_target_pairs={{0,32},{64,96},{128,160},{192,224},{256,288},{320,352},{384,416},{... | collective-permute-start | bytes 1769480 | tf_op jit(solution)/shard_map/ppermute | solution.py:21

commit v3 on v2

v3 whole, which is shorter than its diff:
```python
import functools

import jax
import jax.numpy as jnp
from jax import lax
from jax.experimental import pallas as pl
from jax.experimental.pallas import tpu as pltpu
from jax.sharding import PartitionSpec as P

BOTH = ("bx", "by")
LANES = 128


def pair_gather(values, axis, apart):
    count = lax.axis_size(axis)
    pairs = [[i, i ^ 1 << apart] for i in range(count) if not i >> apart & 1]
    return lax.all_gather(values, axis, axis_index_groups=pairs)


def sent_on(values, step_x, step_y):
    count_x, count_y = lax.axis_size("bx"), lax.axis_size("by")
    moves = []
    for x in range(0, count_x, 2):
        for y in range(count_y):
            to_x, to_y = x + step_x, y + step_y
            if 0 <= to_x < count_x and 0 <= to_y < count_y:
                moves.append((x * count_y + y, to_x * count_y + to_y))
    return lax.ppermute(values, BOTH, moves)


def surroundings(sources):
    below, above = sent_on(sources, 0, 1), sent_on(sources, 0, -1)
    column = jnp.stack([below, sources, above], axis=1)
    before, after = sent_on(column[1], 2, 0), sent_on(column[0], -2, 0)
    return jnp.concatenate([before[None], column, after[None]])


def near_field(around, near_blocks, near_index):
    positions, excite, unknowns = around.shape
    blocks, block_len = near_blocks.shape[0], near_blocks.shape[2]
    source_blocks = around.reshape(positions, excite, blocks, block_len)
    onehot = (
        near_index[:, :, None] == jnp.arange(blocks, dtype=near_index.dtype)[None, None, :]
    ).astype(jnp.bfloat16)
    picked = jnp.einsum(
        "rkb,kcbj->rkcj", onehot, source_blocks, preferred_element_type=jnp.float32
    ).astype(jnp.bfloat16)
    near_sum = jnp.einsum(
        "rkij,rkcj->cri", near_blocks, picked, preferred_element_type=jnp.float32
    )
    return near_sum.reshape(excite, unknowns)


class Packing:
    def __init__(self, mixing_rows, excite, unknowns):
        self.excite, self.blocks = excite, unknowns // LANES
        self.coeffs = mixing_rows
        self.sources = self.coeffs + excite
        self.index = self.sources + self.blocks * excite
        self.rows = self.index + excite


def pack(packing, mixing_hbm, sources_hbm, project_hbm, index_ref, packed, sources, project, sems):
    excite = packing.excite
    wide = [
        pltpu.make_async_copy(sources_hbm, sources, sems.at[0]),
        pltpu.make_async_copy(project_hbm, project, sems.at[1]),
    ]
    for copy in wide:
        copy.start()
    rest = [
        pltpu.make_async_copy(mixing_hbm, packed.at[pl.ds(0, packing.coeffs)], sems.at[2])
    ]
    for block in range(packing.blocks):
        rest.append(
            pltpu.make_async_copy(
                sources_hbm.at[:, pl.ds(block * LANES, LANES)],
                packed.at[pl.ds(packing.sources + block * excite, excite)],
                sems.at[3 + block],
            )
        )
    for copy in rest:
        copy.start()
    rows, positions = index_ref.shape
    index = jnp.concatenate(
        [index_ref[...], jnp.zeros((rows, LANES - positions), jnp.int32)], axis=1
    )
    index = jnp.concatenate([index, jnp.zeros((excite - rows, LANES), jnp.int32)], axis=0)
    packed[pl.ds(packing.index, excite)] = index.astype(jnp.float32).astype(jnp.bfloat16)
    for copy in wide:
        copy.wait()
    packed[pl.ds(packing.coeffs, excite)] = jnp.dot(
        sources[...], project[...], preferred_element_type=jnp.float32
    ).astype(jnp.bfloat16)
    for copy in rest:
        copy.wait()


def packed_own(packing, mixing, sources, project, index):
    rank = project.shape[1]
    return pl.pallas_call(
        functools.partial(pack, packing),
        name="pack",
        out_shape=pltpu.VMEM((packing.rows, LANES), jnp.bfloat16),
        in_specs=[pl.BlockSpec(memory_space=pl.ANY)] * 3
        + [pl.BlockSpec(memory_space=pltpu.VMEM)],
        out_specs=pl.BlockSpec(memory_space=pltpu.VMEM),
        scratch_shapes=[
            pltpu.VMEM(sources.shape, sources.dtype),
            pltpu.VMEM(project.shape, project.dtype),
            pltpu.SemaphoreType.DMA((3 + packing.blocks,)),
        ],
    )(mixing.reshape(-1, rank), sources, project, index)


def first_level(packing, theirs, own, coeffs):
    excite, rank = packing.excite, coeffs.shape[2]
    given = [ref[pl.ds(packing.coeffs, excite)] for ref in (theirs, own)]
    for box, ref in enumerate((theirs, own)):
        pair = jnp.concatenate([given[box], given[1 - box]], axis=1)
        coeffs[box] = jnp.dot(
            pair, ref[pl.ds(0, 2 * rank)], preferred_element_type=jnp.float32
        ).astype(coeffs.dtype)


def mixed(packing, level, place, both, theirs, own):
    axis, apart = place
    rank = both.shape[3]
    upper = lax.axis_index(axis) >> apart & 1
    sums = []
    for box, ref in enumerate((theirs, own)):
        pair = jnp.concatenate([both[upper, box], both[1 - upper, box]], axis=1)
        sums.append(
            jnp.dot(
                pair, ref[pl.ds(level * 2 * rank, 2 * rank)], preferred_element_type=jnp.float32
            ).astype(jnp.bfloat16)
        )
    return sums


def next_level(packing, level, place, both, theirs, own, coeffs):
    for box, value in enumerate(mixed(packing, level, place, both, theirs, own)):
        coeffs[box] = value


def last_level(packing, level, place, both, theirs, own, given, final):
    value, final[...] = mixed(packing, level, place, both, theirs, own)
    rank = value.shape[1]
    given[:, rank:] = jnp.zeros((given.shape[0], given.shape[1] - rank), given.dtype)
    given[:, :rank] = value.astype(given.dtype)


def in_vmem(kernel, name, out_shape, operands):
    return pl.pallas_call(
        kernel,
        name=name,
        out_shape=out_shape,
        in_specs=[pl.BlockSpec(memory_space=pltpu.VMEM)] * operands,
        out_specs=jax.tree.map(lambda _: pl.BlockSpec(memory_space=pltpu.VMEM), out_shape),
    )


def butterfly(packing, theirs, own, rank, unknowns):
    excite = packing.excite
    levels = [("bx", n) for n in range(lax.axis_size("bx").bit_length() - 1)]
    levels += [("by", n) for n in range(lax.axis_size("by").bit_length() - 1)]
    shape = pltpu.VMEM((2, excite, rank), jnp.bfloat16)
    coeffs = in_vmem(functools.partial(first_level, packing), "level_0", shape, 2)(theirs, own)
    for level, place in enumerate(levels):
        if level == 0:
            continue
        both = pair_gather(coeffs, *place)
        kernel = functools.partial(next_level, packing, level, place)
        if level == len(levels) - 1:
            kernel = functools.partial(last_level, packing, level, place)
            shape = (
                pltpu.VMEM((excite, unknowns), jnp.float32),
                pltpu.VMEM((excite, rank), jnp.bfloat16),
            )
        coeffs = in_vmem(kernel, f"level_{level}", shape, 3)(both, theirs, own)
    return coeffs


def per_device(sources, near_blocks, near_index, far_project, far_mixing, far_expand):
    own_sources, own_blocks, own_index = sources[:, 0, 0], near_blocks[0, 0], near_index[0, 0]
    excite, unknowns = own_sources.shape
    rank = far_project.shape[3]
    rows, positions = own_index.shape
    core = lax.axis_index("bx") & 1
    packing = Packing(far_mixing[0, 0].size // rank, excite, unknowns)
    packed = packed_own(packing, far_mixing[0, 0], own_sources, far_project[0, 0], own_index)
    partners = [(i, i ^ 1) for i in range(lax.axis_size("bx"))]
    theirs = lax.ppermute(packed, "bx", partners)
    their_blocks = lax.ppermute(own_blocks, "bx", partners[1::2])

    def near_fields():
        their_sources = theirs[packing.sources : packing.index]
        their_sources = their_sources.reshape(packing.blocks, excite, LANES)
        their_sources = their_sources.transpose(1, 0, 2).reshape(excite, unknowns)
        around = surroundings(jnp.stack([own_sources, their_sources]))
        their_index = theirs[packing.index : packing.index + rows, :positions].astype(jnp.int32)
        mine = near_field(around[:3].reshape(-1, excite, unknowns), own_blocks, own_index)
        given = near_field(around[1:].reshape(-1, excite, unknowns), their_blocks, their_index)
        return mine, given, jnp.zeros((excite, rank), jnp.bfloat16)

    def butterflies():
        given, final = butterfly(packing, theirs, packed, rank, unknowns)
        return given, given, final

    mine, given, final = lax.cond(core == 0, near_fields, butterflies)
    taken = pair_gather(given, "bx", 0)
    near_part = jnp.where(core == 0, mine, taken[0])
    final = jnp.where(core == 0, taken[1, :, :rank].astype(jnp.bfloat16), final)
    far_part = jnp.dot(final, far_expand[0, 0], preferred_element_type=jnp.float32)
    return (near_part + far_part)[:, None, None]


def solution(mesh):
    placed = (
        P(None, "bx", "by", None),
        P("bx", "by", None, None, None, None),
        P("bx", "by", None, None),
        P("bx", "by", None, None),
        P("bx", "by", None, None, None, None),
        P("bx", "by", None, None),
    )
    return jax.shard_map(
        per_device, mesh=mesh, in_specs=placed, out_specs=P(None, "bx", "by", None), check_vma=False
    )
```

time: 63 us -> 65.5 us (1.040)
  Pallas kernels: 2.96 us -> 9.29 us
  matrix products: 2.51 us -> 0.16 us
  local copies, waits for them, and re-layouts: 3.09 us -> 0.82 us
  waiting for transfers between devices: 0.01 us -> 2.08 us
  blocking collectives: 42 us -> 40 us
  starting transfers between devices: 10.3 us -> 12.2 us
  other arithmetic: 1.57 us -> 0.01 us
    pallas_call x1 -> x10, Pallas kernels: 2.96 us -> 9.29 us  [the longest x8 7.17 us: butterfly(): coeffs = in_vmem(kernel, f'level_{level}', shape, 3)(both, theirs, own)]
    dot_general x10 -> x0, matrix products: 2.36 us -> none  [the longest x1 1.15 us: per_device(): jnp.dot(own_sources, far_project[0, 0], preferred_element_type=jnp.float32)]
    squeeze x3 -> x0, local copies, waits for them, and re-layouts: 2.26 us -> none  [the longest x1 1.4 us: butterfly(): ordered[:, at]]
    ppermute x2, waiting for transfers between devices: 0.01 us -> 2.08 us  [the longest x1 2.08 us: per_device(): theirs = lax.ppermute(packed, 'bx', partners)]
    all_gather x10 -> x9, blocking collectives: 42 us -> 40 us  [pair_gather(): return lax.all_gather(values, axis, axis_index_groups=pairs)]
    ppermute x2, starting transfers between devices: 10.3 us -> 12.2 us  [the longest x1 10.3 us: per_device(): their_blocks = lax.ppermute(own_blocks, 'bx', partners[1::2])]
    concatenate x1 -> x0, other arithmetic: 0.85 us -> none  [per_device(): jnp.concatenate([own_sources, coeffs, index_values], axis=1)]
    convert_element_type x1 -> x0, other arithmetic: 0.69 us -> none  [per_device(): own_index.astype(jnp.bfloat16)]
  transfers between devices with their start and end apart: 2 -> 2, of which waited for: 0 -> 1; matrix products, arithmetic and copies ran while one was open for 4% -> 0% of each run, Pallas kernels for 0% -> 3%
where the time goes in v3:
time: 65.5 us; the launch traced here: 64.7 us
  blocking collectives  40 us (61%)
  starting transfers between devices  12.2 us (19%)
  Pallas kernels  9.29 us (14%)
  waiting for transfers between devices  2.08 us (3%)
  local copies, waits for them, and re-layouts  0.82 us (1%)
    all_gather x9, blocking collectives, pair_gather(): return lax.all_gather(values, axis, axis_index_groups=pairs)  40 us
    ppermute x1, starting transfers between devices, per_device(): their_blocks = lax.ppermute(own_blocks, 'bx', partners[1::2])  10.3 us
    pallas_call x8, Pallas kernels, butterfly(): coeffs = in_vmem(kernel, f'level_{level}', shape, 3)(both, theirs, own)  7.17 us
    ppermute x1, waiting for transfers between devices, per_device(): theirs = lax.ppermute(packed, 'bx', partners)  2.08 us
    pallas_call x1, Pallas kernels, packed_own(): pl.pallas_call(functools.partial(pack, packing), name='pack', out_shape=p...  1.98 us
    ppermute x1, starting transfers between devices, per_device(): theirs = lax.ppermute(packed, 'bx', partners)  1.92 us
  transfers between devices with their start and end apart: 2, of which 1 were waited for; matrix products, arithmetic and copies ran while one was open for 0% of the time, Pallas kernels for 3%

profile of v3, /device:TPU:1, one launch (start us, length us, event | category | flops | bytes accessed | tf_op | source)
XLA Modules:
  0.0 64.7 jit_solution(3856381471888219364)
XLA Ops:
  0.0 0.0 copy-start
  0.0 10.3 %collective-permute-start.5 = (bf16[8,9,128,128]{3,2,1,0:T(8,128)(2,1)}, bf16[8,9,128,128]{3,2,1,0:T(8,128)(2,1)}, u32[]{:S(2)}, u32[]{:S(2)}) collective-permute-start(bf16[8,9,128,128]{3,2,1,0:T(8,128)(2,1)} %bitcast.97), channel_id=1, source_target_pairs={{32,0},{96,64},{160,128},{224,192},{288,256},{352,320},{416,384},{... | collective-permute-start | bytes 7077896 | tf_op jit(solution)/shard_map/ppermute | solution.py:194
  10.3 2.0 %pack.1 = bf16[2624,128]{1,0:T(8,128)(2,1)S(1)} custom-call(bf16[2304,128]{1,0:T(8,128)(2,1)} %bitcast.103, bf16[32,1024]{1,0:T(8,128)(2,1)} %bitcast.109, bf16[1024,128]{1,0:T(8,128)(2,1)} %bitcast.108, s32[8,9]{1,0:T(8,128)} %bitcast.123), custom_call_target="tpu_custom_call" | custom-call | tf_op jit(solution)/shard_map/pack/pallas_call | solution.py:101
  12.3 1.9 %collective-permute-start.4 = (bf16[2624,128]{1,0:T(8,128)(2,1)S(1)}, bf16[2624,128]{1,0:T(8,128)(2,1)S(1)}, u32[]{:S(2)}, u32[]{:S(2)}) collective-permute-start(bf16[2624,128]{1,0:T(8,128)(2,1)S(1)} %pack.1), channel_id=1, source_target_pairs={{0,32},{32,0},{64,96},{96,64},{128,160},{160,128},{192,224},{224,1... | collective-permute-start | bytes 2015240 | tf_op jit(solution)/shard_map/ppermute | solution.py:193
  14.2 2.1 %collective-permute-done.4 = bf16[2624,128]{1,0:T(8,128)(2,1)S(1)} collective-permute-done((bf16[2624,128]{1,0:T(8,128)(2,1)S(1)}, bf16[2624,128]{1,0:T(8,128)(2,1)S(1)}, u32[]{:S(2)}, u32[]{:S(2)}) %collective-permute-start.4) | collective-permute-done | bytes 671776 | tf_op jit(solution)/shard_map/ppermute | solution.py:193
  16.3 0.0 collective-permute-done.5
  16.3 45.4 %conditional.1 = (f32[32,1024]{1,0:T(8,128)S(1)}, f32[32,1024]{1,0:T(8,128)S(1)}, bf16[32,128]{1,0:T(8,128)(2,1)S(1)}) conditional(s32[]{:T(128)} %convert_element_type.24, (bf16[2624,128]{1,0:T(8,128)(2,1)S(1)}, bf16[2624,128]{1,0:T(8,128)(2,1)S(1)}) %tuple.13, (bf16[32,1,1,1024]{3,0,2,1:T(8,128)(2,1)}, bf16[2624,128]{1,0:T(8,128)(2,1)S(1)}, ...), branch_computations={%region_0.0_spmd, %region_1.0_spmd} | conditional | flops 163251392 | bytes 30158306 | solution.py:210
  16.3 0.1 level_0.1
  16.5 3.4 %all-gather = bf16[4,32,128]{2,1,0:T(8,128)(2,1)} all-gather(bf16[2,32,128]{2,1,0:T(8,128)(2,1)S(1)} %level_0.1), channel_id=2, replica_groups={{0,64},{32,96},{128,192},{160,224},{256,320},{288,352},{384,448},{416,4..., dimensions={0}, use_global_device_ids=true | all-gather | bytes 49152 | tf_op jit(solution)/shard_map/cond/branch_0_fun/all_gather | solution.py:17
  19.8 0.9 %level_1.1 = bf16[2,32,128]{2,1,0:T(8,128)(2,1)S(1)} custom-call(bf16[2,2,32,128]{3,2,1,0:T(8,128)(2,1)} %bitcast.116, bf16[2624,128]{1,0:T(8,128)(2,1)S(1)} %get-tuple-element.19.theirs, bf16[2624,128]{1,0:T(8,128)(2,1)S(1)} %get-tuple-element.20.own), custom_call_target="tpu_custom_call" | custom-call | tf_op jit(solution)/shard_map/cond/branch_0_fun/level_1/pallas_call | solution.py:180
  20.7 4.9 %all-gather.1 = bf16[4,32,128]{2,1,0:T(8,128)(2,1)} all-gather(bf16[2,32,128]{2,1,0:T(8,128)(2,1)S(1)} %level_1.1), channel_id=3, replica_groups={{0,128},{32,160},{64,192},{96,224},{256,384},{288,416},{320,448},{352,4..., dimensions={0}, use_global_device_ids=true | all-gather | bytes 49152 | tf_op jit(solution)/shard_map/cond/branch_0_fun/all_gather | solution.py:17
  25.6 0.9 %level_2.1 = bf16[2,32,128]{2,1,0:T(8,128)(2,1)S(1)} custom-call(bf16[2,2,32,128]{3,2,1,0:T(8,128)(2,1)} %bitcast.117, bf16[2624,128]{1,0:T(8,128)(2,1)S(1)} %get-tuple-element.19.theirs, bf16[2624,128]{1,0:T(8,128)(2,1)S(1)} %get-tuple-element.20.own), custom_call_target="tpu_custom_call" | custom-call | tf_op jit(solution)/shard_map/cond/branch_0_fun/level_2/pallas_call | solution.py:180
  26.5 7.3 %all-gather.2 = bf16[4,32,128]{2,1,0:T(8,128)(2,1)} all-gather(bf16[2,32,128]{2,1,0:T(8,128)(2,1)S(1)} %level_2.1), channel_id=4, replica_groups={{0,256},{32,288},{64,320},{96,352},{128,384},{160,416},{192,448},{224,4..., dimensions={0}, use_global_device_ids=true | all-gather | bytes 49152 | tf_op jit(solution)/shard_map/cond/branch_0_fun/all_gather | solution.py:17
  33.8 0.9 %level_3.1 = bf16[2,32,128]{2,1,0:T(8,128)(2,1)S(1)} custom-call(bf16[2,2,32,128]{3,2,1,0:T(8,128)(2,1)} %bitcast.118, bf16[2624,128]{1,0:T(8,128)(2,1)S(1)} %get-tuple-element.19.theirs, bf16[2624,128]{1,0:T(8,128)(2,1)S(1)} %get-tuple-element.20.own), custom_call_target="tpu_custom_call" | custom-call | tf_op jit(solution)/shard_map/cond/branch_0_fun/level_3/pallas_call | solution.py:180
  34.7 3.4 %all-gather.3 = bf16[4,32,128]{2,1,0:T(8,128)(2,1)} all-gather(bf16[2,32,128]{2,1,0:T(8,128)(2,1)S(1)} %level_3.1), channel_id=5, replica_groups={{0,1},{2,3},{4,5},{6,7},{8,9},{10,11},{12,13},{14,15},{16,17},{18,19},{..., dimensions={0}, use_global_device_ids=true | all-gather | bytes 49152 | tf_op jit(solution)/shard_map/cond/branch_0_fun/all_gather | solution.py:17
  38.0 0.9 %level_4.1 = bf16[2,32,128]{2,1,0:T(8,128)(2,1)S(1)} custom-call(bf16[2,2,32,128]{3,2,1,0:T(8,128)(2,1)} %bitcast.119, bf16[2624,128]{1,0:T(8,128)(2,1)S(1)} %get-tuple-element.19.theirs, bf16[2624,128]{1,0:T(8,128)(2,1)S(1)} %get-tuple-element.20.own), custom_call_target="tpu_custom_call" | custom-call | tf_op jit(solution)/shard_map/cond/branch_0_fun/level_4/pallas_call | solution.py:180
  38.9 4.3 %all-gather.4 = bf16[4,32,128]{2,1,0:T(8,128)(2,1)} all-gather(bf16[2,32,128]{2,1,0:T(8,128)(2,1)S(1)} %level_4.1), channel_id=6, replica_groups={{0,2},{1,3},{4,6},{5,7},{8,10},{9,11},{12,14},{13,15},{16,18},{17,19},{..., dimensions={0}, use_global_device_ids=true | all-gather | bytes 49152 | tf_op jit(solution)/shard_map/cond/branch_0_fun/all_gather | solution.py:17
  43.2 0.9 %level_5.1 = bf16[2,32,128]{2,1,0:T(8,128)(2,1)S(1)} custom-call(bf16[2,2,32,128]{3,2,1,0:T(8,128)(2,1)} %bitcast.120, bf16[2624,128]{1,0:T(8,128)(2,1)S(1)} %get-tuple-element.19.theirs, bf16[2624,128]{1,0:T(8,128)(2,1)S(1)} %get-tuple-element.20.own), custom_call_target="tpu_custom_call" | custom-call | tf_op jit(solution)/shard_map/cond/branch_0_fun/level_5/pallas_call | solution.py:180
  44.1 7.3 %all-gather.5 = bf16[4,32,128]{2,1,0:T(8,128)(2,1)} all-gather(bf16[2,32,128]{2,1,0:T(8,128)(2,1)S(1)} %level_5.1), channel_id=7, replica_groups={{0,4},{1,5},{2,6},{3,7},{8,12},{9,13},{10,14},{11,15},{16,20},{17,21},{..., dimensions={0}, use_global_device_ids=true | all-gather | bytes 49152 | tf_op jit(solution)/shard_map/cond/branch_0_fun/all_gather | solution.py:17
  51.4 0.9 %level_6.1 = bf16[2,32,128]{2,1,0:T(8,128)(2,1)S(1)} custom-call(bf16[2,2,32,128]{3,2,1,0:T(8,128)(2,1)} %bitcast.121, bf16[2624,128]{1,0:T(8,128)(2,1)S(1)} %get-tuple-element.19.theirs, bf16[2624,128]{1,0:T(8,128)(2,1)S(1)} %get-tuple-element.20.own), custom_call_target="tpu_custom_call" | custom-call | tf_op jit(solution)/shard_map/cond/branch_0_fun/level_6/pallas_call | solution.py:180
  52.3 3.4 %all-gather.6 = bf16[4,32,128]{2,1,0:T(8,128)(2,1)} all-gather(bf16[2,32,128]{2,1,0:T(8,128)(2,1)S(1)} %level_6.1), channel_id=8, replica_groups={{0,8},{1,9},{2,10},{3,11},{4,12},{5,13},{6,14},{7,15},{16,24},{17,25},{..., dimensions={0}, use_global_device_ids=true | all-gather | bytes 49152 | tf_op jit(solution)/shard_map/cond/branch_0_fun/all_gather | solution.py:17
  55.6 0.9 %level_7.1 = bf16[2,32,128]{2,1,0:T(8,128)(2,1)S(1)} custom-call(bf16[2,2,32,128]{3,2,1,0:T(8,128)(2,1)} %bitcast.122, bf16[2624,128]{1,0:T(8,128)(2,1)S(1)} %get-tuple-element.19.theirs, bf16[2624,128]{1,0:T(8,128)(2,1)S(1)} %get-tuple-element.20.own), custom_call_target="tpu_custom_call" | custom-call | tf_op jit(solution)/shard_map/cond/branch_0_fun/level_7/pallas_call | solution.py:180
  56.5 4.3 %all-gather.7 = bf16[4,32,128]{2,1,0:T(8,128)(2,1)} all-gather(bf16[2,32,128]{2,1,0:T(8,128)(2,1)S(1)} %level_7.1), channel_id=9, replica_groups={{0,16},{1,17},{2,18},{3,19},{4,20},{5,21},{6,22},{7,23},{8,24},{9,25},{..., dimensions={0}, use_global_device_ids=true | all-gather | bytes 49152 | tf_op jit(solution)/shard_map/cond/branch_0_fun/all_gather | solution.py:17
  60.8 0.9 %level_8.1 = (f32[32,1024]{1,0:T(8,128)S(1)}, bf16[32,128]{1,0:T(8,128)(2,1)S(1)}) custom-call(bf16[2,2,32,128]{3,2,1,0:T(8,128)(2,1)} %bitcast.115, bf16[2624,128]{1,0:T(8,128)(2,1)S(1)} %get-tuple-element.19.theirs, bf16[2624,128]{1,0:T(8,128)(2,1)S(1)} %get-tuple-element.20.own), custom_call_target="tpu_custom_call" | custom-call | tf_op jit(solution)/shard_map/cond/branch_0_fun/level_8/pallas_call | solution.py:180
  61.7 2.0 %all-gather.8 = f32[64,1024]{1,0:T(8,128)S(1)} all-gather(f32[32,1024]{1,0:T(8,128)S(1)} %get-tuple-element.32), channel_id=10, replica_groups={{0,32},{64,96},{128,160},{192,224},{256,288},{320,352},{384,416},{448,4..., dimensions={0}, use_global_device_ids=true | all-gather | bytes 393216 | tf_op jit(solution)/shard_map/all_gather | solution.py:17
  63.7 0.0 copy-done
  63.7 0.2 fusion.16
  63.9 0.8 %copy.43 = f32[32,1,1,1024]{3,2,1,0:T(1,128)} copy(f32[32,1,1,1024]{3,0,2,1:T(8,128)S(1)} %fusion.16) | data formatting | bytes 262144 | tf_op jit(solution)/shard_map/broadcast_in_dim | solution.py:215
  (2 shorter events, 0.0 us)
Async XLA Ops:
  0.0 63.7 %copy-start = (bf16[1,1,128,1024]{3,2,1,0:T(8,128)(2,1)S(1)}, bf16[1,1,128,1024]{3,2,1,0:T(8,128)(2,1)}, u32[]{:S(2)}) copy-start(bf16[1,1,128,1024]{3,2,1,0:T(8,128)(2,1)} %param.13) | copy-start | bytes 786436
  0.0 16.3 %collective-permute-start.5 = (bf16[8,9,128,128]{3,2,1,0:T(8,128)(2,1)}, bf16[8,9,128,128]{3,2,1,0:T(8,128)(2,1)}, u32[]{:S(2)}, u32[]{:S(2)}) collective-permute-start(bf16[8,9,128,128]{3,2,1,0:T(8,128)(2,1)} %bitcast.97), channel_id=1, source_target_pairs={{32,0},{96,64},{160,128},{224,192},{288,256},{352,320},{416,384},{... | collective-permute-start | bytes 7077896 | tf_op jit(solution)/shard_map/ppermute | solution.py:194
  12.3 4.0 %collective-permute-start.4 = (bf16[2624,128]{1,0:T(8,128)(2,1)S(1)}, bf16[2624,128]{1,0:T(8,128)(2,1)S(1)}, u32[]{:S(2)}, u32[]{:S(2)}) collective-permute-start(bf16[2624,128]{1,0:T(8,128)(2,1)S(1)} %pack.1), channel_id=1, source_target_pairs={{0,32},{32,0},{64,96},{96,64},{128,160},{160,128},{192,224},{224,1... | collective-permute-start | bytes 2015240 | tf_op jit(solution)/shard_map/ppermute | solution.py:193

commit v4 on v3

v4 whole, which is shorter than its diff:
```python
import functools

import jax
import jax.numpy as jnp
from jax import lax
from jax.experimental import pallas as pl
from jax.experimental.pallas import tpu as pltpu
from jax.sharding import PartitionSpec as P

BOTH = ("bx", "by")
LANES = 128


def pair_gather(values, axis, apart):
    count = lax.axis_size(axis)
    pairs = [[i, i ^ 1 << apart] for i in range(count) if not i >> apart & 1]
    return lax.all_gather(values, axis, axis_index_groups=pairs)


def sent_on(values, step_x, step_y):
    count_x, count_y = lax.axis_size("bx"), lax.axis_size("by")
    moves = []
    for x in range(0, count_x, 2):
        for y in range(count_y):
            to_x, to_y = x + step_x, y + step_y
            if 0 <= to_x < count_x and 0 <= to_y < count_y:
                moves.append((x * count_y + y, to_x * count_y + to_y))
    return lax.ppermute(values, BOTH, moves)


def surroundings(sources):
    before, after = sent_on(sources[1], 2, 0), sent_on(sources[0], -2, 0)
    row = jnp.concatenate([before[None], sources, after[None]])
    return jnp.stack([sent_on(row, 0, 1), row, sent_on(row, 0, -1)], axis=1)


def near_field(around, near_blocks, near_index):
    blocks, excite, lanes = around.shape[2:]
    source_blocks = around.reshape(-1, blocks, excite, lanes)
    onehot = (
        near_index[:, :, None] == jnp.arange(blocks, dtype=near_index.dtype)[None, None, :]
    ).astype(jnp.bfloat16)
    picked = jnp.einsum(
        "rkb,kbcj->rkcj", onehot, source_blocks, preferred_element_type=jnp.float32
    ).astype(jnp.bfloat16)
    near_sum = jnp.einsum(
        "rkij,rkcj->cri", near_blocks, picked, preferred_element_type=jnp.float32
    )
    return near_sum.reshape(excite, blocks * lanes)


class Packing:
    def __init__(self, levels, rank, excite, unknowns):
        self.excite, self.blocks = excite, unknowns // LANES
        self.split = levels // 2
        self.level_rows = 2 * rank
        self.coeffs = self.split * self.level_rows
        self.sources = self.coeffs + excite
        self.index = self.sources + self.blocks * excite
        self.rows = (self.index + excite, (levels - self.split) * self.level_rows)

    def of_level(self, level):
        late = level >= self.split
        return int(late), pl.ds((level - self.split * late) * self.level_rows, self.level_rows)


def pack(
    packing, mixing_hbm, sources_hbm, project_hbm, index_ref, packed, later, sources, project, sems
):
    excite = packing.excite
    wide = [
        pltpu.make_async_copy(sources_hbm, sources, sems.at[0]),
        pltpu.make_async_copy(project_hbm, project, sems.at[1]),
    ]
    for copy in wide:
        copy.start()
    rest = [
        pltpu.make_async_copy(
            mixing_hbm.at[pl.ds(0, packing.coeffs)],
            packed.at[pl.ds(0, packing.coeffs)],
            sems.at[2],
        ),
        pltpu.make_async_copy(
            mixing_hbm.at[pl.ds(packing.coeffs, packing.rows[1])], later, sems.at[3]
        ),
    ]
    for block in range(packing.blocks):
        rest.append(
            pltpu.make_async_copy(
                sources_hbm.at[:, pl.ds(block * LANES, LANES)],
                packed.at[pl.ds(packing.sources + block * excite, excite)],
                sems.at[4 + block],
            )
        )
    for copy in rest:
        copy.start()
    rows, positions = index_ref.shape
    index = jnp.concatenate(
        [index_ref[...], jnp.zeros((rows, LANES - positions), jnp.int32)], axis=1
    )
    index = jnp.concatenate([index, jnp.zeros((excite - rows, LANES), jnp.int32)], axis=0)
    packed[pl.ds(packing.index, excite)] = index.astype(jnp.float32).astype(jnp.bfloat16)
    for copy in wide:
        copy.wait()
    packed[pl.ds(packing.coeffs, excite)] = jnp.dot(
        sources[...], project[...], preferred_element_type=jnp.float32
    ).astype(jnp.bfloat16)
    for copy in rest:
        copy.wait()


def packed_own(packing, mixing, sources, project, index):
    vmem = pl.BlockSpec(memory_space=pltpu.VMEM)
    return pl.pallas_call(
        functools.partial(pack, packing),
        name="pack",
        out_shape=tuple(pltpu.VMEM((rows, LANES), jnp.bfloat16) for rows in packing.rows),
        in_specs=[pl.BlockSpec(memory_space=pl.ANY)] * 3 + [vmem],
        out_specs=(vmem, vmem),
        scratch_shapes=[
            pltpu.VMEM(sources.shape, sources.dtype),
            pltpu.VMEM(project.shape, project.dtype),
            pltpu.SemaphoreType.DMA((4 + packing.blocks,)),
        ],
    )(mixing.reshape(-1, LANES), sources, project, index)


def first_level(packing, early, coeffs):
    given = [early[box, pl.ds(packing.coeffs, packing.excite)] for box in range(2)]
    rows = packing.of_level(0)[1]
    for box in range(2):
        pair = jnp.concatenate([given[box], given[1 - box]], axis=1)
        coeffs[box] = jnp.dot(
            pair, early[box, rows], preferred_element_type=jnp.float32
        ).astype(coeffs.dtype)


def mixed(packing, level, place, both, blocks):
    axis, apart = place
    upper = lax.axis_index(axis) >> apart & 1
    rows = packing.of_level(level)[1]
    sums = []
    for box in range(2):
        pair = jnp.concatenate([both[upper, box], both[1 - upper, box]], axis=1)
        sums.append(
            jnp.dot(pair, blocks[box, rows], preferred_element_type=jnp.float32).astype(
                jnp.bfloat16
            )
        )
    return sums


def next_level(packing, level, place, both, blocks, coeffs):
    for box, value in enumerate(mixed(packing, level, place, both, blocks)):
        coeffs[box] = value


def last_level(packing, level, place, both, blocks, given, final):
    value, final[...] = mixed(packing, level, place, both, blocks)
    rank = value.shape[1]
    given[:, rank:] = jnp.zeros((given.shape[0], given.shape[1] - rank), given.dtype)
    given[:, :rank] = value.astype(given.dtype)


def in_vmem(kernel, name, out_shape, operands):
    vmem = pl.BlockSpec(memory_space=pltpu.VMEM)
    call = pl.pallas_call(
        kernel,
        name=name,
        out_shape=out_shape,
        in_specs=[vmem] * len(operands),
        out_specs=jax.tree.map(lambda _: vmem, out_shape),
    )
    return call(*(pltpu.with_memory_space_constraint(x, pltpu.VMEM) for x in operands))


def butterfly_levels(packing, shared, levels, coeffs, first, last, unknowns):
    excite, rank = packing.excite, LANES
    for level in range(first, last):
        if level == 0:
            shape = pltpu.VMEM((2, excite, rank), jnp.bfloat16)
            kernel = functools.partial(first_level, packing)
            coeffs = in_vmem(kernel, "level_0", shape, (shared[0],))
            continue
        place = levels[level]
        both = pair_gather(coeffs, *place)
        kernel = functools.partial(next_level, packing, level, place)
        shape = pltpu.VMEM((2, excite, rank), jnp.bfloat16)
        if level == len(levels) - 1:
            kernel = functools.partial(last_level, packing, level, place)
            shape = (
                pltpu.VMEM((excite, unknowns), jnp.float32),
                pltpu.VMEM((excite, rank), jnp.bfloat16),
            )
        blocks = shared[packing.of_level(level)[0]]
        coeffs = in_vmem(kernel, f"level_{level}", shape, (both, blocks))
    return coeffs


def per_device(sources, near_blocks, near_index, far_project, far_mixing, far_expand):
    own_sources, own_blocks, own_index = sources[:, 0, 0], near_blocks[0, 0], near_index[0, 0]
    excite, unknowns = own_sources.shape
    rank = far_project.shape[3]
    rows, positions = own_index.shape
    first_of_pair = lax.axis_index("bx") & 1 == 0
    levels = [("bx", n) for n in range(lax.axis_size("bx").bit_length() - 1)]
    levels += [("by", n) for n in range(lax.axis_size("by").bit_length() - 1)]
    packing = Packing(len(levels), rank, excite, unknowns)
    packed = packed_own(packing, far_mixing[0, 0], own_sources, far_project[0, 0], own_index)
    shared = tuple(pair_gather(array, "bx", 0) for array in packed)
    butterfly = functools.partial(butterfly_levels, packing, shared, levels, unknowns=unknowns)
    late = len(levels) - 3

    def gathering():
        boxes = shared[0][:, packing.sources : packing.index]
        around = surroundings(boxes.reshape(2, packing.blocks, excite, LANES))
        return around, jnp.zeros((2, excite, rank), jnp.bfloat16)

    def levels_early():
        around = jnp.zeros((4, 3, packing.blocks, excite, LANES), jnp.bfloat16)
        return around, butterfly(None, 0, late)

    around, coeffs = lax.cond(first_of_pair, gathering, levels_early)
    handed_blocks, coeffs = lax.optimization_barrier((own_blocks, coeffs))
    handed = [(i, i ^ 1) for i in range(1, lax.axis_size("bx"), 2)]
    their_blocks = lax.ppermute(handed_blocks, "bx", handed)

    def near_own():
        return near_field(around[:3], own_blocks, own_index), coeffs

    def level_between():
        return jnp.zeros((excite, unknowns), jnp.float32), butterfly(coeffs, late, late + 1)

    mine, coeffs = lax.cond(first_of_pair, near_own, level_between)

    def near_other():
        index = shared[0][1, packing.index : packing.index + rows, :positions].astype(jnp.int32)
        return near_field(around[1:], their_blocks, index), jnp.zeros((excite, rank), jnp.bfloat16)

    def levels_late():
        return tuple(butterfly(coeffs, late + 1, len(levels)))

    given, final = lax.cond(first_of_pair, near_other, levels_late)
    taken = pair_gather(given, "bx", 0)
    near_part = jnp.where(first_of_pair, mine, taken[0])
    final = jnp.where(first_of_pair, taken[1, :, :rank].astype(jnp.bfloat16), final)
    far_part = jnp.dot(final, far_expand[0, 0], preferred_element_type=jnp.float32)
    return (near_part + far_part)[:, None, None]


def solution(mesh):
    placed = (
        P(None, "bx", "by", None),
        P("bx", "by", None, None, None, None),
        P("bx", "by", None, None),
        P("bx", "by", None, None),
        P("bx", "by", None, None, None, None),
        P("bx", "by", None, None),
    )
    return jax.shard_map(
        per_device, mesh=mesh, in_specs=placed, out_specs=P(None, "bx", "by", None), check_vma=False
    )
```

time: 65.5 us -> 59.9 us (0.915)
  the two profiles are of different devices: /device:TPU:1 before, /device:TPU:449 now
where the time goes in v4:
time: 59.9 us; the launch traced here: 59.6 us
  blocking collectives  44.5 us (74%)
  starting transfers between devices  10.6 us (18%)
  Pallas kernels  3.23 us (5%)
  local copies, waits for them, and re-layouts  0.96 us (2%)
    all_gather x11, blocking collectives, pair_gather(): return lax.all_gather(values, axis, axis_index_groups=pairs)  44.5 us
    ppermute x1, starting transfers between devices, per_device(): their_blocks = lax.ppermute(handed_blocks, 'bx', handed)  10.6 us
    pallas_call x1, Pallas kernels, packed_own(): pl.pallas_call(functools.partial(pack, packing), name='pack', out_shape=t...  2.02 us
    pallas_call x9, Pallas kernels, in_vmem(): call(*(pltpu.with_memory_space_constraint(x, pltpu.VMEM) for x in operands))  1.21 us
  transfers between devices with their start and end apart: 1, of which 0 were waited for; matrix products, arithmetic and copies ran while one was open for 0% of the time, Pallas kernels for 0%

profile of v4, /device:TPU:449, one launch (start us, length us, event | category | flops | bytes accessed | tf_op | source)
XLA Modules:
  0.0 59.6 jit_solution(15459372747109922519)
XLA Ops:
  0.0 0.0 copy-start
  0.0 2.0 %pack.1 = (bf16[1344,128]{1,0:T(8,128)(2,1)S(1)}, bf16[1280,128]{1,0:T(8,128)(2,1)S(1)}) custom-call(bf16[2304,128]{1,0:T(8,128)(2,1)} %bitcast.100, bf16[32,1024]{1,0:T(8,128)(2,1)} %bitcast.107, bf16[1024,128]{1,0:T(8,128)(2,1)} %bitcast.103, s32[8,9]{1,0:T(8,128)} %bitcast.112), custom_call_target="tpu_custom_call" | custom-call | tf_op jit(solution)/shard_map/pack/pallas_call | solution.py:114
  2.0 2.6 %all-gather.8 = bf16[2688,128]{1,0:T(8,128)(2,1)S(1)} all-gather(bf16[1344,128]{1,0:T(8,128)(2,1)S(1)} %get-tuple-element.55), channel_id=10, replica_groups={{0,32},{64,96},{128,160},{192,224},{256,288},{320,352},{384,416},{448,4..., dimensions={0}, use_global_device_ids=true | all-gather | bytes 1032192 | tf_op jit(solution)/shard_map/all_gather | solution.py:17
  4.6 2.3 %all-gather.9 = bf16[2560,128]{1,0:T(8,128)(2,1)S(1)} all-gather(bf16[1280,128]{1,0:T(8,128)(2,1)S(1)} %get-tuple-element.56), channel_id=11, replica_groups={{0,32},{64,96},{128,160},{192,224},{256,288},{320,352},{384,416},{448,4..., dimensions={0}, use_global_device_ids=true | all-gather | bytes 983040 | tf_op jit(solution)/shard_map/all_gather | solution.py:17
  6.9 0.0 copy-start.1
  6.9 24.0 %conditional.3 = (bf16[4,3,8,32,128]{4,3,2,1,0:T(8,128)(2,1)S(1)}, bf16[2,32,128]{2,1,0:T(8,128)(2,1)S(1)}) conditional(s32[]{:T(128)} %convert_element_type.33, (bf16[2,1344,128]{2,1,0:T(8,128)(2,1)S(1)}, bf16[2,1280,128]{2,1,0:T(8,128)(2,1)S(1)}) %tuple.50, bf16[2,1344,128]{2,1,0:T(8,128)(2,1)S(1)} %bitcast.84), branch_computations={%region_0.0_spmd, %region_1.0_spmd} | conditional | flops 1048576 | bytes 5521586 | solution.py:223
  6.9 0.1 level_0.1
  7.0 3.3 %all-gather = bf16[4,32,128]{2,1,0:T(8,128)(2,1)S(1)} all-gather(bf16[2,32,128]{2,1,0:T(8,128)(2,1)S(1)} %level_0.1), channel_id=2, replica_groups={{0,64},{32,96},{128,192},{160,224},{256,320},{288,352},{384,448},{416,4..., dimensions={0}, use_global_device_ids=true | all-gather | bytes 49152 | tf_op jit(solution)/shard_map/cond/branch_0_fun/all_gather | solution.py:17
  10.3 0.1 level_1.1
  10.4 4.8 %all-gather.1 = bf16[4,32,128]{2,1,0:T(8,128)(2,1)S(1)} all-gather(bf16[2,32,128]{2,1,0:T(8,128)(2,1)S(1)} %level_1.1), channel_id=3, replica_groups={{0,128},{32,160},{64,192},{96,224},{256,384},{288,416},{320,448},{352,4..., dimensions={0}, use_global_device_ids=true | all-gather | bytes 49152 | tf_op jit(solution)/shard_map/cond/branch_0_fun/all_gather | solution.py:17
  15.2 0.1 level_2.1
  15.3 7.5 %all-gather.2 = bf16[4,32,128]{2,1,0:T(8,128)(2,1)S(1)} all-gather(bf16[2,32,128]{2,1,0:T(8,128)(2,1)S(1)} %level_2.1), channel_id=4, replica_groups={{0,256},{32,288},{64,320},{96,352},{128,384},{160,416},{192,448},{224,4..., dimensions={0}, use_global_device_ids=true | all-gather | bytes 49152 | tf_op jit(solution)/shard_map/cond/branch_0_fun/all_gather | solution.py:17
  22.8 0.1 level_3.1
  22.9 3.3 %all-gather.3 = bf16[4,32,128]{2,1,0:T(8,128)(2,1)S(1)} all-gather(bf16[2,32,128]{2,1,0:T(8,128)(2,1)S(1)} %level_3.1), channel_id=5, replica_groups={{0,1},{2,3},{4,5},{6,7},{8,9},{10,11},{12,13},{14,15},{16,17},{18,19},{..., dimensions={0}, use_global_device_ids=true | all-gather | bytes 49152 | tf_op jit(solution)/shard_map/cond/branch_0_fun/all_gather | solution.py:17
  26.2 0.1 level_4.1
  26.3 4.3 %all-gather.4 = bf16[4,32,128]{2,1,0:T(8,128)(2,1)S(1)} all-gather(bf16[2,32,128]{2,1,0:T(8,128)(2,1)S(1)} %level_4.1), channel_id=6, replica_groups={{0,2},{1,3},{4,6},{5,7},{8,10},{9,11},{12,14},{13,15},{16,18},{17,19},{..., dimensions={0}, use_global_device_ids=true | all-gather | bytes 49152 | tf_op jit(solution)/shard_map/cond/branch_0_fun/all_gather | solution.py:17
  30.6 0.1 level_5.1
  30.8 0.1 broadcast.8
  30.9 10.6 %collective-permute-start.4 = (bf16[8,9,128,128]{3,2,1,0:T(8,128)(2,1)}, bf16[8,9,128,128]{3,2,1,0:T(8,128)(2,1)}, u32[]{:S(2)}, u32[]{:S(2)}) collective-permute-start(bf16[8,9,128,128]{3,2,1,0:T(8,128)(2,1)} %bitcast.96), channel_id=1, source_target_pairs={{32,0},{96,64},{160,128},{224,192},{288,256},{352,320},{416,384},{... | collective-permute-start | bytes 7077896 | tf_op jit(solution)/shard_map/ppermute | solution.py:226
  41.5 0.0 copy-done.1
  41.5 7.3 %conditional.4 = (f32[32,1024]{1,0:T(8,128)S(1)}, bf16[2,32,128]{2,1,0:T(8,128)(2,1)S(1)}) conditional(s32[]{:T(128)} %convert_element_type.33, (bf16[2,32,128]{2,1,0:T(8,128)(2,1)S(1)}, bf16[2,1280,128]{2,1,0:T(8,128)(2,1)S(1)}) %tuple.48, (s32[1,1,8,9]{3,2,1,0:T(8,128)S(1)}, bf16[4,3,8,32,128]{4,3,2,1,0:T(8,128)(2,1)S(1)}, ...), branch_computations={%region_2.0_spmd, %region_3.0_spmd} | conditional | flops 80511552 | bytes 7275376 | solution.py:234
  41.5 7.1 %all-gather.5 = bf16[4,32,128]{2,1,0:T(8,128)(2,1)S(1)} all-gather(bf16[2,32,128]{2,1,0:T(8,128)(2,1)S(1)} %get-tuple-element.34), channel_id=7, replica_groups={{0,4},{1,5},{2,6},{3,7},{8,12},{9,13},{10,14},{11,15},{16,20},{17,21},{..., dimensions={0}, use_global_device_ids=true | all-gather | bytes 49152 | tf_op jit(solution)/shard_map/cond/branch_0_fun/all_gather | solution.py:17
  48.7 0.1 level_6.1
  48.9 0.0 collective-permute-done.4
  48.9 7.7 %conditional.5 = ((f32[32,1024]{1,0:T(8,128)S(1)}, bf16[32,128]{1,0:T(8,128)(2,1)S(1)})) conditional(s32[]{:T(128)} %convert_element_type.33, (bf16[2,32,128]{2,1,0:T(8,128)(2,1)S(1)}, bf16[2,1280,128]{2,1,0:T(8,128)(2,1)S(1)}) %tuple.49, (bf16[2,1344,128]{2,1,0:T(8,128)(2,1)S(1)}, bf16[4,3,8,32,128]{4,3,2,1,0:T(8,128)(2,1)S(1)}, ...), branch_computations={%region_4.0_spmd, %region_5.0_spmd} | conditional | flops 80511624 | bytes 7284010 | solution.py:243
  48.9 3.3 %all-gather.6 = bf16[4,32,128]{2,1,0:T(8,128)(2,1)S(1)} all-gather(bf16[2,32,128]{2,1,0:T(8,128)(2,1)S(1)} %get-tuple-element.40), channel_id=8, replica_groups={{0,8},{1,9},{2,10},{3,11},{4,12},{5,13},{6,14},{7,15},{16,24},{17,25},{..., dimensions={0}, use_global_device_ids=true | all-gather | bytes 49152 | tf_op jit(solution)/shard_map/cond/branch_0_fun/all_gather | solution.py:17
  52.1 0.1 level_7.1
  52.3 4.2 %all-gather.7 = bf16[4,32,128]{2,1,0:T(8,128)(2,1)S(1)} all-gather(bf16[2,32,128]{2,1,0:T(8,128)(2,1)S(1)} %level_7.1), channel_id=9, replica_groups={{0,16},{1,17},{2,18},{3,19},{4,20},{5,21},{6,22},{7,23},{8,24},{9,25},{..., dimensions={0}, use_global_device_ids=true | all-gather | bytes 49152 | tf_op jit(solution)/shard_map/cond/branch_0_fun/all_gather | solution.py:17
  56.4 0.1 level_8.1
  56.6 2.0 %all-gather.10 = f32[64,1024]{1,0:T(8,128)S(1)} all-gather(f32[32,1024]{1,0:T(8,128)S(1)} %get-tuple-element.63), channel_id=12, replica_groups={{0,32},{64,96},{128,160},{192,224},{256,288},{320,352},{384,416},{448,4..., dimensions={0}, use_global_device_ids=true | all-gather | bytes 393216 | tf_op jit(solution)/shard_map/all_gather | solution.py:17
  58.6 0.0 copy-done
  58.6 0.2 fusion.11
  58.8 0.8 %copy.25 = f32[32,1,1,1024]{3,2,1,0:T(1,128)} copy(f32[32,1,1,1024]{3,0,2,1:T(8,128)S(1)} %fusion.11) | data formatting | bytes 262144 | tf_op jit(solution)/shard_map/broadcast_in_dim | solution.py:248
  (2 shorter events, 0.0 us)
Async XLA Ops:
  0.0 58.6 %copy-start = (bf16[1,1,128,1024]{3,2,1,0:T(8,128)(2,1)S(1)}, bf16[1,1,128,1024]{3,2,1,0:T(8,128)(2,1)}, u32[]{:S(2)}) copy-start(bf16[1,1,128,1024]{3,2,1,0:T(8,128)(2,1)} %param.17) | copy-start | bytes 786436
  6.9 34.6 %copy-start.1 = (s32[1,1,8,9]{3,2,1,0:T(8,128)S(1)}, s32[1,1,8,9]{3,2,1,0:T(8,128)}, u32[]{:S(2)}) copy-start(s32[1,1,8,9]{3,2,1,0:T(8,128)} %param.14) | copy-start | bytes 868
  30.9 17.9 %collective-permute-start.4 = (bf16[8,9,128,128]{3,2,1,0:T(8,128)(2,1)}, bf16[8,9,128,128]{3,2,1,0:T(8,128)(2,1)}, u32[]{:S(2)}, u32[]{:S(2)}) collective-permute-start(bf16[8,9,128,128]{3,2,1,0:T(8,128)(2,1)} %bitcast.96), channel_id=1, source_target_pairs={{32,0},{96,64},{160,128},{224,192},{288,256},{352,320},{416,384},{... | collective-permute-start | bytes 7077896 | tf_op jit(solution)/shard_map/ppermute | solution.py:226

commit v5 on v4

v5 whole, which is shorter than its diff:
```python
import functools

import jax
import jax.numpy as jnp
from jax import lax
from jax.experimental import pallas as pl
from jax.experimental.pallas import tpu as pltpu
from jax.sharding import PartitionSpec as P

BOTH = ("bx", "by")
LANES = 128


def pair_gather(values, axis, apart):
    count = lax.axis_size(axis)
    pairs = [[i, i ^ 1 << apart] for i in range(count) if not i >> apart & 1]
    return lax.all_gather(values, axis, axis_index_groups=pairs)


def sent_on(values, step_x, step_y):
    count_x, count_y = lax.axis_size("bx"), lax.axis_size("by")
    moves = []
    for x in range(0, count_x, 2):
        for y in range(count_y):
            to_x, to_y = x + step_x, y + step_y
            if 0 <= to_x < count_x and 0 <= to_y < count_y:
                moves.append((x * count_y + y, to_x * count_y + to_y))
    return lax.ppermute(values, BOTH, moves)


class Packing:
    def __init__(self, levels, rank, excite, unknowns):
        self.excite, self.blocks = excite, unknowns // LANES
        self.split = levels // 2
        self.level_rows = 2 * rank
        self.box_rows = self.blocks * excite
        self.coeffs = self.split * self.level_rows
        self.sources = self.coeffs + excite
        self.first_rows = self.sources + self.box_rows
        self.second_rows = (levels - self.split) * self.level_rows
        self.final = 7 * self.box_rows
        self.third_rows = self.final + excite

    def place_of(self, level):
        return (level if level < self.split else level - self.split) * self.level_rows


def pack(packing, mixing_hbm, sources_hbm, project_hbm, packed, later, sources, project, sems):
    excite = packing.excite
    wide = [
        pltpu.make_async_copy(sources_hbm, sources, sems.at[0]),
        pltpu.make_async_copy(project_hbm, project, sems.at[1]),
    ]
    for copy in wide:
        copy.start()
    rest = [
        pltpu.make_async_copy(
            mixing_hbm.at[pl.ds(0, packing.coeffs)],
            packed.at[pl.ds(0, packing.coeffs)],
            sems.at[2],
        ),
        pltpu.make_async_copy(
            mixing_hbm.at[pl.ds(packing.coeffs, packing.second_rows)], later, sems.at[3]
        ),
    ]
    for block in range(packing.blocks):
        rest.append(
            pltpu.make_async_copy(
                sources_hbm.at[:, pl.ds(block * LANES, LANES)],
                packed.at[pl.ds(packing.sources + block * excite, excite)],
                sems.at[4 + block],
            )
        )
    for copy in rest:
        copy.start()
    for copy in wide:
        copy.wait()
    packed[pl.ds(packing.coeffs, excite)] = jnp.dot(
        sources[...], project[...], preferred_element_type=jnp.float32
    ).astype(jnp.bfloat16)
    for copy in rest:
        copy.wait()


def packed_own(packing, mixing, sources, project):
    vmem = pl.BlockSpec(memory_space=pltpu.VMEM)
    return pl.pallas_call(
        functools.partial(pack, packing),
        name="pack",
        out_shape=tuple(
            pltpu.VMEM((rows, LANES), jnp.bfloat16)
            for rows in (packing.first_rows, packing.second_rows)
        ),
        in_specs=[pl.BlockSpec(memory_space=pl.ANY)] * 3,
        out_specs=(vmem, vmem),
        scratch_shapes=[
            pltpu.VMEM(sources.shape, sources.dtype),
            pltpu.VMEM(project.shape, project.dtype),
            pltpu.SemaphoreType.DMA((4 + packing.blocks,)),
        ],
    )(mixing.reshape(-1, LANES), sources, project)


def first_level(packing, early, coeffs):
    given = [early[box, pl.ds(packing.coeffs, packing.excite)] for box in range(2)]
    for box in range(2):
        pair = jnp.concatenate([given[box], given[1 - box]], axis=1)
        coeffs[box] = jnp.dot(
            pair, early[box, pl.ds(0, packing.level_rows)], preferred_element_type=jnp.float32
        ).astype(coeffs.dtype)


def mixed(packing, level, place, both, blocks):
    axis, apart = place
    upper = lax.axis_index(axis) >> apart & 1
    if level < packing.split:
        blocks = [blocks[0].at[box] for box in range(2)]
    rows = pl.ds(packing.place_of(level), packing.level_rows)
    sums = []
    for box in range(2):
        pair = jnp.concatenate([both[upper, box], both[1 - upper, box]], axis=1)
        sums.append(
            jnp.dot(pair, blocks[box][rows], preferred_element_type=jnp.float32).astype(
                jnp.bfloat16
            )
        )
    return sums


def next_level(packing, level, place, both, *rest):
    *blocks, coeffs = rest
    for box, value in enumerate(mixed(packing, level, place, both, blocks)):
        coeffs[box] = value


def last_level(packing, level, place, both, *rest):
    *blocks, given, final = rest
    given[pl.ds(packing.final, packing.excite)], final[...] = mixed(
        packing, level, place, both, blocks
    )


def in_vmem(kernel, name, out_shape, operands):
    vmem = pl.BlockSpec(memory_space=pltpu.VMEM)
    call = pl.pallas_call(
        kernel,
        name=name,
        out_shape=out_shape,
        in_specs=[vmem] * len(operands),
        out_specs=jax.tree.map(lambda _: vmem, out_shape),
    )
    return call(*(pltpu.with_memory_space_constraint(x, pltpu.VMEM) for x in operands))


def respond(
    packing,
    taken,
    column,
    shared,
    own_final,
    far_expand,
    near_hbm,
    index_hbm,
    response,
    near_blocks,
    around,
    index,
    sems,
):
    excite, rows = packing.excite, packing.box_rows
    targets, positions = index.shape
    block_len = near_blocks.shape[1]
    depth = positions * block_len
    first_of_pair = lax.axis_index("bx") & 1 == 0
    indices = pltpu.make_async_copy(index_hbm, index, sems.at[targets])
    indices.start()
    copies = []
    for target in range(targets):
        part = pl.ds(target * depth, depth)
        copies.append(
            pltpu.make_async_copy(near_hbm.at[part], near_blocks.at[part], sems.at[target])
        )
        copies[-1].start()

    def box_at(x, y):
        if x == 0:
            return column[pl.ds(y * rows, rows)]
        if y == 1 and x < 3:
            return shared[x - 1, pl.ds(packing.sources, rows)]
        return taken[0, pl.ds((3 if y == 1 else x - 1 + 2 * y) * rows, rows)]

    for offset, chosen in enumerate((first_of_pair, jnp.logical_not(first_of_pair))):

        @pl.when(chosen)
        def _():
            for position in range(positions):
                x, y = position // 3, position % 3
                around[pl.ds(position * rows, rows)] = box_at(x + offset, y)

    final = jnp.where(first_of_pair, taken[1, pl.ds(packing.final, excite)], own_final[...])
    indices.wait()
    for target in range(targets):
        picked = []
        for position in range(positions):
            start = position * rows + index[target, position] * excite
            picked.append(around[pl.ds(pl.multiple_of(start, excite), excite)])
        lanes = pl.ds(target * block_len, block_len)
        total = jnp.dot(final, far_expand[:, lanes], preferred_element_type=jnp.float32)
        copies[target].wait()
        blocks = [
            near_blocks[pl.ds(target * depth + position * block_len, block_len)]
            for position in range(positions)
        ]
        total += lax.dot_general(
            jnp.concatenate(picked, axis=1),
            jnp.concatenate(blocks, axis=1),
            (((1,), (1,)), ((), ())),
            preferred_element_type=jnp.float32,
        )
        response[:, 0, 0, lanes] = total


def response_of(packing, taken, column, shared, own_final, far_expand, near_blocks, near_index):
    targets, positions, block_len = near_blocks.shape[:3]
    vmem, hbm = pl.BlockSpec(memory_space=pltpu.VMEM), pl.BlockSpec(memory_space=pl.ANY)
    near_rows = near_blocks.reshape(-1, block_len)
    held = [
        pltpu.with_memory_space_constraint(x, pltpu.VMEM)
        for x in (taken, column, shared, own_final, far_expand)
    ]
    return pl.pallas_call(
        functools.partial(respond, packing),
        name="respond",
        out_shape=jax.ShapeDtypeStruct(
            (packing.excite, 1, 1, far_expand.shape[1]), jnp.float32
        ),
        in_specs=[vmem] * len(held) + [hbm, hbm],
        out_specs=vmem,
        scratch_shapes=[
            pltpu.VMEM(near_rows.shape, near_rows.dtype),
            pltpu.VMEM((positions * packing.box_rows, LANES), column.dtype),
            pltpu.SMEM(near_index.shape, near_index.dtype),
            pltpu.SemaphoreType.DMA((targets + 1,)),
        ],
    )(*held, near_rows, near_index)


def butterfly_levels(packing, levels, blocks, coeffs, first, last):
    rank = LANES
    for level in range(first, last):
        shape = pltpu.VMEM((2, packing.excite, rank), jnp.bfloat16)
        if level == 0:
            coeffs = in_vmem(functools.partial(first_level, packing), "level_0", shape, blocks)
            continue
        place = levels[level]
        both = pair_gather(coeffs, *place)
        kernel = functools.partial(next_level, packing, level, place)
        if level == len(levels) - 1:
            kernel = functools.partial(last_level, packing, level, place)
            shape = (
                pltpu.VMEM((packing.third_rows, LANES), jnp.bfloat16),
                pltpu.VMEM((packing.excite, rank), jnp.bfloat16),
            )
        coeffs = in_vmem(kernel, f"level_{level}", shape, (both, *blocks))
    return coeffs


def per_device(sources, near_blocks, near_index, far_project, far_mixing, far_expand):
    own_sources, own_blocks, own_index = sources[:, 0, 0], near_blocks[0, 0], near_index[0, 0]
    excite, unknowns = own_sources.shape
    rank = far_project.shape[3]
    first_of_pair = lax.axis_index("bx") & 1 == 0
    levels = [("bx", n) for n in range(lax.axis_size("bx").bit_length() - 1)]
    levels += [("by", n) for n in range(lax.axis_size("by").bit_length() - 1)]
    packing = Packing(len(levels), rank, excite, unknowns)
    packed, later = packed_own(packing, far_mixing[0, 0], own_sources, far_project[0, 0])
    shared = pair_gather(packed, "bx", 0)
    later, shared = lax.optimization_barrier((later, shared))
    handed = [(i, i ^ 1) for i in range(0, lax.axis_size("bx"), 2)]
    their_later = lax.ppermute(later, "bx", handed)
    boxes = shared[:, packing.sources :].reshape(2, packing.blocks, excite, LANES)

    def along_first():
        before, after = sent_on(boxes[1], 2, 0), sent_on(boxes[0], -2, 0)
        row = jnp.concatenate([before[None], boxes, after[None]])
        return row, jnp.zeros((2, excite, rank), jnp.bfloat16)

    def levels_early():
        row = jnp.zeros((4, packing.blocks, excite, LANES), jnp.bfloat16)
        return row, butterfly_levels(packing, levels, (shared,), None, 0, packing.split)

    row, coeffs = lax.cond(first_of_pair, along_first, levels_early)
    their_later, coeffs = lax.optimization_barrier((their_later, coeffs))

    def along_second():
        below, above = sent_on(row, 0, 1), sent_on(row, 0, -1)
        given = jnp.concatenate([below[1:], row[3:], above[1:]]).reshape(-1, LANES)
        given = jnp.pad(given, ((0, excite), (0, 0)))
        column = jnp.stack([below[0], row[0], above[0]])
        return column, given, jnp.zeros((excite, rank), jnp.bfloat16)

    def levels_late():
        column = jnp.zeros((3, packing.blocks, excite, LANES), jnp.bfloat16)
        blocks = (their_later, later)
        return column, *butterfly_levels(
            packing, levels, blocks, coeffs, packing.split, len(levels)
        )

    column, given, final = lax.cond(first_of_pair, along_second, levels_late)
    taken = pair_gather(given, "bx", 0)
    return response_of(
        packing,
        taken,
        column.reshape(-1, LANES),
        shared,
        final,
        far_expand[0, 0],
        own_blocks,
        own_index,
    )


def solution(mesh):
    placed = (
        P(None, "bx", "by", None),
        P("bx", "by", None, None, None, None),
        P("bx", "by", None, None),
        P("bx", "by", None, None),
        P("bx", "by", None, None, None, None),
        P("bx", "by", None, None),
    )
    return jax.shard_map(
        per_device, mesh=mesh, in_specs=placed, out_specs=P(None, "bx", "by", None), check_vma=False
    )
```

time: 59.9 us -> 56.6 us (0.945)
  the two profiles are of different devices: /device:TPU:449 before, /device:TPU:1 now
where the time goes in v5:
time: 56.6 us; the launch traced here: 56.3 us
  blocking collectives  48.5 us (86%)
  Pallas kernels  6.35 us (11%)
  starting transfers between devices  1.28 us (2%)
    all_gather x10, blocking collectives, pair_gather(): return lax.all_gather(values, axis, axis_index_groups=pairs)  48.5 us
    pallas_call x1, Pallas kernels, response_of(): pl.pallas_call(functools.partial(respond, packing), name='respond', out_s...  3.87 us
    pallas_call x1, Pallas kernels, packed_own(): pl.pallas_call(functools.partial(pack, packing), name='pack', out_shape=t...  1.29 us
    ppermute x1, starting transfers between devices, per_device(): their_later = lax.ppermute(later, 'bx', handed)  1.28 us
    pallas_call x9, Pallas kernels, in_vmem(): call(*(pltpu.with_memory_space_constraint(x, pltpu.VMEM) for x in operands))  1.19 us
  transfers between devices with their start and end apart: 1, of which 0 were waited for; matrix products, arithmetic and copies ran while one was open for 0% of the time, Pallas kernels for 1%

profile of v5, /device:TPU:1, one launch (start us, length us, event | category | flops | bytes accessed | tf_op | source)
XLA Modules:
  0.0 56.3 jit_solution(1466375339209120877)
XLA Ops:
  0.0 1.3 %pack.1 = (bf16[1312,128]{1,0:T(8,128)(2,1)S(1)}, bf16[1280,128]{1,0:T(8,128)(2,1)S(1)}) custom-call(bf16[2304,128]{1,0:T(8,128)(2,1)} %bitcast.39, bf16[32,1024]{1,0:T(8,128)(2,1)} %bitcast.42, bf16[1024,128]{1,0:T(8,128)(2,1)} %bitcast.41), custom_call_target="tpu_custom_call" | custom-call | tf_op jit(solution)/shard_map/pack/pallas_call | solution.py:87
  1.3 8.8 %all-gather.8 = bf16[2624,128]{1,0:T(8,128)(2,1)S(1)} all-gather(bf16[1312,128]{1,0:T(8,128)(2,1)S(1)} %get-tuple-element.35), channel_id=10, replica_groups={{0,32},{64,96},{128,160},{192,224},{256,288},{320,352},{384,416},{448,4..., dimensions={0}, use_global_device_ids=true | all-gather | bytes 1007616 | tf_op jit(solution)/shard_map/all_gather | solution.py:17
  10.0 1.3 %collective-permute-start.4 = (bf16[1280,128]{1,0:T(8,128)(2,1)S(1)}, bf16[1280,128]{1,0:T(8,128)(2,1)S(1)}, u32[]{:S(2)}, u32[]{:S(2)}) collective-permute-start(bf16[1280,128]{1,0:T(8,128)(2,1)S(1)} %get-tuple-element.36), channel_id=1, source_target_pairs={{0,32},{64,96},{128,160},{192,224},{256,288},{320,352},{384,416},{... | collective-permute-start | bytes 983048 | tf_op jit(solution)/shard_map/ppermute | solution.py:280
  11.3 15.8 %conditional.2 = (bf16[2,32,128]{2,1,0:T(8,128)(2,1)S(1)}, bf16[4,8,32,128]{3,2,1,0:T(8,128)(2,1)S(1)}) conditional(s32[]{:T(128)} %convert_element_type.6, bf16[2,1312,128]{2,1,0:T(8,128)(2,1)S(1)} %bitcast.23, bf16[2,1312,128]{2,1,0:T(8,128)(2,1)S(1)} %bitcast.24), branch_computations={%region_0.0_spmd, %region_1.0_spmd} | conditional | flops 262144 | bytes 1589346 | solution.py:292
  11.4 0.1 level_0.1
  11.5 3.3 %all-gather = bf16[4,32,128]{2,1,0:T(8,128)(2,1)S(1)} all-gather(bf16[2,32,128]{2,1,0:T(8,128)(2,1)S(1)} %level_0.1), channel_id=2, replica_groups={{0,64},{32,96},{128,192},{160,224},{256,320},{288,352},{384,448},{416,4..., dimensions={0}, use_global_device_ids=true | all-gather | bytes 49152 | tf_op jit(solution)/shard_map/cond/branch_0_fun/all_gather | solution.py:17
  14.7 0.1 level_1.1
  14.9 4.8 %all-gather.1 = bf16[4,32,128]{2,1,0:T(8,128)(2,1)S(1)} all-gather(bf16[2,32,128]{2,1,0:T(8,128)(2,1)S(1)} %level_1.1), channel_id=3, replica_groups={{0,128},{32,160},{64,192},{96,224},{256,384},{288,416},{320,448},{352,4..., dimensions={0}, use_global_device_ids=true | all-gather | bytes 49152 | tf_op jit(solution)/shard_map/cond/branch_0_fun/all_gather | solution.py:17
  19.6 0.1 level_2.1
  19.8 7.2 %all-gather.2 = bf16[4,32,128]{2,1,0:T(8,128)(2,1)S(1)} all-gather(bf16[2,32,128]{2,1,0:T(8,128)(2,1)S(1)} %level_2.1), channel_id=4, replica_groups={{0,256},{32,288},{64,320},{96,352},{128,384},{160,416},{192,448},{224,4..., dimensions={0}, use_global_device_ids=true | all-gather | bytes 49152 | tf_op jit(solution)/shard_map/cond/branch_0_fun/all_gather | solution.py:17
  26.9 0.1 level_3.1
  27.1 0.0 collective-permute-done.4
  27.1 0.0 copy-start
  27.1 22.8 %conditional.3 = (bf16[1824,128]{1,0:T(8,128)(2,1)S(1)}, bf16[32,128]{1,0:T(8,128)(2,1)S(1)}, bf16[768,128]{1,0:T(8,128)(2,1)S(1)}) conditional(s32[]{:T(128)} %convert_element_type.6, (bf16[2,32,128]{2,1,0:T(8,128)(2,1)S(1)}, bf16[1280,128]{1,0:T(8,128)(2,1)S(1)}, bf16[1280,128]{1,0:T(8,128)(2,1)S(1)}) %tuple.31, ...), branch_computations={%region_2.0_spmd, %region_3.4_spmd} | conditional | flops 655360 | bytes 5652588 | solution.py:309
  27.1 3.4 %all-gather.3 = bf16[4,32,128]{2,1,0:T(8,128)(2,1)S(1)} all-gather(bf16[2,32,128]{2,1,0:T(8,128)(2,1)S(1)} %get-tuple-element.18), channel_id=5, replica_groups={{0,1},{2,3},{4,5},{6,7},{8,9},{10,11},{12,13},{14,15},{16,17},{18,19},{..., dimensions={0}, use_global_device_ids=true | all-gather | bytes 49152 | tf_op jit(solution)/shard_map/cond/branch_0_fun/all_gather | solution.py:17
  30.5 0.1 level_4.1
  30.7 4.2 %all-gather.4 = bf16[4,32,128]{2,1,0:T(8,128)(2,1)S(1)} all-gather(bf16[2,32,128]{2,1,0:T(8,128)(2,1)S(1)} %level_4.1), channel_id=6, replica_groups={{0,2},{1,3},{4,6},{5,7},{8,10},{9,11},{12,14},{13,15},{16,18},{17,19},{..., dimensions={0}, use_global_device_ids=true | all-gather | bytes 49152 | tf_op jit(solution)/shard_map/cond/branch_0_fun/all_gather | solution.py:17
  34.8 0.1 level_5.1
  34.9 7.2 %all-gather.5 = bf16[4,32,128]{2,1,0:T(8,128)(2,1)S(1)} all-gather(bf16[2,32,128]{2,1,0:T(8,128)(2,1)S(1)} %level_5.1), channel_id=7, replica_groups={{0,4},{1,5},{2,6},{3,7},{8,12},{9,13},{10,14},{11,15},{16,20},{17,21},{..., dimensions={0}, use_global_device_ids=true | all-gather | bytes 49152 | tf_op jit(solution)/shard_map/cond/branch_0_fun/all_gather | solution.py:17
  42.1 0.1 level_6.1
  42.2 3.3 %all-gather.6 = bf16[4,32,128]{2,1,0:T(8,128)(2,1)S(1)} all-gather(bf16[2,32,128]{2,1,0:T(8,128)(2,1)S(1)} %level_6.1), channel_id=8, replica_groups={{0,8},{1,9},{2,10},{3,11},{4,12},{5,13},{6,14},{7,15},{16,24},{17,25},{..., dimensions={0}, use_global_device_ids=true | all-gather | bytes 49152 | tf_op jit(solution)/shard_map/cond/branch_0_fun/all_gather | solution.py:17
  45.5 0.1 level_7.1
  45.6 4.2 %all-gather.7 = bf16[4,32,128]{2,1,0:T(8,128)(2,1)S(1)} all-gather(bf16[2,32,128]{2,1,0:T(8,128)(2,1)S(1)} %level_7.1), channel_id=9, replica_groups={{0,16},{1,17},{2,18},{3,19},{4,20},{5,21},{6,22},{7,23},{8,24},{9,25},{..., dimensions={0}, use_global_device_ids=true | all-gather | bytes 49152 | tf_op jit(solution)/shard_map/cond/branch_0_fun/all_gather | solution.py:17
  49.8 0.1 level_8.1
  50.0 2.5 %all-gather.9 = bf16[3648,128]{1,0:T(8,128)(2,1)S(1)} all-gather(bf16[1824,128]{1,0:T(8,128)(2,1)S(1)} %get-tuple-element.42), channel_id=11, replica_groups={{0,32},{64,96},{128,160},{192,224},{256,288},{320,352},{384,416},{448,4..., dimensions={0}, use_global_device_ids=true | all-gather | bytes 1400832 | tf_op jit(solution)/shard_map/all_gather | solution.py:17
  52.4 0.0 copy-done
  52.4 3.9 %respond.1 = f32[32,1,1,1024]{3,2,1,0:T(1,128)} custom-call(bf16[2,1824,128]{2,1,0:T(8,128)(2,1)S(1)} %bitcast.26, bf16[768,128]{1,0:T(8,128)(2,1)S(1)} %get-tuple-element.43.column, bf16[2,1312,128]{2,1,0:T(8,128)(2,1)S(1)} %bitcast.25, bf16[32,128]{1,0:T(8,128)(2,1)S(1)} %get-tuple-element.44.own_final, bf16[128,1024]{1,0:T(8,128)(2,1)S(1)} %bitcast.28, ...), custom_call_target="tpu_custom_call" | custom-call | tf_op jit(solution)/shard_map/respond/pallas_call | solution.py:231
  (2 shorter events, 0.1 us)
Async XLA Ops:
  10.0 17.1 %collective-permute-start.4 = (bf16[1280,128]{1,0:T(8,128)(2,1)S(1)}, bf16[1280,128]{1,0:T(8,128)(2,1)S(1)}, u32[]{:S(2)}, u32[]{:S(2)}) collective-permute-start(bf16[1280,128]{1,0:T(8,128)(2,1)S(1)} %get-tuple-element.36), channel_id=1, source_target_pairs={{0,32},{64,96},{128,160},{192,224},{256,288},{320,352},{384,416},{... | collective-permute-start | bytes 983048 | tf_op jit(solution)/shard_map/ppermute | solution.py:280
  27.1 25.3 %copy-start = (bf16[1,1,128,1024]{3,2,1,0:T(8,128)(2,1)S(1)}, bf16[1,1,128,1024]{3,2,1,0:T(8,128)(2,1)}, u32[]{:S(2)}) copy-start(bf16[1,1,128,1024]{3,2,1,0:T(8,128)(2,1)} %param.15) | copy-start | bytes 786436

commit v6 on v5

--- a/solution.py
+++ b/solution.py
@@ -31,7 +31,7 @@
 class Packing:
     def __init__(self, levels, rank, excite, unknowns):
         self.excite, self.blocks = excite, unknowns // LANES
-        self.split = levels // 2
+        self.split = 2
         self.level_rows = 2 * rank
         self.box_rows = self.blocks * excite
         self.coeffs = self.split * self.level_rows
@@ -161,6 +161,7 @@
     far_expand,
     near_hbm,
     index_hbm,
+    response_hbm,
     response,
     near_blocks,
     around,
@@ -199,6 +200,7 @@
 
     final = jnp.where(first_of_pair, taken[1, pl.ds(packing.final, excite)], own_final[...])
     indices.wait()
+    written = []
     for target in range(targets):
         picked = []
         for position in range(positions):
@@ -218,11 +220,17 @@
             preferred_element_type=jnp.float32,
         )
         response[:, 0, 0, lanes] = total
+        part = response.at[:, :, :, lanes], response_hbm.at[:, :, :, lanes]
+        written.append(pltpu.make_async_copy(*part, sems.at[targets + 1 + target]))
+        written[-1].start()
+    for copy in written:
+        copy.wait()
 
 
 def response_of(packing, taken, column, shared, own_final, far_expand, near_blocks, near_index):
     targets, positions, block_len = near_blocks.shape[:3]
     vmem, hbm = pl.BlockSpec(memory_space=pltpu.VMEM), pl.BlockSpec(memory_space=pl.ANY)
+    shape = (packing.excite, 1, 1, far_expand.shape[1])
     near_rows = near_blocks.reshape(-1, block_len)
     held = [
         pltpu.with_memory_space_constraint(x, pltpu.VMEM)
@@ -231,16 +239,15 @@
     return pl.pallas_call(
         functools.partial(respond, packing),
         name="respond",
-        out_shape=jax.ShapeDtypeStruct(
-            (packing.excite, 1, 1, far_expand.shape[1]), jnp.float32
-        ),
+        out_shape=jax.ShapeDtypeStruct(shape, jnp.float32),
         in_specs=[vmem] * len(held) + [hbm, hbm],
-        out_specs=vmem,
+        out_specs=hbm,
         scratch_shapes=[
+            pltpu.VMEM(shape, jnp.float32),
             pltpu.VMEM(near_rows.shape, near_rows.dtype),
             pltpu.VMEM((positions * packing.box_rows, LANES), column.dtype),
             pltpu.SMEM(near_index.shape, near_index.dtype),
-            pltpu.SemaphoreType.DMA((targets + 1,)),
+            pltpu.SemaphoreType.DMA((2 * targets + 1,)),
         ],
     )(*held, near_rows, near_index)
 

time: 56.6 us -> 56.5 us (level)
  transfers between devices with their start and end apart: 1 -> 1, of which waited for: 0 -> 0; matrix products, arithmetic and copies ran while one was open for 0% -> 0% of each run, Pallas kernels for 1% -> 0%
where the time goes in v6:
time: 56.5 us; the launch traced here: 56.2 us
  blocking collectives  48.3 us (85%)
  Pallas kernels  6.42 us (11%)
  starting transfers between devices  1.28 us (2%)
    all_gather x10, blocking collectives, pair_gather(): return lax.all_gather(values, axis, axis_index_groups=pairs)  48.3 us
    pallas_call x1, Pallas kernels, response_of(): pl.pallas_call(functools.partial(respond, packing), name='respond', out_s...  3.91 us
    pallas_call x1, Pallas kernels, packed_own(): pl.pallas_call(functools.partial(pack, packing), name='pack', out_shape=t...  1.32 us
    ppermute x1, starting transfers between devices, per_device(): their_later = lax.ppermute(later, 'bx', handed)  1.28 us
    pallas_call x9, Pallas kernels, in_vmem(): call(*(pltpu.with_memory_space_constraint(x, pltpu.VMEM) for x in operands))  1.2 us
  transfers between devices with their start and end apart: 1, of which 0 were waited for; matrix products, arithmetic and copies ran while one was open for 0% of the time, Pallas kernels for 0%

profile of v6, /device:TPU:1, one launch (start us, length us, event | category | flops | bytes accessed | tf_op | source)
XLA Modules:
  0.0 56.2 jit_solution(8384560105449704275)
XLA Ops:
  0.0 1.3 %pack.1 = (bf16[800,128]{1,0:T(8,128)(2,1)S(1)}, bf16[1792,128]{1,0:T(8,128)(2,1)S(1)}) custom-call(bf16[2304,128]{1,0:T(8,128)(2,1)} %bitcast.39, bf16[32,1024]{1,0:T(8,128)(2,1)} %bitcast.42, bf16[1024,128]{1,0:T(8,128)(2,1)} %bitcast.41), custom_call_target="tpu_custom_call" | custom-call | tf_op jit(solution)/shard_map/pack/pallas_call | solution.py:87
  1.3 8.6 %all-gather.8 = bf16[1600,128]{1,0:T(8,128)(2,1)S(1)} all-gather(bf16[800,128]{1,0:T(8,128)(2,1)S(1)} %get-tuple-element.35), channel_id=10, replica_groups={{0,32},{64,96},{128,160},{192,224},{256,288},{320,352},{384,416},{448,4..., dimensions={0}, use_global_device_ids=true | all-gather | bytes 614400 | tf_op jit(solution)/shard_map/all_gather | solution.py:17
  9.9 1.3 %collective-permute-start.4 = (bf16[1792,128]{1,0:T(8,128)(2,1)S(1)}, bf16[1792,128]{1,0:T(8,128)(2,1)S(1)}, u32[]{:S(2)}, u32[]{:S(2)}) collective-permute-start(bf16[1792,128]{1,0:T(8,128)(2,1)S(1)} %get-tuple-element.36), channel_id=1, source_target_pairs={{0,32},{64,96},{128,160},{192,224},{256,288},{320,352},{384,416},{... | collective-permute-start | bytes 1376264 | tf_op jit(solution)/shard_map/ppermute | solution.py:287
  11.2 3.6 %conditional.2 = (bf16[2,32,128]{2,1,0:T(8,128)(2,1)S(1)}, bf16[4,8,32,128]{3,2,1,0:T(8,128)(2,1)S(1)}) conditional(s32[]{:T(128)} %convert_element_type.6, bf16[2,800,128]{2,1,0:T(8,128)(2,1)S(1)} %bitcast.23, bf16[2,800,128]{2,1,0:T(8,128)(2,1)S(1)} %bitcast.24), branch_computations={%region_0.0_spmd, %region_1.0_spmd} | conditional | flops 262144 | bytes 1589346 | solution.py:299
  11.2 0.1 level_0.1
  11.3 3.3 %all-gather = bf16[4,32,128]{2,1,0:T(8,128)(2,1)S(1)} all-gather(bf16[2,32,128]{2,1,0:T(8,128)(2,1)S(1)} %level_0.1), channel_id=2, replica_groups={{0,64},{32,96},{128,192},{160,224},{256,320},{288,352},{384,448},{416,4..., dimensions={0}, use_global_device_ids=true | all-gather | bytes 49152 | tf_op jit(solution)/shard_map/cond/branch_0_fun/all_gather | solution.py:17
  14.6 0.1 level_1.1
  14.8 0.0 collective-permute-done.4
  14.8 0.0 copy-start
  14.8 35.0 %conditional.3 = (bf16[1824,128]{1,0:T(8,128)(2,1)S(1)}, bf16[32,128]{1,0:T(8,128)(2,1)S(1)}, bf16[768,128]{1,0:T(8,128)(2,1)S(1)}) conditional(s32[]{:T(128)} %convert_element_type.6, (bf16[2,32,128]{2,1,0:T(8,128)(2,1)S(1)}, bf16[1792,128]{1,0:T(8,128)(2,1)S(1)}, bf16[1792,128]{1,0:T(8,128)(2,1)S(1)}) %tuple.31, ...), branch_computations={%region_2.0_spmd, %region_3.4_spmd} | conditional | flops 655360 | bytes 5652588 | solution.py:316
  14.8 4.9 %all-gather.1 = bf16[4,32,128]{2,1,0:T(8,128)(2,1)S(1)} all-gather(bf16[2,32,128]{2,1,0:T(8,128)(2,1)S(1)} %get-tuple-element.18), channel_id=3, replica_groups={{0,128},{32,160},{64,192},{96,224},{256,384},{288,416},{320,448},{352,4..., dimensions={0}, use_global_device_ids=true | all-gather | bytes 49152 | tf_op jit(solution)/shard_map/cond/branch_0_fun/all_gather | solution.py:17
  19.7 0.1 level_2.1
  19.8 7.2 %all-gather.2 = bf16[4,32,128]{2,1,0:T(8,128)(2,1)S(1)} all-gather(bf16[2,32,128]{2,1,0:T(8,128)(2,1)S(1)} %level_2.1), channel_id=4, replica_groups={{0,256},{32,288},{64,320},{96,352},{128,384},{160,416},{192,448},{224,4..., dimensions={0}, use_global_device_ids=true | all-gather | bytes 49152 | tf_op jit(solution)/shard_map/cond/branch_0_fun/all_gather | solution.py:17
  27.0 0.1 level_3.1
  27.1 3.3 %all-gather.3 = bf16[4,32,128]{2,1,0:T(8,128)(2,1)S(1)} all-gather(bf16[2,32,128]{2,1,0:T(8,128)(2,1)S(1)} %level_3.1), channel_id=5, replica_groups={{0,1},{2,3},{4,5},{6,7},{8,9},{10,11},{12,13},{14,15},{16,17},{18,19},{..., dimensions={0}, use_global_device_ids=true | all-gather | bytes 49152 | tf_op jit(solution)/shard_map/cond/branch_0_fun/all_gather | solution.py:17
  30.4 0.1 level_4.1
  30.5 4.2 %all-gather.4 = bf16[4,32,128]{2,1,0:T(8,128)(2,1)S(1)} all-gather(bf16[2,32,128]{2,1,0:T(8,128)(2,1)S(1)} %level_4.1), channel_id=6, replica_groups={{0,2},{1,3},{4,6},{5,7},{8,10},{9,11},{12,14},{13,15},{16,18},{17,19},{..., dimensions={0}, use_global_device_ids=true | all-gather | bytes 49152 | tf_op jit(solution)/shard_map/cond/branch_0_fun/all_gather | solution.py:17
  34.7 0.1 level_5.1
  34.8 7.2 %all-gather.5 = bf16[4,32,128]{2,1,0:T(8,128)(2,1)S(1)} all-gather(bf16[2,32,128]{2,1,0:T(8,128)(2,1)S(1)} %level_5.1), channel_id=7, replica_groups={{0,4},{1,5},{2,6},{3,7},{8,12},{9,13},{10,14},{11,15},{16,20},{17,21},{..., dimensions={0}, use_global_device_ids=true | all-gather | bytes 49152 | tf_op jit(solution)/shard_map/cond/branch_0_fun/all_gather | solution.py:17
  42.0 0.1 level_6.1
  42.1 3.3 %all-gather.6 = bf16[4,32,128]{2,1,0:T(8,128)(2,1)S(1)} all-gather(bf16[2,32,128]{2,1,0:T(8,128)(2,1)S(1)} %level_6.1), channel_id=8, replica_groups={{0,8},{1,9},{2,10},{3,11},{4,12},{5,13},{6,14},{7,15},{16,24},{17,25},{..., dimensions={0}, use_global_device_ids=true | all-gather | bytes 49152 | tf_op jit(solution)/shard_map/cond/branch_0_fun/all_gather | solution.py:17
  45.4 0.1 level_7.1
  45.5 4.2 %all-gather.7 = bf16[4,32,128]{2,1,0:T(8,128)(2,1)S(1)} all-gather(bf16[2,32,128]{2,1,0:T(8,128)(2,1)S(1)} %level_7.1), channel_id=9, replica_groups={{0,16},{1,17},{2,18},{3,19},{4,20},{5,21},{6,22},{7,23},{8,24},{9,25},{..., dimensions={0}, use_global_device_ids=true | all-gather | bytes 49152 | tf_op jit(solution)/shard_map/cond/branch_0_fun/all_gather | solution.py:17
  49.6 0.1 level_8.1
  49.8 2.5 %all-gather.9 = bf16[3648,128]{1,0:T(8,128)(2,1)S(1)} all-gather(bf16[1824,128]{1,0:T(8,128)(2,1)S(1)} %get-tuple-element.42), channel_id=11, replica_groups={{0,32},{64,96},{128,160},{192,224},{256,288},{320,352},{384,416},{448,4..., dimensions={0}, use_global_device_ids=true | all-gather | bytes 1400832 | tf_op jit(solution)/shard_map/all_gather | solution.py:17
  52.3 0.0 copy-done
  52.3 3.9 %respond.1 = f32[32,1,1,1024]{3,2,1,0:T(1,128)} custom-call(bf16[2,1824,128]{2,1,0:T(8,128)(2,1)S(1)} %bitcast.26, bf16[768,128]{1,0:T(8,128)(2,1)S(1)} %get-tuple-element.43.column, bf16[2,800,128]{2,1,0:T(8,128)(2,1)S(1)} %bitcast.25, bf16[32,128]{1,0:T(8,128)(2,1)S(1)} %get-tuple-element.44.own_final, bf16[128,1024]{1,0:T(8,128)(2,1)S(1)} %bitcast.28, ...), custom_call_target="tpu_custom_call" | custom-call | tf_op jit(solution)/shard_map/respond/pallas_call | solution.py:239
  (2 shorter events, 0.1 us)
Async XLA Ops:
  9.9 4.9 %collective-permute-start.4 = (bf16[1792,128]{1,0:T(8,128)(2,1)S(1)}, bf16[1792,128]{1,0:T(8,128)(2,1)S(1)}, u32[]{:S(2)}, u32[]{:S(2)}) collective-permute-start(bf16[1792,128]{1,0:T(8,128)(2,1)S(1)} %get-tuple-element.36), channel_id=1, source_target_pairs={{0,32},{64,96},{128,160},{192,224},{256,288},{320,352},{384,416},{... | collective-permute-start | bytes 1376264 | tf_op jit(solution)/shard_map/ppermute | solution.py:287
  14.8 37.5 %copy-start = (bf16[1,1,128,1024]{3,2,1,0:T(8,128)(2,1)S(1)}, bf16[1,1,128,1024]{3,2,1,0:T(8,128)(2,1)}, u32[]{:S(2)}) copy-start(bf16[1,1,128,1024]{3,2,1,0:T(8,128)(2,1)} %param.15) | copy-start | bytes 786436

commit v7 on v4

v7 whole, which is shorter than its diff:
```python
import functools

import jax
import jax.numpy as jnp
from jax import lax
from jax.experimental import pallas as pl
from jax.experimental.pallas import tpu as pltpu
from jax.sharding import PartitionSpec as P

BOTH = ("bx", "by")
LANES = 128
GRANT = pltpu.CompilerParams(vmem_limit_bytes=8 << 20)


def pair_gather(values, axis, apart):
    count = lax.axis_size(axis)
    pairs = [[i, i ^ 1 << apart] for i in range(count) if not i >> apart & 1]
    return lax.all_gather(values, axis, axis_index_groups=pairs)


def sent_on(values, step_x, step_y):
    count_x, count_y = lax.axis_size("bx"), lax.axis_size("by")
    moves = []
    for x in range(0, count_x, 2):
        for y in range(count_y):
            to_x, to_y = x + step_x, y + step_y
            if 0 <= to_x < count_x and 0 <= to_y < count_y:
                moves.append((x * count_y + y, to_x * count_y + to_y))
    return lax.ppermute(values, BOTH, moves)


class Packing:
    def __init__(self, levels, rank, excite, unknowns):
        self.excite, self.blocks = excite, unknowns // LANES
        self.split = levels - 3
        self.level_rows = 2 * rank
        self.box_rows = self.blocks * excite
        self.coeffs = self.split * self.level_rows
        self.sources = self.coeffs + excite
        self.first_rows = self.sources + self.box_rows
        self.late_rows = (levels - self.split) * self.level_rows
        self.late = 7 * self.box_rows
        self.second_rows = self.late + self.late_rows

    def place_of(self, level):
        return (level if level < self.split else level - self.split) * self.level_rows


def pack(packing, mixing_hbm, sources_hbm, project_hbm, packed, later, sources, project, sems):
    excite = packing.excite
    wide = [
        pltpu.make_async_copy(sources_hbm, sources, sems.at[0]),
        pltpu.make_async_copy(project_hbm, project, sems.at[1]),
    ]
    for copy in wide:
        copy.start()
    rest = [
        pltpu.make_async_copy(
            mixing_hbm.at[pl.ds(0, packing.coeffs)],
            packed.at[pl.ds(0, packing.coeffs)],
            sems.at[2],
        ),
        pltpu.make_async_copy(
            mixing_hbm.at[pl.ds(packing.coeffs, packing.late_rows)], later, sems.at[3]
        ),
    ]
    for block in range(packing.blocks):
        rest.append(
            pltpu.make_async_copy(
                sources_hbm.at[:, pl.ds(block * LANES, LANES)],
                packed.at[pl.ds(packing.sources + block * excite, excite)],
                sems.at[4 + block],
            )
        )
    for copy in rest:
        copy.start()
    for copy in wide:
        copy.wait()
    packed[pl.ds(packing.coeffs, excite)] = jnp.dot(
        sources[...], project[...], preferred_element_type=jnp.float32
    ).astype(jnp.bfloat16)
    for copy in rest:
        copy.wait()


def packed_own(packing, mixing, sources, project):
    vmem = pl.BlockSpec(memory_space=pltpu.VMEM)
    operands = (mixing.reshape(-1, LANES), sources, project)
    return pl.pallas_call(
        functools.partial(pack, packing),
        name="pack",
        compiler_params=GRANT,
        out_shape=tuple(
            pltpu.VMEM((rows, LANES), jnp.bfloat16)
            for rows in (packing.first_rows, packing.late_rows)
        ),
        in_specs=[pl.BlockSpec(memory_space=pl.ANY)] * 3,
        out_specs=(vmem, vmem),
        scratch_shapes=[
            pltpu.VMEM(sources.shape, sources.dtype),
            pltpu.VMEM(project.shape, project.dtype),
            pltpu.SemaphoreType.DMA((4 + packing.blocks,)),
        ],
    )(*(pltpu.with_memory_space_constraint(x, pltpu.HBM) for x in operands))


def first_level(packing, early, coeffs):
    given = [early[box, pl.ds(packing.coeffs, packing.excite)] for box in range(2)]
    for box in range(2):
        pair = jnp.concatenate([given[box], given[1 - box]], axis=1)
        coeffs[box] = jnp.dot(
            pair, early[box, pl.ds(0, packing.level_rows)], preferred_element_type=jnp.float32
        ).astype(coeffs.dtype)


def mixed(packing, level, place, both, blocks):
    axis, apart = place
    upper = lax.axis_index(axis) >> apart & 1
    if level < packing.split:
        blocks = [blocks[0].at[box] for box in range(2)]
        starts = [packing.place_of(level)] * 2
    else:
        starts = [packing.late + packing.place_of(level), packing.place_of(level)]
    sums = []
    for box in range(2):
        pair = jnp.concatenate([both[upper, box], both[1 - upper, box]], axis=1)
        weights = blocks[box][pl.ds(starts[box], packing.level_rows)]
        sums.append(
            jnp.dot(pair, weights, preferred_element_type=jnp.float32).astype(jnp.bfloat16)
        )
    return sums


def next_level(packing, level, place, both, *rest):
    blocks = rest[: 1 if level < packing.split else 2]
    coeffs = rest[len(blocks)]
    for box, value in enumerate(mixed(packing, level, place, both, blocks)):
        coeffs[box] = value


def last_level(packing, level, place, both, theirs, own, given, final):
    given[...], final[...] = mixed(packing, level, place, both, (theirs, own))


def in_vmem(kernel, name, out_shape, operands):
    vmem = pl.BlockSpec(memory_space=pltpu.VMEM)
    call = pl.pallas_call(
        kernel,
        name=name,
        compiler_params=GRANT,
        out_shape=out_shape,
        in_specs=[vmem] * len(operands),
        out_specs=jax.tree.map(lambda _: vmem, out_shape),
    )
    return call(*(pltpu.with_memory_space_constraint(x, pltpu.VMEM) for x in operands))


def near_field(
    packing, offset, beside, shared, *rest
):
    column, (near_blocks, index_ref, near, index, sem) = rest[:-5], rest[-5:]
    excite, rows = packing.excite, packing.box_rows
    targets, positions = index.shape
    block_len = near_blocks.shape[1]
    indices = pltpu.make_async_copy(index_ref, index, sem)
    indices.start()
    indices.wait()

    def block_at(x, y, block):
        at = pl.multiple_of(block * excite, excite)
        if x == 0:
            return column[0][pl.ds(y * rows + at, excite)]
        if y == 1 and x < 3:
            return shared[x - 1, pl.ds(packing.sources + at, excite)]
        return beside[pl.ds((3 if y == 1 else x - 1 + 2 * y) * rows + at, excite)]

    for target in range(targets):
        picked, blocks = [], []
        for position in range(positions):
            x, y = position // 3 + offset, position % 3
            picked.append(block_at(x, y, index[target, position]))
            start = (target * positions + position) * block_len
            blocks.append(near_blocks[pl.ds(start, block_len)])
        near[:, pl.ds(target * block_len, block_len)] = lax.dot_general(
            jnp.concatenate(picked, axis=1),
            jnp.concatenate(blocks, axis=1),
            (((1,), (1,)), ((), ())),
            preferred_element_type=jnp.float32,
        )


def near_of(packing, offset, beside, shared, column, near_blocks, near_index):
    vmem = pl.BlockSpec(memory_space=pltpu.VMEM)
    around = (beside, shared, *column)
    operands = [pltpu.with_memory_space_constraint(x, pltpu.VMEM) for x in around]
    operands += [near_blocks.reshape(-1, near_blocks.shape[3]), near_index]
    return pl.pallas_call(
        functools.partial(near_field, packing, offset),
        name=f"near_{offset}",
        compiler_params=GRANT,
        out_shape=pltpu.VMEM((packing.excite, packing.blocks * LANES), jnp.float32),
        in_specs=[vmem] * len(operands),
        out_specs=vmem,
        scratch_shapes=[
            pltpu.SMEM(near_index.shape, near_index.dtype),
            pltpu.SemaphoreType.DMA,
        ],
    )(*operands)


def respond(taken, own_final, near, far_expand, response_hbm, response, sems):
    first_of_pair = lax.axis_index("bx") & 1 == 0
    final = jnp.where(first_of_pair, taken[1], own_final[...])
    width = response.shape[3] // sems.shape[0]
    copies = []
    for part in range(sems.shape[0]):
        lanes = pl.ds(part * width, width)
        response[:, 0, 0, lanes] = near[:, lanes] + jnp.dot(
            final, far_expand[:, lanes], preferred_element_type=jnp.float32
        )
        ends = response.at[:, :, :, lanes], response_hbm.at[:, :, :, lanes]
        copies.append(pltpu.make_async_copy(*ends, sems.at[part]))
        copies[-1].start()
    for copy in copies:
        copy.wait()


def response_of(taken, final, near, far_expand):
    vmem = pl.BlockSpec(memory_space=pltpu.VMEM)
    shape = (near.shape[0], 1, 1, near.shape[1])
    held = [pltpu.with_memory_space_constraint(x, pltpu.VMEM) for x in (taken, final, near)]
    return pl.pallas_call(
        respond,
        name="respond",
        compiler_params=GRANT,
        out_shape=jax.ShapeDtypeStruct(shape, jnp.float32),
        in_specs=[vmem] * 4,
        out_specs=pl.BlockSpec(memory_space=pl.ANY),
        scratch_shapes=[pltpu.VMEM(shape, jnp.float32), pltpu.SemaphoreType.DMA((4,))],
    )(*held, far_expand)


def per_device(sources, near_blocks, near_index, far_project, far_mixing, far_expand):
    own_sources, own_blocks, own_index = sources[:, 0, 0], near_blocks[0, 0], near_index[0, 0]
    excite, unknowns = own_sources.shape
    rank = far_project.shape[3]
    first_of_pair = lax.axis_index("bx") & 1 == 0
    levels = [("bx", n) for n in range(lax.axis_size("bx").bit_length() - 1)]
    levels += [("by", n) for n in range(lax.axis_size("by").bit_length() - 1)]
    packing = Packing(len(levels), rank, excite, unknowns)
    packed, later = packed_own(packing, far_mixing[0, 0], own_sources, far_project[0, 0])
    shared = pair_gather(packed, "bx", 0)
    coeffs_shape = pltpu.VMEM((2, excite, rank), jnp.bfloat16)
    column_shape = pltpu.VMEM((3 * packing.box_rows, LANES), jnp.bfloat16)
    given_shape = pltpu.VMEM((packing.second_rows, LANES), jnp.bfloat16)

    def gathering():
        boxes = shared[:, packing.sources :].reshape(2, packing.blocks, excite, LANES)
        before, after = sent_on(boxes[1], 2, 0), sent_on(boxes[0], -2, 0)
        row = jnp.concatenate([before[None], boxes, after[None]])
        below, above = sent_on(row, 0, 1), sent_on(row, 0, -1)
        given = jnp.concatenate([below[1:], row[3:], above[1:]]).reshape(-1, LANES)
        column = jnp.stack([below[0], row[0], above[0]]).reshape(-1, LANES)
        return jnp.zeros((2, excite, rank), jnp.bfloat16), jnp.concatenate([given, later]), column

    def levels_early():
        coeffs = in_vmem(functools.partial(first_level, packing), "level_0", coeffs_shape, (shared,))
        for level in range(1, packing.split):
            shape = coeffs_shape
            if level == packing.split - 1:
                shape = (coeffs_shape, given_shape, column_shape)
            both = pair_gather(coeffs, *levels[level])
            kernel = functools.partial(next_level, packing, level, levels[level])
            coeffs = in_vmem(kernel, f"level_{level}", shape, (both, shared))
        return tuple(coeffs)

    coeffs, given, column = lax.cond(first_of_pair, gathering, levels_early)
    handed = lax.ppermute(given, "bx", [(i, i ^ 1) for i in range(0, lax.axis_size("bx"), 2)])
    both = lax.cond(
        first_of_pair,
        lambda: jnp.stack([coeffs, coeffs]),
        lambda: pair_gather(coeffs, *levels[packing.split]),
    )

    def near_only():
        near = near_of(packing, 0, given, shared, (column,), own_blocks, own_index)
        return near, coeffs[0], coeffs[1]

    def levels_late():
        gathered = both
        for level in range(packing.split, len(levels)):
            kernel = functools.partial(next_level, packing, level, levels[level])
            shape = coeffs_shape
            if level == len(levels) - 1:
                kernel = functools.partial(last_level, packing, level, levels[level])
                shape = (pltpu.VMEM((excite, rank), jnp.bfloat16),) * 2
            result = in_vmem(kernel, f"level_{level}", shape, (gathered, handed, later))
            if level < len(levels) - 1:
                gathered = pair_gather(result, *levels[level + 1])
        beside, result = lax.optimization_barrier((handed, tuple(result)))
        near = near_of(packing, 1, beside, shared, (), own_blocks, own_index)
        return near, *result

    near, final_given, final = lax.cond(first_of_pair, near_only, levels_late)
    taken = pair_gather(final_given, "bx", 0)
    return response_of(taken, final, near, far_expand[0, 0])


def solution(mesh):
    placed = (
        P(None, "bx", "by", None),
        P("bx", "by", None, None, None, None),
        P("bx", "by", None, None),
        P("bx", "by", None, None),
        P("bx", "by", None, None, None, None),
        P("bx", "by", None, None),
    )
    return jax.shard_map(
        per_device, mesh=mesh, in_specs=placed, out_specs=P(None, "bx", "by", None), check_vma=False
    )
```

time: 59.9 us -> 54.6 us (0.912)
  the two profiles are of different devices: /device:TPU:449 before, /device:TPU:1 now
where the time goes in v7:
time: 54.6 us; the launch traced here: 54.3 us
  blocking collectives  48 us (88%)
  Pallas kernels  4.84 us (9%)
  starting transfers between devices  1.29 us (2%)
    all_gather x10, blocking collectives, pair_gather(): return lax.all_gather(values, axis, axis_index_groups=pairs)  48 us
    pallas_call x1, Pallas kernels, near_of(): pl.pallas_call(functools.partial(near_field, packing, offset), name=f'nea...  1.54 us
    ppermute x1, starting transfers between devices, per_device(): lax.ppermute(given, 'bx', [(i, i ^ 1) for i in range(0, lax.axis_size('bx...  1.29 us
    pallas_call x1, Pallas kernels, packed_own(): pl.pallas_call(functools.partial(pack, packing), name='pack', compiler_pa...  1.28 us
    pallas_call x9, Pallas kernels, in_vmem(): call(*(pltpu.with_memory_space_constraint(x, pltpu.VMEM) for x in operands))  1.18 us
  transfers between devices with their start and end apart: 1, of which 0 were waited for; matrix products, arithmetic and copies ran while one was open for 0% of the time, Pallas kernels for 0%

profile of v7, /device:TPU:1, one launch (start us, length us, event | category | flops | bytes accessed | tf_op | source)
XLA Modules:
  0.0 54.3 jit_solution(16352861470816073034)
XLA Ops:
  0.0 1.3 %pack.1 = (bf16[1824,128]{1,0:T(8,128)(2,1)S(1)}, bf16[768,128]{1,0:T(8,128)(2,1)S(1)}) custom-call(bf16[2304,128]{1,0:T(8,128)(2,1)} %bitcast.47, bf16[32,1024]{1,0:T(8,128)(2,1)} %bitcast.55, bf16[1024,128]{1,0:T(8,128)(2,1)} %bitcast.49), custom_call_target="tpu_custom_call" | custom-call | tf_op jit(solution)/shard_map/pack/pallas_call | solution.py:89
  1.3 8.9 %all-gather.8 = bf16[3648,128]{1,0:T(8,128)(2,1)S(1)} all-gather(bf16[1824,128]{1,0:T(8,128)(2,1)S(1)} %get-tuple-element.74), channel_id=10, replica_groups={{0,32},{64,96},{128,160},{192,224},{256,288},{320,352},{384,416},{448,4..., dimensions={0}, use_global_device_ids=true | all-gather | bytes 1400832 | tf_op jit(solution)/shard_map/all_gather | solution.py:18
  10.2 0.0 copy-start.2
  10.2 23.4 %conditional.3 = (bf16[2,32,128]{2,1,0:T(8,128)(2,1)S(1)}, bf16[2560,128]{1,0:T(8,128)(2,1)S(1)}, bf16[768,128]{1,0:T(8,128)(2,1)S(1)}, bf16[2,32,128]{2,1,0:T(8,128)(2,1)S(1)}) conditional(s32[]{:T(128)} %convert_element_type.2, bf16[2,1824,128]{2,1,0:T(8,128)(2,1)S(1)} %bitcast.29, (bf16[2,1824,128]{2,1,0:T(8,128)(2,1)S(1)}, ...), branch_computations={%region_0.0_spmd, %region_1.0_spmd} | conditional | flops 2228224 | bytes 7372996 | solution.py:277
  10.2 0.1 level_0.1
  10.4 3.3 %all-gather = bf16[4,32,128]{2,1,0:T(8,128)(2,1)S(1)} all-gather(bf16[2,32,128]{2,1,0:T(8,128)(2,1)S(1)} %level_0.1), channel_id=2, replica_groups={{0,64},{32,96},{128,192},{160,224},{256,320},{288,352},{384,448},{416,4..., dimensions={0}, use_global_device_ids=true | all-gather | bytes 49152 | tf_op jit(solution)/shard_map/cond/branch_0_fun/all_gather | solution.py:18
  13.6 0.1 level_1.1
  13.7 4.8 %all-gather.1 = bf16[4,32,128]{2,1,0:T(8,128)(2,1)S(1)} all-gather(bf16[2,32,128]{2,1,0:T(8,128)(2,1)S(1)} %level_1.1), channel_id=3, replica_groups={{0,128},{32,160},{64,192},{96,224},{256,384},{288,416},{320,448},{352,4..., dimensions={0}, use_global_device_ids=true | all-gather | bytes 49152 | tf_op jit(solution)/shard_map/cond/branch_0_fun/all_gather | solution.py:18
  18.5 0.1 level_2.1
  18.6 7.2 %all-gather.2 = bf16[4,32,128]{2,1,0:T(8,128)(2,1)S(1)} all-gather(bf16[2,32,128]{2,1,0:T(8,128)(2,1)S(1)} %level_2.1), channel_id=4, replica_groups={{0,256},{32,288},{64,320},{96,352},{128,384},{160,416},{192,448},{224,4..., dimensions={0}, use_global_device_ids=true | all-gather | bytes 49152 | tf_op jit(solution)/shard_map/cond/branch_0_fun/all_gather | solution.py:18
  25.8 0.1 level_3.1
  25.9 3.3 %all-gather.3 = bf16[4,32,128]{2,1,0:T(8,128)(2,1)S(1)} all-gather(bf16[2,32,128]{2,1,0:T(8,128)(2,1)S(1)} %level_3.1), channel_id=5, replica_groups={{0,1},{2,3},{4,5},{6,7},{8,9},{10,11},{12,13},{14,15},{16,17},{18,19},{..., dimensions={0}, use_global_device_ids=true | all-gather | bytes 49152 | tf_op jit(solution)/shard_map/cond/branch_0_fun/all_gather | solution.py:18
  29.2 0.1 level_4.1
  29.3 4.2 %all-gather.4 = bf16[4,32,128]{2,1,0:T(8,128)(2,1)S(1)} all-gather(bf16[2,32,128]{2,1,0:T(8,128)(2,1)S(1)} %level_4.1), channel_id=6, replica_groups={{0,2},{1,3},{4,6},{5,7},{8,10},{9,11},{12,14},{13,15},{16,18},{17,19},{..., dimensions={0}, use_global_device_ids=true | all-gather | bytes 49152 | tf_op jit(solution)/shard_map/cond/branch_0_fun/all_gather | solution.py:18
  33.4 0.1 level_5.1
  33.6 1.3 %collective-permute-start.4 = (bf16[2560,128]{1,0:T(8,128)(2,1)S(1)}, bf16[2560,128]{1,0:T(8,128)(2,1)S(1)}, u32[]{:S(2)}, u32[]{:S(2)}) collective-permute-start(bf16[2560,128]{1,0:T(8,128)(2,1)S(1)} %get-tuple-element.77), channel_id=1, source_target_pairs={{0,32},{64,96},{128,160},{192,224},{256,288},{320,352},{384,416},{... | collective-permute-start | bytes 1966088 | tf_op jit(solution)/shard_map/ppermute | solution.py:278
  34.9 7.2 %conditional.4 = (bf16[2,2,32,128]{3,2,1,0:T(8,128)(2,1)S(1)}) conditional(s32[]{:T(128)} %convert_element_type.2, bf16[2,32,128]{2,1,0:T(8,128)(2,1)S(1)} %get-tuple-element.76, bf16[2,32,128]{2,1,0:T(8,128)(2,1)S(1)} %get-tuple-element.76), branch_computations={%region_2.0_spmd, %region_3.0_spmd} | conditional | flops 16384 | bytes 49160 | solution.py:279
  34.9 7.2 %all-gather.5 = bf16[4,32,128]{2,1,0:T(8,128)(2,1)S(1)} all-gather(bf16[2,32,128]{2,1,0:T(8,128)(2,1)S(1)} %param.2), channel_id=7, replica_groups={{0,4},{1,5},{2,6},{3,7},{8,12},{9,13},{10,14},{11,15},{16,20},{17,21},{..., dimensions={0}, use_global_device_ids=true | all-gather | bytes 49152 | tf_op jit(solution)/shard_map/cond/branch_0_fun/all_gather | solution.py:18
  42.1 0.0 collective-permute-done.4
  42.1 0.0 copy-done.2
  42.1 0.0 copy-start
  42.1 9.5 %conditional.5 = (f32[32,1024]{1,0:T(8,128)S(1)}, bf16[32,128]{1,0:T(8,128)(2,1)S(1)}, bf16[32,128]{1,0:T(8,128)(2,1)S(1)}) conditional(s32[]{:T(128)} %convert_element_type.2, (bf16[2,2,32,128]{3,2,1,0:T(8,128)(2,1)S(1)}, bf16[2560,128]{1,0:T(8,128)(2,1)S(1)}, bf16[768,128]{1,0:T(8,128)(2,1)S(1)}, bf16[1,1,8,9,128,128]{5,4,3,2,1,0:T(8,128)(2,1)}, ...), branch_computations={%region_4.0_spmd, %region_5.0_spmd} | conditional | bytes 9535540 | solution.py:304
  42.1 0.0 copy-start.1
  42.1 0.1 level_6.1
  42.2 3.4 %all-gather.6 = bf16[4,32,128]{2,1,0:T(8,128)(2,1)S(1)} all-gather(bf16[2,32,128]{2,1,0:T(8,128)(2,1)S(1)} %level_6.1), channel_id=8, replica_groups={{0,8},{1,9},{2,10},{3,11},{4,12},{5,13},{6,14},{7,15},{16,24},{17,25},{..., dimensions={0}, use_global_device_ids=true | all-gather | bytes 49152 | tf_op jit(solution)/shard_map/cond/branch_0_fun/all_gather | solution.py:18
  45.6 0.1 level_7.1
  45.8 4.2 %all-gather.7 = bf16[4,32,128]{2,1,0:T(8,128)(2,1)S(1)} all-gather(bf16[2,32,128]{2,1,0:T(8,128)(2,1)S(1)} %level_7.1), channel_id=9, replica_groups={{0,16},{1,17},{2,18},{3,19},{4,20},{5,21},{6,22},{7,23},{8,24},{9,25},{..., dimensions={0}, use_global_device_ids=true | all-gather | bytes 49152 | tf_op jit(solution)/shard_map/cond/branch_0_fun/all_gather | solution.py:18
  49.9 0.1 level_8.1
  50.0 0.0 copy-done.1
  50.1 1.5 %near_1.1 = f32[32,1024]{1,0:T(8,128)S(1)} custom-call(bf16[2560,128]{1,0:T(8,128)(2,1)S(1)} %get-tuple-element.53.rest_0_.theirs.beside, bf16[2,1824,128]{2,1,0:T(8,128)(2,1)S(1)} %get-tuple-element.54.shared, bf16[9216,128]{1,0:T(8,128)(2,1)S(1)} %bitcast.44, s32[8,9]{1,0:T(8,128)S(1)} %get-tuple-element.56.rest_1_), custom_call_target="tpu_custom_call" | custom-call | tf_op jit(solution)/shard_map/cond/branch_0_fun/near_1/pallas_call | solution.py:197
  51.6 1.8 %all-gather.9 = bf16[64,128]{1,0:T(8,128)(2,1)S(1)} all-gather(bf16[32,128]{1,0:T(8,128)(2,1)S(1)} %get-tuple-element.80), channel_id=11, replica_groups={{0,32},{64,96},{128,160},{192,224},{256,288},{320,352},{384,416},{448,4..., dimensions={0}, use_global_device_ids=true | all-gather | bytes 24576 | tf_op jit(solution)/shard_map/all_gather | solution.py:18
  53.4 0.0 copy-done
  53.4 0.8 %respond.1 = f32[32,1,1,1024]{3,2,1,0:T(1,128)} custom-call(bf16[2,32,128]{2,1,0:T(8,128)(2,1)S(1)} %bitcast.43, bf16[32,128]{1,0:T(8,128)(2,1)S(1)} %get-tuple-element.81.own_final, f32[32,1024]{1,0:T(8,128)S(1)} %get-tuple-element.82.near, bf16[128,1024]{1,0:T(8,128)(2,1)S(1)} %bitcast.33), custom_call_target="tpu_custom_call" | custom-call | tf_op jit(solution)/shard_map/respond/pallas_call | solution.py:232
  (1 shorter events, 0.0 us)
Async XLA Ops:
  10.2 31.8 %copy-start.2 = (s32[1,1,8,9]{3,2,1,0:T(8,128)S(1)}, s32[1,1,8,9]{3,2,1,0:T(8,128)}, u32[]{:S(2)}) copy-start(s32[1,1,8,9]{3,2,1,0:T(8,128)} %param.14) | copy-start | bytes 868
  33.6 8.5 %collective-permute-start.4 = (bf16[2560,128]{1,0:T(8,128)(2,1)S(1)}, bf16[2560,128]{1,0:T(8,128)(2,1)S(1)}, u32[]{:S(2)}, u32[]{:S(2)}) collective-permute-start(bf16[2560,128]{1,0:T(8,128)(2,1)S(1)} %get-tuple-element.77), channel_id=1, source_target_pairs={{0,32},{64,96},{128,160},{192,224},{256,288},{320,352},{384,416},{... | collective-permute-start | bytes 1966088 | tf_op jit(solution)/shard_map/ppermute | solution.py:278
  42.1 11.4 %copy-start = (bf16[1,1,128,1024]{3,2,1,0:T(8,128)(2,1)S(1)}, bf16[1,1,128,1024]{3,2,1,0:T(8,128)(2,1)}, u32[]{:S(2)}) copy-start(bf16[1,1,128,1024]{3,2,1,0:T(8,128)(2,1)} %param.17) | copy-start | bytes 786436
  42.1 8.0 %copy-start.1 = (bf16[1,1,8,9,128,128]{5,4,3,2,1,0:T(8,128)(2,1)S(1)}, bf16[1,1,8,9,128,128]{5,4,3,2,1,0:T(8,128)(2,1)}, u32[]{:S(2)}) copy-start(bf16[1,1,8,9,128,128]{5,4,3,2,1,0:T(8,128)(2,1)} %get-tuple-element.55) | copy-start | bytes 7077892 | tf_op jit(solution)/shard_map/cond

commit v8 on v7

--- a/solution.py
+++ b/solution.py
@@ -18,15 +18,28 @@
     return lax.all_gather(values, axis, axis_index_groups=pairs)
 
 
-def sent_on(values, step_x, step_y):
+def swapped(values, axis, phase):
     count_x, count_y = lax.axis_size("bx"), lax.axis_size("by")
     moves = []
     for x in range(0, count_x, 2):
         for y in range(count_y):
-            to_x, to_y = x + step_x, y + step_y
-            if 0 <= to_x < count_x and 0 <= to_y < count_y:
-                moves.append((x * count_y + y, to_x * count_y + to_y))
+            place, count = (x // 2, count_x // 2) if axis == "bx" else (y, count_y)
+            other = place + (1 if place % 2 == phase else -1)
+            if 0 <= other < count:
+                target = 2 * other * count_y + y if axis == "bx" else x * count_y + other
+                moves.append((x * count_y + y, target))
     return lax.ppermute(values, BOTH, moves)
+
+
+def surroundings(boxes):
+    even = lax.axis_index("bx") >> 1 & 1 == 0
+    first = swapped(jnp.where(even, boxes[1], boxes[0]), "bx", 0)
+    second = swapped(jnp.where(even, boxes[0], boxes[1]), "bx", 1)
+    before, after = jnp.where(even, second, first), jnp.where(even, first, second)
+    row = jnp.concatenate([before[None], boxes, after[None]])
+    even = lax.axis_index("by") & 1 == 0
+    first, second = swapped(row, "by", 0), swapped(row, "by", 1)
+    return jnp.where(even, second, first), row, jnp.where(even, first, second)
 
 
 class Packing:
@@ -256,9 +269,7 @@
 
     def gathering():
         boxes = shared[:, packing.sources :].reshape(2, packing.blocks, excite, LANES)
-        before, after = sent_on(boxes[1], 2, 0), sent_on(boxes[0], -2, 0)
-        row = jnp.concatenate([before[None], boxes, after[None]])
-        below, above = sent_on(row, 0, 1), sent_on(row, 0, -1)
+        below, row, above = surroundings(boxes)
         given = jnp.concatenate([below[1:], row[3:], above[1:]]).reshape(-1, LANES)
         column = jnp.stack([below[0], row[0], above[0]]).reshape(-1, LANES)
         return jnp.zeros((2, excite, rank), jnp.bfloat16), jnp.concatenate([given, later]), column

time: 54.6 us -> 54.6 us (level)
  no operation moved by 1% of the time
where the time goes in v8:
time: 54.6 us; the launch traced here: 54.3 us
  blocking collectives  48 us (88%)
  Pallas kernels  4.85 us (9%)
  starting transfers between devices  1.29 us (2%)
    all_gather x10, blocking collectives, pair_gather(): return lax.all_gather(values, axis, axis_index_groups=pairs)  48 us
    pallas_call x1, Pallas kernels, near_of(): pl.pallas_call(functools.partial(near_field, packing, offset), name=f'nea...  1.54 us
    ppermute x1, starting transfers between devices, per_device(): lax.ppermute(given, 'bx', [(i, i ^ 1) for i in range(0, lax.axis_size('bx...  1.29 us
    pallas_call x1, Pallas kernels, packed_own(): pl.pallas_call(functools.partial(pack, packing), name='pack', compiler_pa...  1.28 us
    pallas_call x9, Pallas kernels, in_vmem(): call(*(pltpu.with_memory_space_constraint(x, pltpu.VMEM) for x in operands))  1.18 us
  transfers between devices with their start and end apart: 1, of which 0 were waited for; matrix products, arithmetic and copies ran while one was open for 0% of the time, Pallas kernels for 0%

profile of v8, /device:TPU:1, one launch (start us, length us, event | category | flops | bytes accessed | tf_op | source)
XLA Modules:
  0.0 54.3 jit_solution(16624588655137517538)
XLA Ops:
  0.0 1.3 %pack.1 = (bf16[1824,128]{1,0:T(8,128)(2,1)S(1)}, bf16[768,128]{1,0:T(8,128)(2,1)S(1)}) custom-call(bf16[2304,128]{1,0:T(8,128)(2,1)} %bitcast.49, bf16[32,1024]{1,0:T(8,128)(2,1)} %bitcast.53, bf16[1024,128]{1,0:T(8,128)(2,1)} %bitcast.51), custom_call_target="tpu_custom_call" | custom-call | tf_op jit(solution)/shard_map/pack/pallas_call | solution.py:102
  1.3 8.9 %all-gather.8 = bf16[3648,128]{1,0:T(8,128)(2,1)S(1)} all-gather(bf16[1824,128]{1,0:T(8,128)(2,1)S(1)} %get-tuple-element.74), channel_id=10, replica_groups={{0,32},{64,96},{128,160},{192,224},{256,288},{320,352},{384,416},{448,4..., dimensions={0}, use_global_device_ids=true | all-gather | bytes 1400832 | tf_op jit(solution)/shard_map/all_gather | solution.py:18
  10.2 0.0 copy-start.2
  10.2 23.4 %conditional.3 = (bf16[2,32,128]{2,1,0:T(8,128)(2,1)S(1)}, bf16[2560,128]{1,0:T(8,128)(2,1)S(1)}, bf16[768,128]{1,0:T(8,128)(2,1)S(1)}, bf16[2,32,128]{2,1,0:T(8,128)(2,1)S(1)}) conditional(s32[]{:T(128)} %convert_element_type.2, bf16[2,1824,128]{2,1,0:T(8,128)(2,1)S(1)} %bitcast.31, (bf16[2,1824,128]{2,1,0:T(8,128)(2,1)S(1)}, ...), branch_computations={%region_0.0_spmd, %region_1.2_spmd} | conditional | flops 2621450 | bytes 8683825 | solution.py:288
  10.2 0.1 level_0.1
  10.4 3.3 %all-gather = bf16[4,32,128]{2,1,0:T(8,128)(2,1)S(1)} all-gather(bf16[2,32,128]{2,1,0:T(8,128)(2,1)S(1)} %level_0.1), channel_id=2, replica_groups={{0,64},{32,96},{128,192},{160,224},{256,320},{288,352},{384,448},{416,4..., dimensions={0}, use_global_device_ids=true | all-gather | bytes 49152 | tf_op jit(solution)/shard_map/cond/branch_0_fun/all_gather | solution.py:18
  13.6 0.1 level_1.1
  13.7 4.8 %all-gather.1 = bf16[4,32,128]{2,1,0:T(8,128)(2,1)S(1)} all-gather(bf16[2,32,128]{2,1,0:T(8,128)(2,1)S(1)} %level_1.1), channel_id=3, replica_groups={{0,128},{32,160},{64,192},{96,224},{256,384},{288,416},{320,448},{352,4..., dimensions={0}, use_global_device_ids=true | all-gather | bytes 49152 | tf_op jit(solution)/shard_map/cond/branch_0_fun/all_gather | solution.py:18
  18.5 0.1 level_2.1
  18.6 7.2 %all-gather.2 = bf16[4,32,128]{2,1,0:T(8,128)(2,1)S(1)} all-gather(bf16[2,32,128]{2,1,0:T(8,128)(2,1)S(1)} %level_2.1), channel_id=4, replica_groups={{0,256},{32,288},{64,320},{96,352},{128,384},{160,416},{192,448},{224,4..., dimensions={0}, use_global_device_ids=true | all-gather | bytes 49152 | tf_op jit(solution)/shard_map/cond/branch_0_fun/all_gather | solution.py:18
  25.8 0.1 level_3.1
  25.9 3.3 %all-gather.3 = bf16[4,32,128]{2,1,0:T(8,128)(2,1)S(1)} all-gather(bf16[2,32,128]{2,1,0:T(8,128)(2,1)S(1)} %level_3.1), channel_id=5, replica_groups={{0,1},{2,3},{4,5},{6,7},{8,9},{10,11},{12,13},{14,15},{16,17},{18,19},{..., dimensions={0}, use_global_device_ids=true | all-gather | bytes 49152 | tf_op jit(solution)/shard_map/cond/branch_0_fun/all_gather | solution.py:18
  29.2 0.1 level_4.1
  29.3 4.2 %all-gather.4 = bf16[4,32,128]{2,1,0:T(8,128)(2,1)S(1)} all-gather(bf16[2,32,128]{2,1,0:T(8,128)(2,1)S(1)} %level_4.1), channel_id=6, replica_groups={{0,2},{1,3},{4,6},{5,7},{8,10},{9,11},{12,14},{13,15},{16,18},{17,19},{..., dimensions={0}, use_global_device_ids=true | all-gather | bytes 49152 | tf_op jit(solution)/shard_map/cond/branch_0_fun/all_gather | solution.py:18
  33.4 0.1 level_5.1
  33.6 1.3 %collective-permute-start.4 = (bf16[2560,128]{1,0:T(8,128)(2,1)S(1)}, bf16[2560,128]{1,0:T(8,128)(2,1)S(1)}, u32[]{:S(2)}, u32[]{:S(2)}) collective-permute-start(bf16[2560,128]{1,0:T(8,128)(2,1)S(1)} %get-tuple-element.77), channel_id=1, source_target_pairs={{0,32},{64,96},{128,160},{192,224},{256,288},{320,352},{384,416},{... | collective-permute-start | bytes 1966088 | tf_op jit(solution)/shard_map/ppermute | solution.py:289
  34.9 7.2 %conditional.4 = (bf16[2,2,32,128]{3,2,1,0:T(8,128)(2,1)S(1)}) conditional(s32[]{:T(128)} %convert_element_type.2, bf16[2,32,128]{2,1,0:T(8,128)(2,1)S(1)} %get-tuple-element.76, bf16[2,32,128]{2,1,0:T(8,128)(2,1)S(1)} %get-tuple-element.76), branch_computations={%region_2.3_spmd, %region_3.4_spmd} | conditional | flops 16384 | bytes 49160 | solution.py:290
  34.9 7.2 %all-gather.5 = bf16[4,32,128]{2,1,0:T(8,128)(2,1)S(1)} all-gather(bf16[2,32,128]{2,1,0:T(8,128)(2,1)S(1)} %param.2), channel_id=7, replica_groups={{0,4},{1,5},{2,6},{3,7},{8,12},{9,13},{10,14},{11,15},{16,20},{17,21},{..., dimensions={0}, use_global_device_ids=true | all-gather | bytes 49152 | tf_op jit(solution)/shard_map/cond/branch_0_fun/all_gather | solution.py:18
  42.1 0.0 collective-permute-done.4
  42.1 0.0 copy-done.2
  42.1 0.0 copy-start
  42.1 9.5 %conditional.5 = (f32[32,1024]{1,0:T(8,128)S(1)}, bf16[32,128]{1,0:T(8,128)(2,1)S(1)}, bf16[32,128]{1,0:T(8,128)(2,1)S(1)}) conditional(s32[]{:T(128)} %convert_element_type.2, (bf16[2,2,32,128]{3,2,1,0:T(8,128)(2,1)S(1)}, bf16[2560,128]{1,0:T(8,128)(2,1)S(1)}, bf16[768,128]{1,0:T(8,128)(2,1)S(1)}, bf16[1,1,8,9,128,128]{5,4,3,2,1,0:T(8,128)(2,1)}, ...), branch_computations={%region_4.5_spmd, %region_5.6_spmd} | conditional | bytes 9535540 | solution.py:315
  42.1 0.0 copy-start.1
  42.1 0.1 level_6.1
  42.2 3.4 %all-gather.6 = bf16[4,32,128]{2,1,0:T(8,128)(2,1)S(1)} all-gather(bf16[2,32,128]{2,1,0:T(8,128)(2,1)S(1)} %level_6.1), channel_id=8, replica_groups={{0,8},{1,9},{2,10},{3,11},{4,12},{5,13},{6,14},{7,15},{16,24},{17,25},{..., dimensions={0}, use_global_device_ids=true | all-gather | bytes 49152 | tf_op jit(solution)/shard_map/cond/branch_0_fun/all_gather | solution.py:18
  45.6 0.1 level_7.1
  45.8 4.2 %all-gather.7 = bf16[4,32,128]{2,1,0:T(8,128)(2,1)S(1)} all-gather(bf16[2,32,128]{2,1,0:T(8,128)(2,1)S(1)} %level_7.1), channel_id=9, replica_groups={{0,16},{1,17},{2,18},{3,19},{4,20},{5,21},{6,22},{7,23},{8,24},{9,25},{..., dimensions={0}, use_global_device_ids=true | all-gather | bytes 49152 | tf_op jit(solution)/shard_map/cond/branch_0_fun/all_gather | solution.py:18
  49.9 0.1 level_8.1
  50.0 0.0 copy-done.1
  50.1 1.5 %near_1.1 = f32[32,1024]{1,0:T(8,128)S(1)} custom-call(bf16[2560,128]{1,0:T(8,128)(2,1)S(1)} %get-tuple-element.53.rest_0_.theirs.beside, bf16[2,1824,128]{2,1,0:T(8,128)(2,1)S(1)} %get-tuple-element.54.shared, bf16[9216,128]{1,0:T(8,128)(2,1)S(1)} %bitcast.46, s32[8,9]{1,0:T(8,128)S(1)} %get-tuple-element.56.rest_1_), custom_call_target="tpu_custom_call" | custom-call | tf_op jit(solution)/shard_map/cond/branch_0_fun/near_1/pallas_call | solution.py:210
  51.6 1.8 %all-gather.9 = bf16[64,128]{1,0:T(8,128)(2,1)S(1)} all-gather(bf16[32,128]{1,0:T(8,128)(2,1)S(1)} %get-tuple-element.80), channel_id=11, replica_groups={{0,32},{64,96},{128,160},{192,224},{256,288},{320,352},{384,416},{448,4..., dimensions={0}, use_global_device_ids=true | all-gather | bytes 24576 | tf_op jit(solution)/shard_map/all_gather | solution.py:18
  53.4 0.0 copy-done
  53.4 0.8 %respond.1 = f32[32,1,1,1024]{3,2,1,0:T(1,128)} custom-call(bf16[2,32,128]{2,1,0:T(8,128)(2,1)S(1)} %bitcast.45, bf16[32,128]{1,0:T(8,128)(2,1)S(1)} %get-tuple-element.81.own_final, f32[32,1024]{1,0:T(8,128)S(1)} %get-tuple-element.82.near, bf16[128,1024]{1,0:T(8,128)(2,1)S(1)} %bitcast.35), custom_call_target="tpu_custom_call" | custom-call | tf_op jit(solution)/shard_map/respond/pallas_call | solution.py:245
  (1 shorter events, 0.0 us)
Async XLA Ops:
  10.2 31.8 %copy-start.2 = (s32[1,1,8,9]{3,2,1,0:T(8,128)S(1)}, s32[1,1,8,9]{3,2,1,0:T(8,128)}, u32[]{:S(2)}) copy-start(s32[1,1,8,9]{3,2,1,0:T(8,128)} %param.14) | copy-start | bytes 868
  33.6 8.5 %collective-permute-start.4 = (bf16[2560,128]{1,0:T(8,128)(2,1)S(1)}, bf16[2560,128]{1,0:T(8,128)(2,1)S(1)}, u32[]{:S(2)}, u32[]{:S(2)}) collective-permute-start(bf16[2560,128]{1,0:T(8,128)(2,1)S(1)} %get-tuple-element.77), channel_id=1, source_target_pairs={{0,32},{64,96},{128,160},{192,224},{256,288},{320,352},{384,416},{... | collective-permute-start | bytes 1966088 | tf_op jit(solution)/shard_map/ppermute | solution.py:289
  42.1 11.4 %copy-start = (bf16[1,1,128,1024]{3,2,1,0:T(8,128)(2,1)S(1)}, bf16[1,1,128,1024]{3,2,1,0:T(8,128)(2,1)}, u32[]{:S(2)}) copy-start(bf16[1,1,128,1024]{3,2,1,0:T(8,128)(2,1)} %param.17) | copy-start | bytes 786436
  42.1 8.0 %copy-start.1 = (bf16[1,1,8,9,128,128]{5,4,3,2,1,0:T(8,128)(2,1)S(1)}, bf16[1,1,8,9,128,128]{5,4,3,2,1,0:T(8,128)(2,1)}, u32[]{:S(2)}) copy-start(bf16[1,1,8,9,128,128]{5,4,3,2,1,0:T(8,128)(2,1)} %get-tuple-element.55) | copy-start | bytes 7077892 | tf_op jit(solution)/shard_map/cond

commit v9 on v8

--- a/solution.py
+++ b/solution.py
@@ -16,6 +16,14 @@
     count = lax.axis_size(axis)
     pairs = [[i, i ^ 1 << apart] for i in range(count) if not i >> apart & 1]
     return lax.all_gather(values, axis, axis_index_groups=pairs)
+
+
+def four_exchange(copies, axis, apart):
+    groups = []
+    for base in range(lax.axis_size(axis)):
+        if not base >> apart & 3:
+            groups.append([base | g << apart for g in range(4)])
+    return lax.all_to_all(copies, axis, 0, 0, axis_index_groups=groups)
 
 
 def swapped(values, axis, phase):
@@ -31,6 +39,12 @@
     return lax.ppermute(values, BOTH, moves)
 
 
+def fetched_from(values, apart):
+    count_x, count_y = lax.axis_size("bx"), lax.axis_size("by")
+    at = [x * count_y + y for x in range(0, count_x, 2) for y in range(count_y)]
+    return lax.ppermute(values, BOTH, [(i, i ^ 1 << apart) for i in at])
+
+
 def surroundings(boxes):
     even = lax.axis_index("bx") >> 1 & 1 == 0
     first = swapped(jnp.where(even, boxes[1], boxes[0]), "bx", 0)
@@ -53,7 +67,8 @@
         self.first_rows = self.sources + self.box_rows
         self.late_rows = (levels - self.split) * self.level_rows
         self.late = 7 * self.box_rows
-        self.second_rows = self.late + self.late_rows
+        self.fetched = self.late + self.late_rows
+        self.second_rows = self.fetched + 2 * self.level_rows
 
     def place_of(self, level):
         return (level if level < self.split else level - self.split) * self.level_rows
@@ -144,6 +159,37 @@
     return sums
 
 
+def two_levels(packing, level, place, four, shared, theirs, own, coeffs):
+    axis, apart = place
+    rows = packing.level_rows
+    bit, next_bit = (lax.axis_index(axis) >> apart + n & 1 for n in range(2))
+    start = packing.place_of(level)
+
+    def product(low, high, weights):
+        pair = jnp.concatenate([low, high], axis=1)
+        return jnp.dot(pair, weights, preferred_element_type=jnp.float32).astype(jnp.bfloat16)
+
+    for box in range(2):
+        near, far = 2 * next_bit, 2 * (1 - next_bit)
+        here = product(
+            four[near + bit, box], four[near + 1 - bit, box], shared[box, pl.ds(start, rows)]
+        )
+        there = product(
+            four[far + bit, box],
+            four[far + 1 - bit, box],
+            theirs[pl.ds(packing.fetched + box * rows, rows)],
+        )
+        at = packing.place_of(level + 1)
+        weights = theirs[pl.ds(packing.late + at, rows)] if box == 0 else own[pl.ds(at, rows)]
+        coeffs[box] = product(here, there, weights)
+
+
+def spread_level(packing, level, place, both, *rest):
+    for box, value in enumerate(mixed(packing, level, place, both, rest[:1])):
+        for member in range(4):
+            rest[1][member, box] = value
+
+
 def next_level(packing, level, place, both, *rest):
     blocks = rest[: 1 if level < packing.split else 2]
     coeffs = rest[len(blocks)]
@@ -264,50 +310,54 @@
     packed, later = packed_own(packing, far_mixing[0, 0], own_sources, far_project[0, 0])
     shared = pair_gather(packed, "bx", 0)
     coeffs_shape = pltpu.VMEM((2, excite, rank), jnp.bfloat16)
+    four_shape = pltpu.VMEM((4, 2, excite, rank), jnp.bfloat16)
     column_shape = pltpu.VMEM((3 * packing.box_rows, LANES), jnp.bfloat16)
     given_shape = pltpu.VMEM((packing.second_rows, LANES), jnp.bfloat16)
+    merged = packing.split - 1
+    apart = levels[merged][1]
 
     def gathering():
+        start = packing.place_of(merged)
+        fetched = fetched_from(shared[:, start : start + packing.level_rows], apart + 1)
         boxes = shared[:, packing.sources :].reshape(2, packing.blocks, excite, LANES)
         below, row, above = surroundings(boxes)
         given = jnp.concatenate([below[1:], row[3:], above[1:]]).reshape(-1, LANES)
         column = jnp.stack([below[0], row[0], above[0]]).reshape(-1, LANES)
-        return jnp.zeros((2, excite, rank), jnp.bfloat16), jnp.concatenate([given, later]), column
+        given = jnp.concatenate([given, later, fetched.reshape(-1, LANES)])
+        return jnp.zeros((4, 2, excite, rank), jnp.bfloat16), given, column
 
     def levels_early():
         coeffs = in_vmem(functools.partial(first_level, packing), "level_0", coeffs_shape, (shared,))
-        for level in range(1, packing.split):
-            shape = coeffs_shape
-            if level == packing.split - 1:
-                shape = (coeffs_shape, given_shape, column_shape)
+        for level in range(1, merged):
+            kernel, shape = next_level, coeffs_shape
+            if level == merged - 1:
+                kernel, shape = spread_level, (four_shape, given_shape, column_shape)
             both = pair_gather(coeffs, *levels[level])
-            kernel = functools.partial(next_level, packing, level, levels[level])
+            kernel = functools.partial(kernel, packing, level, levels[level])
             coeffs = in_vmem(kernel, f"level_{level}", shape, (both, shared))
         return tuple(coeffs)
 
-    coeffs, given, column = lax.cond(first_of_pair, gathering, levels_early)
+    copies, given, column = lax.cond(first_of_pair, gathering, levels_early)
     handed = lax.ppermute(given, "bx", [(i, i ^ 1) for i in range(0, lax.axis_size("bx"), 2)])
-    both = lax.cond(
-        first_of_pair,
-        lambda: jnp.stack([coeffs, coeffs]),
-        lambda: pair_gather(coeffs, *levels[packing.split]),
+    four = lax.cond(
+        first_of_pair, lambda: copies, lambda: four_exchange(copies, *levels[merged])
     )
 
     def near_only():
         near = near_of(packing, 0, given, shared, (column,), own_blocks, own_index)
-        return near, coeffs[0], coeffs[1]
+        return near, copies[0, 0], copies[0, 1]
 
     def levels_late():
-        gathered = both
-        for level in range(packing.split, len(levels)):
+        kernel = functools.partial(two_levels, packing, merged, levels[merged])
+        result = in_vmem(kernel, "two_levels", coeffs_shape, (four, shared, handed, later))
+        for level in range(merged + 2, len(levels)):
             kernel = functools.partial(next_level, packing, level, levels[level])
             shape = coeffs_shape
             if level == len(levels) - 1:
                 kernel = functools.partial(last_level, packing, level, levels[level])
                 shape = (pltpu.VMEM((excite, rank), jnp.bfloat16),) * 2
-            result = in_vmem(kernel, f"level_{level}", shape, (gathered, handed, later))
-            if level < len(levels) - 1:
-                gathered = pair_gather(result, *levels[level + 1])
+            both = pair_gather(result, *levels[level])
+            result = in_vmem(kernel, f"level_{level}", shape, (both, handed, later))
         beside, result = lax.optimization_barrier((handed, tuple(result)))
         near = near_of(packing, 1, beside, shared, (), own_blocks, own_index)
         return near, *result

time: 54.6 us -> 57.6 us (1.055)
  the two profiles are of different devices: /device:TPU:1 before, /device:TPU:449 now
where the time goes in v9:
time: 57.6 us; the launch traced here: 57.3 us
  blocking collectives  44.6 us (77%)
  waiting for transfers between devices  6.35 us (11%)
  Pallas kernels  4.97 us (9%)
  starting transfers between devices  1.29 us (2%)
    all_gather x8, blocking collectives, pair_gather(): return lax.all_gather(values, axis, axis_index_groups=pairs)  30.6 us
    all_to_all x1, blocking collectives, four_exchange(): return lax.all_to_all(copies, axis, 0, 0, axis_index_groups=groups)  14 us
    ppermute x1, waiting for transfers between devices, per_device(): lax.ppermute(given, 'bx', [(i, i ^ 1) for i in range(0, lax.axis_size('bx...  6.35 us
    pallas_call x1, Pallas kernels, near_of(): pl.pallas_call(functools.partial(near_field, packing, offset), name=f'nea...  1.54 us
    pallas_call x8, Pallas kernels, in_vmem(): call(*(pltpu.with_memory_space_constraint(x, pltpu.VMEM) for x in operands))  1.31 us
    ppermute x1, starting transfers between devices, per_device(): lax.ppermute(given, 'bx', [(i, i ^ 1) for i in range(0, lax.axis_size('bx...  1.29 us
    pallas_call x1, Pallas kernels, packed_own(): pl.pallas_call(functools.partial(pack, packing), name='pack', compiler_pa...  1.28 us
  transfers between devices with their start and end apart: 1, of which 1 were waited for; matrix products, arithmetic and copies ran while one was open for 0% of the time, Pallas kernels for 0%

profile of v9, /device:TPU:449, one launch (start us, length us, event | category | flops | bytes accessed | tf_op | source)
XLA Modules:
  0.0 57.3 jit_solution(7342340320245401610)
XLA Ops:
  0.0 1.3 %pack.1 = (bf16[1824,128]{1,0:T(8,128)(2,1)S(1)}, bf16[768,128]{1,0:T(8,128)(2,1)S(1)}) custom-call(bf16[2304,128]{1,0:T(8,128)(2,1)} %bitcast.45, bf16[32,1024]{1,0:T(8,128)(2,1)} %bitcast.49, bf16[1024,128]{1,0:T(8,128)(2,1)} %bitcast.47), custom_call_target="tpu_custom_call" | custom-call | tf_op jit(solution)/shard_map/pack/pallas_call | solution.py:117
  1.3 2.8 %all-gather.6 = bf16[3648,128]{1,0:T(8,128)(2,1)S(1)} all-gather(bf16[1824,128]{1,0:T(8,128)(2,1)S(1)} %get-tuple-element.74), channel_id=8, replica_groups={{0,32},{64,96},{128,160},{192,224},{256,288},{320,352},{384,416},{448,4..., dimensions={0}, use_global_device_ids=true | all-gather | bytes 1400832 | tf_op jit(solution)/shard_map/all_gather | solution.py:18
  4.1 0.0 copy-start.2
  4.1 19.1 %conditional.3 = (bf16[4,2,32,128]{3,2,1,0:T(8,128)(2,1)S(1)}, bf16[3072,128]{1,0:T(8,128)(2,1)S(1)}, bf16[768,128]{1,0:T(8,128)(2,1)S(1)}, bf16[4,2,32,128]{3,2,1,0:T(8,128)(2,1)S(1)}) conditional(s32[]{:T(128)} %convert_element_type.2, bf16[2,1824,128]{2,1,0:T(8,128)(2,1)S(1)} %bitcast.29, (bf16[2,1824,128]{2,1,0:T(8,128)(2,1)S(1)}, ...), branch_computations={%region_0.0_spmd, %region_1.2_spmd} | conditional | flops 3670026 | bytes 9830745 | solution.py:340
  4.1 0.1 level_0.1
  4.2 3.3 %all-gather = bf16[4,32,128]{2,1,0:T(8,128)(2,1)S(1)} all-gather(bf16[2,32,128]{2,1,0:T(8,128)(2,1)S(1)} %level_0.1), channel_id=2, replica_groups={{0,64},{32,96},{128,192},{160,224},{256,320},{288,352},{384,448},{416,4..., dimensions={0}, use_global_device_ids=true | all-gather | bytes 49152 | tf_op jit(solution)/shard_map/cond/branch_0_fun/all_gather | solution.py:18
  7.4 0.1 level_1.1
  7.6 4.8 %all-gather.1 = bf16[4,32,128]{2,1,0:T(8,128)(2,1)S(1)} all-gather(bf16[2,32,128]{2,1,0:T(8,128)(2,1)S(1)} %level_1.1), channel_id=3, replica_groups={{0,128},{32,160},{64,192},{96,224},{256,384},{288,416},{320,448},{352,4..., dimensions={0}, use_global_device_ids=true | all-gather | bytes 49152 | tf_op jit(solution)/shard_map/cond/branch_0_fun/all_gather | solution.py:18
  12.3 0.1 level_2.1
  12.5 7.2 %all-gather.2 = bf16[4,32,128]{2,1,0:T(8,128)(2,1)S(1)} all-gather(bf16[2,32,128]{2,1,0:T(8,128)(2,1)S(1)} %level_2.1), channel_id=4, replica_groups={{0,256},{32,288},{64,320},{96,352},{128,384},{160,416},{192,448},{224,4..., dimensions={0}, use_global_device_ids=true | all-gather | bytes 49152 | tf_op jit(solution)/shard_map/cond/branch_0_fun/all_gather | solution.py:18
  19.7 0.1 level_3.1
  19.8 3.3 %all-gather.3 = bf16[4,32,128]{2,1,0:T(8,128)(2,1)S(1)} all-gather(bf16[2,32,128]{2,1,0:T(8,128)(2,1)S(1)} %level_3.1), channel_id=5, replica_groups={{0,1},{2,3},{4,5},{6,7},{8,9},{10,11},{12,13},{14,15},{16,17},{18,19},{..., dimensions={0}, use_global_device_ids=true | all-gather | bytes 49152 | tf_op jit(solution)/shard_map/cond/branch_0_fun/all_gather | solution.py:18
  23.0 0.1 level_4.1
  23.2 1.3 %collective-permute-start.5 = (bf16[3072,128]{1,0:T(8,128)(2,1)S(1)}, bf16[3072,128]{1,0:T(8,128)(2,1)S(1)}, u32[]{:S(2)}, u32[]{:S(2)}) collective-permute-start(bf16[3072,128]{1,0:T(8,128)(2,1)S(1)} %get-tuple-element.77), channel_id=1, source_target_pairs={{0,32},{64,96},{128,160},{192,224},{256,288},{320,352},{384,416},{... | collective-permute-start | bytes 2359304 | tf_op jit(solution)/shard_map/ppermute | solution.py:341
  24.5 14.0 %conditional.4 = (bf16[4,2,32,128]{3,2,1,0:T(8,128)(2,1)S(1)}) conditional(s32[]{:T(128)} %convert_element_type.2, bf16[4,2,32,128]{3,2,1,0:T(8,128)(2,1)S(1)} %get-tuple-element.76, bf16[4,2,32,128]{3,2,1,0:T(8,128)(2,1)S(1)} %get-tuple-element.76), branch_computations={%region_2.3_spmd, %region_3.4_spmd} | conditional | bytes 262152 | solution.py:342
  24.5 14.0 %all_to_all.4 = bf16[4,2,32,128]{3,2,1,0:T(8,128)(2,1)S(1)} all-to-all(bf16[4,2,32,128]{3,2,1,0:T(8,128)(2,1)S(1)} %copy.23), channel_id=1, replica_groups={{0,2,4,6},{1,3,5,7},{8,10,12,14},{9,11,13,15},{16,18,20,22},{17,19,21,2..., dimensions={0} | all-to-all | bytes 131072 | tf_op jit(solution)/shard_map/cond/branch_0_fun/all_to_all | solution.py:26
  38.5 6.3 %collective-permute-done.5 = bf16[3072,128]{1,0:T(8,128)(2,1)S(1)} collective-permute-done((bf16[3072,128]{1,0:T(8,128)(2,1)S(1)}, bf16[3072,128]{1,0:T(8,128)(2,1)S(1)}, u32[]{:S(2)}, u32[]{:S(2)}) %collective-permute-start.5) | collective-permute-done | bytes 786464 | tf_op jit(solution)/shard_map/ppermute | solution.py:341
  44.8 0.0 copy-done.2
  44.8 0.0 copy-start
  44.8 9.8 %conditional.5 = (f32[32,1024]{1,0:T(8,128)S(1)}, bf16[32,128]{1,0:T(8,128)(2,1)S(1)}, bf16[32,128]{1,0:T(8,128)(2,1)S(1)}) conditional(s32[]{:T(128)} %convert_element_type.2, (bf16[4,2,32,128]{3,2,1,0:T(8,128)(2,1)S(1)}, bf16[2,1824,128]{2,1,0:T(8,128)(2,1)S(1)}, bf16[3072,128]{1,0:T(8,128)(2,1)S(1)}, bf16[768,128]{1,0:T(8,128)(2,1)S(1)}, ...), branch_computations={%region_4.5_spmd, %region_5.6_spmd} | conditional | bytes 9535540 | solution.py:365
  44.8 0.0 copy-start.1
  44.9 0.4 two_levels.1
  45.2 3.4 %all-gather.4 = bf16[4,32,128]{2,1,0:T(8,128)(2,1)S(1)} all-gather(bf16[2,32,128]{2,1,0:T(8,128)(2,1)S(1)} %two_levels.1), channel_id=6, replica_groups={{0,8},{1,9},{2,10},{3,11},{4,12},{5,13},{6,14},{7,15},{16,24},{17,25},{..., dimensions={0}, use_global_device_ids=true | all-gather | bytes 49152 | tf_op jit(solution)/shard_map/cond/branch_0_fun/all_gather | solution.py:18
  48.6 0.1 level_7.1
  48.8 4.2 %all-gather.5 = bf16[4,32,128]{2,1,0:T(8,128)(2,1)S(1)} all-gather(bf16[2,32,128]{2,1,0:T(8,128)(2,1)S(1)} %level_7.1), channel_id=7, replica_groups={{0,16},{1,17},{2,18},{3,19},{4,20},{5,21},{6,22},{7,23},{8,24},{9,25},{..., dimensions={0}, use_global_device_ids=true | all-gather | bytes 49152 | tf_op jit(solution)/shard_map/cond/branch_0_fun/all_gather | solution.py:18
  52.9 0.1 level_8.1
  53.1 0.0 copy-done.1
  53.1 1.5 %near_1.1 = f32[32,1024]{1,0:T(8,128)S(1)} custom-call(bf16[3072,128]{1,0:T(8,128)(2,1)S(1)} %get-tuple-element.54.theirs.rest_0_.beside, bf16[2,1824,128]{2,1,0:T(8,128)(2,1)S(1)} %get-tuple-element.50.shared, bf16[9216,128]{1,0:T(8,128)(2,1)S(1)} %bitcast.42, s32[8,9]{1,0:T(8,128)S(1)} %get-tuple-element.56.rest_1_), custom_call_target="tpu_custom_call" | custom-call | tf_op jit(solution)/shard_map/cond/branch_0_fun/near_1/pallas_call | solution.py:256
  54.6 1.8 %all-gather.7 = bf16[64,128]{1,0:T(8,128)(2,1)S(1)} all-gather(bf16[32,128]{1,0:T(8,128)(2,1)S(1)} %get-tuple-element.80), channel_id=9, replica_groups={{0,32},{64,96},{128,160},{192,224},{256,288},{320,352},{384,416},{448,4..., dimensions={0}, use_global_device_ids=true | all-gather | bytes 24576 | tf_op jit(solution)/shard_map/all_gather | solution.py:18
  56.4 0.0 copy-done
  56.4 0.8 %respond.1 = f32[32,1,1,1024]{3,2,1,0:T(1,128)} custom-call(bf16[2,32,128]{2,1,0:T(8,128)(2,1)S(1)} %bitcast.41, bf16[32,128]{1,0:T(8,128)(2,1)S(1)} %get-tuple-element.81.own_final, f32[32,1024]{1,0:T(8,128)S(1)} %get-tuple-element.82.near, bf16[128,1024]{1,0:T(8,128)(2,1)S(1)} %bitcast.33), custom_call_target="tpu_custom_call" | custom-call | tf_op jit(solution)/shard_map/respond/pallas_call | solution.py:291
  (2 shorter events, 0.0 us)
Async XLA Ops:
  4.1 40.8 %copy-start.2 = (s32[1,1,8,9]{3,2,1,0:T(8,128)S(1)}, s32[1,1,8,9]{3,2,1,0:T(8,128)}, u32[]{:S(2)}) copy-start(s32[1,1,8,9]{3,2,1,0:T(8,128)} %param.14) | copy-start | bytes 868
  23.2 21.6 %collective-permute-start.5 = (bf16[3072,128]{1,0:T(8,128)(2,1)S(1)}, bf16[3072,128]{1,0:T(8,128)(2,1)S(1)}, u32[]{:S(2)}, u32[]{:S(2)}) collective-permute-start(bf16[3072,128]{1,0:T(8,128)(2,1)S(1)} %get-tuple-element.77), channel_id=1, source_target_pairs={{0,32},{64,96},{128,160},{192,224},{256,288},{320,352},{384,416},{... | collective-permute-start | bytes 2359304 | tf_op jit(solution)/shard_map/ppermute | solution.py:341
  44.8 11.6 %copy-start = (bf16[1,1,128,1024]{3,2,1,0:T(8,128)(2,1)S(1)}, bf16[1,1,128,1024]{3,2,1,0:T(8,128)(2,1)}, u32[]{:S(2)}) copy-start(bf16[1,1,128,1024]{3,2,1,0:T(8,128)(2,1)} %param.17) | copy-start | bytes 786436
  44.8 8.2 %copy-start.1 = (bf16[1,1,8,9,128,128]{5,4,3,2,1,0:T(8,128)(2,1)S(1)}, bf16[1,1,8,9,128,128]{5,4,3,2,1,0:T(8,128)(2,1)}, u32[]{:S(2)}) copy-start(bf16[1,1,8,9,128,128]{5,4,3,2,1,0:T(8,128)(2,1)} %get-tuple-element.55) | copy-start | bytes 7077892 | tf_op jit(solution)/shard_map/cond

commit v10 on v9

--- a/solution.py
+++ b/solution.py
@@ -45,15 +45,16 @@
     return lax.ppermute(values, BOTH, [(i, i ^ 1 << apart) for i in at])
 
 
-def surroundings(boxes):
+def surroundings(boxes, meanwhile):
     even = lax.axis_index("bx") >> 1 & 1 == 0
     first = swapped(jnp.where(even, boxes[1], boxes[0]), "bx", 0)
     second = swapped(jnp.where(even, boxes[0], boxes[1]), "bx", 1)
     before, after = jnp.where(even, second, first), jnp.where(even, first, second)
     row = jnp.concatenate([before[None], boxes, after[None]])
+    row, meanwhile = lax.optimization_barrier((row, meanwhile))
     even = lax.axis_index("by") & 1 == 0
     first, second = swapped(row, "by", 0), swapped(row, "by", 1)
-    return jnp.where(even, second, first), row, jnp.where(even, first, second)
+    return jnp.where(even, second, first), row, jnp.where(even, first, second), meanwhile
 
 
 class Packing:
@@ -320,7 +321,7 @@
         start = packing.place_of(merged)
         fetched = fetched_from(shared[:, start : start + packing.level_rows], apart + 1)
         boxes = shared[:, packing.sources :].reshape(2, packing.blocks, excite, LANES)
-        below, row, above = surroundings(boxes)
+        below, row, above, fetched = surroundings(boxes, fetched)
         given = jnp.concatenate([below[1:], row[3:], above[1:]]).reshape(-1, LANES)
         column = jnp.stack([below[0], row[0], above[0]]).reshape(-1, LANES)
         given = jnp.concatenate([given, later, fetched.reshape(-1, LANES)])

time: 57.6 us -> 59.6 us (1.035)
  the two profiles are of different devices: /device:TPU:449 before, /device:TPU:7 now
where the time goes in v10:
time: 59.6 us; the launch traced here: 59.3 us
  blocking collectives  52.9 us (89%)
  Pallas kernels  4.97 us (8%)
  starting transfers between devices  1.29 us (2%)
    all_gather x8, blocking collectives, pair_gather(): return lax.all_gather(values, axis, axis_index_groups=pairs)  38.4 us
    all_to_all x1, blocking collectives, four_exchange(): return lax.all_to_all(copies, axis, 0, 0, axis_index_groups=groups)  14.5 us
    pallas_call x1, Pallas kernels, near_of(): pl.pallas_call(functools.partial(near_field, packing, offset), name=f'nea...  1.53 us
    pallas_call x8, Pallas kernels, in_vmem(): call(*(pltpu.with_memory_space_constraint(x, pltpu.VMEM) for x in operands))  1.31 us
    ppermute x1, starting transfers between devices, per_device(): lax.ppermute(given, 'bx', [(i, i ^ 1) for i in range(0, lax.axis_size('bx...  1.29 us
    pallas_call x1, Pallas kernels, packed_own(): pl.pallas_call(functools.partial(pack, packing), name='pack', compiler_pa...  1.28 us
  transfers between devices with their start and end apart: 1, of which 0 were waited for; matrix products, arithmetic and copies ran while one was open for 0% of the time, Pallas kernels for 0%

profile of v10, /device:TPU:7, one launch (start us, length us, event | category | flops | bytes accessed | tf_op | source)
XLA Modules:
  0.0 59.3 jit_solution(6049505917375222664)
XLA Ops:
  0.0 1.3 %pack.1 = (bf16[1824,128]{1,0:T(8,128)(2,1)S(1)}, bf16[768,128]{1,0:T(8,128)(2,1)S(1)}) custom-call(bf16[2304,128]{1,0:T(8,128)(2,1)} %bitcast.45, bf16[32,1024]{1,0:T(8,128)(2,1)} %bitcast.49, bf16[1024,128]{1,0:T(8,128)(2,1)} %bitcast.47), custom_call_target="tpu_custom_call" | custom-call | tf_op jit(solution)/shard_map/pack/pallas_call | solution.py:118
  1.3 2.8 %all-gather.6 = bf16[3648,128]{1,0:T(8,128)(2,1)S(1)} all-gather(bf16[1824,128]{1,0:T(8,128)(2,1)S(1)} %get-tuple-element.76), channel_id=8, replica_groups={{0,32},{64,96},{128,160},{192,224},{256,288},{320,352},{384,416},{448,4..., dimensions={0}, use_global_device_ids=true | all-gather | bytes 1400832 | tf_op jit(solution)/shard_map/all_gather | solution.py:18
  4.1 0.0 copy-start.2
  4.1 22.4 %conditional.3 = (bf16[4,2,32,128]{3,2,1,0:T(8,128)(2,1)S(1)}, bf16[3072,128]{1,0:T(8,128)(2,1)S(1)}, bf16[768,128]{1,0:T(8,128)(2,1)S(1)}, bf16[4,2,32,128]{3,2,1,0:T(8,128)(2,1)S(1)}) conditional(s32[]{:T(128)} %convert_element_type.2, bf16[2,1824,128]{2,1,0:T(8,128)(2,1)S(1)} %bitcast.29, (bf16[2,1824,128]{2,1,0:T(8,128)(2,1)S(1)}, ...), branch_computations={%region_0.0_spmd, %region_1.2_spmd} | conditional | flops 3670026 | bytes 10092889 | solution.py:341
  4.1 0.1 level_0.1
  4.2 3.3 %all-gather = bf16[4,32,128]{2,1,0:T(8,128)(2,1)S(1)} all-gather(bf16[2,32,128]{2,1,0:T(8,128)(2,1)S(1)} %level_0.1), channel_id=2, replica_groups={{0,64},{32,96},{128,192},{160,224},{256,320},{288,352},{384,448},{416,4..., dimensions={0}, use_global_device_ids=true | all-gather | bytes 49152 | tf_op jit(solution)/shard_map/cond/branch_0_fun/all_gather | solution.py:18
  7.4 0.1 level_1.1
  7.6 7.1 %all-gather.1 = bf16[4,32,128]{2,1,0:T(8,128)(2,1)S(1)} all-gather(bf16[2,32,128]{2,1,0:T(8,128)(2,1)S(1)} %level_1.1), channel_id=3, replica_groups={{0,128},{32,160},{64,192},{96,224},{256,384},{288,416},{320,448},{352,4..., dimensions={0}, use_global_device_ids=true | all-gather | bytes 49152 | tf_op jit(solution)/shard_map/cond/branch_0_fun/all_gather | solution.py:18
  14.7 0.1 level_2.1
  14.8 8.1 %all-gather.2 = bf16[4,32,128]{2,1,0:T(8,128)(2,1)S(1)} all-gather(bf16[2,32,128]{2,1,0:T(8,128)(2,1)S(1)} %level_2.1), channel_id=4, replica_groups={{0,256},{32,288},{64,320},{96,352},{128,384},{160,416},{192,448},{224,4..., dimensions={0}, use_global_device_ids=true | all-gather | bytes 49152 | tf_op jit(solution)/shard_map/cond/branch_0_fun/all_gather | solution.py:18
  23.0 0.1 level_3.1
  23.1 3.3 %all-gather.3 = bf16[4,32,128]{2,1,0:T(8,128)(2,1)S(1)} all-gather(bf16[2,32,128]{2,1,0:T(8,128)(2,1)S(1)} %level_3.1), channel_id=5, replica_groups={{0,1},{2,3},{4,5},{6,7},{8,9},{10,11},{12,13},{14,15},{16,17},{18,19},{..., dimensions={0}, use_global_device_ids=true | all-gather | bytes 49152 | tf_op jit(solution)/shard_map/cond/branch_0_fun/all_gather | solution.py:18
  26.4 0.1 level_4.1
  26.5 1.3 %collective-permute-start.5 = (bf16[3072,128]{1,0:T(8,128)(2,1)S(1)}, bf16[3072,128]{1,0:T(8,128)(2,1)S(1)}, u32[]{:S(2)}, u32[]{:S(2)}) collective-permute-start(bf16[3072,128]{1,0:T(8,128)(2,1)S(1)} %get-tuple-element.79), channel_id=1, source_target_pairs={{0,32},{64,96},{128,160},{192,224},{256,288},{320,352},{384,416},{... | collective-permute-start | bytes 2359304 | tf_op jit(solution)/shard_map/ppermute | solution.py:342
  27.8 14.5 %conditional.4 = (bf16[4,2,32,128]{3,2,1,0:T(8,128)(2,1)S(1)}) conditional(s32[]{:T(128)} %convert_element_type.2, bf16[4,2,32,128]{3,2,1,0:T(8,128)(2,1)S(1)} %get-tuple-element.78, bf16[4,2,32,128]{3,2,1,0:T(8,128)(2,1)S(1)} %get-tuple-element.78), branch_computations={%region_2.3_spmd, %region_3.4_spmd} | conditional | bytes 262152 | solution.py:343
  27.8 14.5 %all_to_all.4 = bf16[4,2,32,128]{3,2,1,0:T(8,128)(2,1)S(1)} all-to-all(bf16[4,2,32,128]{3,2,1,0:T(8,128)(2,1)S(1)} %copy.23), channel_id=1, replica_groups={{0,2,4,6},{1,3,5,7},{8,10,12,14},{9,11,13,15},{16,18,20,22},{17,19,21,2..., dimensions={0} | all-to-all | bytes 131072 | tf_op jit(solution)/shard_map/cond/branch_0_fun/all_to_all | solution.py:26
  42.3 0.0 collective-permute-done.5
  42.3 0.0 copy-done.2
  42.3 0.0 copy-start
  42.3 14.3 %conditional.5 = (f32[32,1024]{1,0:T(8,128)S(1)}, bf16[32,128]{1,0:T(8,128)(2,1)S(1)}, bf16[32,128]{1,0:T(8,128)(2,1)S(1)}) conditional(s32[]{:T(128)} %convert_element_type.2, (bf16[4,2,32,128]{3,2,1,0:T(8,128)(2,1)S(1)}, bf16[2,1824,128]{2,1,0:T(8,128)(2,1)S(1)}, bf16[3072,128]{1,0:T(8,128)(2,1)S(1)}, bf16[768,128]{1,0:T(8,128)(2,1)S(1)}, ...), branch_computations={%region_4.5_spmd, %region_5.6_spmd} | conditional | bytes 9535540 | solution.py:366
  42.3 0.0 copy-start.1
  42.4 0.4 two_levels.1
  42.8 7.9 %all-gather.4 = bf16[4,32,128]{2,1,0:T(8,128)(2,1)S(1)} all-gather(bf16[2,32,128]{2,1,0:T(8,128)(2,1)S(1)} %two_levels.1), channel_id=6, replica_groups={{0,8},{1,9},{2,10},{3,11},{4,12},{5,13},{6,14},{7,15},{16,24},{17,25},{..., dimensions={0}, use_global_device_ids=true | all-gather | bytes 49152 | tf_op jit(solution)/shard_map/cond/branch_0_fun/all_gather | solution.py:18
  50.7 0.1 level_7.1
  50.8 4.2 %all-gather.5 = bf16[4,32,128]{2,1,0:T(8,128)(2,1)S(1)} all-gather(bf16[2,32,128]{2,1,0:T(8,128)(2,1)S(1)} %level_7.1), channel_id=7, replica_groups={{0,16},{1,17},{2,18},{3,19},{4,20},{5,21},{6,22},{7,23},{8,24},{9,25},{..., dimensions={0}, use_global_device_ids=true | all-gather | bytes 49152 | tf_op jit(solution)/shard_map/cond/branch_0_fun/all_gather | solution.py:18
  55.0 0.1 level_8.1
  55.1 0.0 copy-done.1
  55.1 1.5 %near_1.1 = f32[32,1024]{1,0:T(8,128)S(1)} custom-call(bf16[3072,128]{1,0:T(8,128)(2,1)S(1)} %get-tuple-element.56.theirs.rest_0_.beside, bf16[2,1824,128]{2,1,0:T(8,128)(2,1)S(1)} %get-tuple-element.52.shared, bf16[9216,128]{1,0:T(8,128)(2,1)S(1)} %bitcast.42, s32[8,9]{1,0:T(8,128)S(1)} %get-tuple-element.58.rest_1_), custom_call_target="tpu_custom_call" | custom-call | tf_op jit(solution)/shard_map/cond/branch_0_fun/near_1/pallas_call | solution.py:257
  56.7 1.8 %all-gather.7 = bf16[64,128]{1,0:T(8,128)(2,1)S(1)} all-gather(bf16[32,128]{1,0:T(8,128)(2,1)S(1)} %get-tuple-element.82), channel_id=9, replica_groups={{0,32},{64,96},{128,160},{192,224},{256,288},{320,352},{384,416},{448,4..., dimensions={0}, use_global_device_ids=true | all-gather | bytes 24576 | tf_op jit(solution)/shard_map/all_gather | solution.py:18
  58.5 0.0 copy-done
  58.5 0.8 %respond.1 = f32[32,1,1,1024]{3,2,1,0:T(1,128)} custom-call(bf16[2,32,128]{2,1,0:T(8,128)(2,1)S(1)} %bitcast.41, bf16[32,128]{1,0:T(8,128)(2,1)S(1)} %get-tuple-element.83.own_final, f32[32,1024]{1,0:T(8,128)S(1)} %get-tuple-element.84.near, bf16[128,1024]{1,0:T(8,128)(2,1)S(1)} %bitcast.33), custom_call_target="tpu_custom_call" | custom-call | tf_op jit(solution)/shard_map/respond/pallas_call | solution.py:292
  (2 shorter events, 0.0 us)
Async XLA Ops:
  4.1 38.3 %copy-start.2 = (s32[1,1,8,9]{3,2,1,0:T(8,128)S(1)}, s32[1,1,8,9]{3,2,1,0:T(8,128)}, u32[]{:S(2)}) copy-start(s32[1,1,8,9]{3,2,1,0:T(8,128)} %param.14) | copy-start | bytes 868
  26.5 15.8 %collective-permute-start.5 = (bf16[3072,128]{1,0:T(8,128)(2,1)S(1)}, bf16[3072,128]{1,0:T(8,128)(2,1)S(1)}, u32[]{:S(2)}, u32[]{:S(2)}) collective-permute-start(bf16[3072,128]{1,0:T(8,128)(2,1)S(1)} %get-tuple-element.79), channel_id=1, source_target_pairs={{0,32},{64,96},{128,160},{192,224},{256,288},{320,352},{384,416},{... | collective-permute-start | bytes 2359304 | tf_op jit(solution)/shard_map/ppermute | solution.py:342
  42.3 16.1 %copy-start = (bf16[1,1,128,1024]{3,2,1,0:T(8,128)(2,1)S(1)}, bf16[1,1,128,1024]{3,2,1,0:T(8,128)(2,1)}, u32[]{:S(2)}) copy-start(bf16[1,1,128,1024]{3,2,1,0:T(8,128)(2,1)} %param.17) | copy-start | bytes 786436
  42.3 12.7 %copy-start.1 = (bf16[1,1,8,9,128,128]{5,4,3,2,1,0:T(8,128)(2,1)S(1)}, bf16[1,1,8,9,128,128]{5,4,3,2,1,0:T(8,128)(2,1)}, u32[]{:S(2)}) copy-start(bf16[1,1,8,9,128,128]{5,4,3,2,1,0:T(8,128)(2,1)} %get-tuple-element.57) | copy-start | bytes 7077892 | tf_op jit(solution)/shard_map/cond

commit v11 on v10

--- a/solution.py
+++ b/solution.py
@@ -47,13 +47,14 @@
 
 def surroundings(boxes, meanwhile):
     even = lax.axis_index("bx") >> 1 & 1 == 0
+    second = swapped(jnp.where(even, boxes[0], boxes[1]), "bx", 1)
     first = swapped(jnp.where(even, boxes[1], boxes[0]), "bx", 0)
-    second = swapped(jnp.where(even, boxes[0], boxes[1]), "bx", 1)
     before, after = jnp.where(even, second, first), jnp.where(even, first, second)
     row = jnp.concatenate([before[None], boxes, after[None]])
+    even = lax.axis_index("by") & 1 == 0
+    first = swapped(row, "by", 0)
     row, meanwhile = lax.optimization_barrier((row, meanwhile))
-    even = lax.axis_index("by") & 1 == 0
-    first, second = swapped(row, "by", 0), swapped(row, "by", 1)
+    second = swapped(row, "by", 1)
     return jnp.where(even, second, first), row, jnp.where(even, first, second), meanwhile
 
 

time: 59.6 us -> 57.7 us (0.968)
  the two profiles are of different devices: /device:TPU:7 before, /device:TPU:63 now
where the time goes in v11:
time: 57.7 us; the launch traced here: 57.4 us
  blocking collectives  43.8 us (76%)
  waiting for transfers between devices  7.24 us (13%)
  Pallas kernels  4.97 us (9%)
  starting transfers between devices  1.29 us (2%)
    all_gather x8, blocking collectives, pair_gather(): return lax.all_gather(values, axis, axis_index_groups=pairs)  34.1 us
    all_to_all x1, blocking collectives, four_exchange(): return lax.all_to_all(copies, axis, 0, 0, axis_index_groups=groups)  9.73 us
    ppermute x1, waiting for transfers between devices, per_device(): lax.ppermute(given, 'bx', [(i, i ^ 1) for i in range(0, lax.axis_size('bx...  7.24 us
    pallas_call x1, Pallas kernels, near_of(): pl.pallas_call(functools.partial(near_field, packing, offset), name=f'nea...  1.54 us
    pallas_call x8, Pallas kernels, in_vmem(): call(*(pltpu.with_memory_space_constraint(x, pltpu.VMEM) for x in operands))  1.31 us
    ppermute x1, starting transfers between devices, per_device(): lax.ppermute(given, 'bx', [(i, i ^ 1) for i in range(0, lax.axis_size('bx...  1.29 us
    pallas_call x1, Pallas kernels, packed_own(): pl.pallas_call(functools.partial(pack, packing), name='pack', compiler_pa...  1.28 us
  transfers between devices with their start and end apart: 1, of which 1 were waited for; matrix products, arithmetic and copies ran while one was open for 0% of the time, Pallas kernels for 0%

profile of v11, /device:TPU:63, one launch (start us, length us, event | category | flops | bytes accessed | tf_op | source)
XLA Modules:
  0.0 57.4 jit_solution(2143507149577813128)
XLA Ops:
  0.0 1.3 %pack.1 = (bf16[1824,128]{1,0:T(8,128)(2,1)S(1)}, bf16[768,128]{1,0:T(8,128)(2,1)S(1)}) custom-call(bf16[2304,128]{1,0:T(8,128)(2,1)} %bitcast.45, bf16[32,1024]{1,0:T(8,128)(2,1)} %bitcast.49, bf16[1024,128]{1,0:T(8,128)(2,1)} %bitcast.47), custom_call_target="tpu_custom_call" | custom-call | tf_op jit(solution)/shard_map/pack/pallas_call | solution.py:119
  1.3 2.8 %all-gather.6 = bf16[3648,128]{1,0:T(8,128)(2,1)S(1)} all-gather(bf16[1824,128]{1,0:T(8,128)(2,1)S(1)} %get-tuple-element.76), channel_id=8, replica_groups={{0,32},{64,96},{128,160},{192,224},{256,288},{320,352},{384,416},{448,4..., dimensions={0}, use_global_device_ids=true | all-gather | bytes 1400832 | tf_op jit(solution)/shard_map/all_gather | solution.py:18
  4.1 0.0 copy-start.2
  4.1 22.6 %conditional.3 = (bf16[4,2,32,128]{3,2,1,0:T(8,128)(2,1)S(1)}, bf16[3072,128]{1,0:T(8,128)(2,1)S(1)}, bf16[768,128]{1,0:T(8,128)(2,1)S(1)}, bf16[4,2,32,128]{3,2,1,0:T(8,128)(2,1)S(1)}) conditional(s32[]{:T(128)} %convert_element_type.2, bf16[2,1824,128]{2,1,0:T(8,128)(2,1)S(1)} %bitcast.29, (bf16[2,1824,128]{2,1,0:T(8,128)(2,1)S(1)}, ...), branch_computations={%region_0.0_spmd, %region_1.2_spmd} | conditional | flops 3670026 | bytes 10092889 | solution.py:342
  4.1 0.1 level_0.1
  4.2 3.3 %all-gather = bf16[4,32,128]{2,1,0:T(8,128)(2,1)S(1)} all-gather(bf16[2,32,128]{2,1,0:T(8,128)(2,1)S(1)} %level_0.1), channel_id=2, replica_groups={{0,64},{32,96},{128,192},{160,224},{256,320},{288,352},{384,448},{416,4..., dimensions={0}, use_global_device_ids=true | all-gather | bytes 49152 | tf_op jit(solution)/shard_map/cond/branch_0_fun/all_gather | solution.py:18
  7.4 0.1 level_1.1
  7.6 4.8 %all-gather.1 = bf16[4,32,128]{2,1,0:T(8,128)(2,1)S(1)} all-gather(bf16[2,32,128]{2,1,0:T(8,128)(2,1)S(1)} %level_1.1), channel_id=3, replica_groups={{0,128},{32,160},{64,192},{96,224},{256,384},{288,416},{320,448},{352,4..., dimensions={0}, use_global_device_ids=true | all-gather | bytes 49152 | tf_op jit(solution)/shard_map/cond/branch_0_fun/all_gather | solution.py:18
  12.3 0.1 level_2.1
  12.5 10.5 %all-gather.2 = bf16[4,32,128]{2,1,0:T(8,128)(2,1)S(1)} all-gather(bf16[2,32,128]{2,1,0:T(8,128)(2,1)S(1)} %level_2.1), channel_id=4, replica_groups={{0,256},{32,288},{64,320},{96,352},{128,384},{160,416},{192,448},{224,4..., dimensions={0}, use_global_device_ids=true | all-gather | bytes 49152 | tf_op jit(solution)/shard_map/cond/branch_0_fun/all_gather | solution.py:18
  23.0 0.1 level_3.1
  23.1 3.4 %all-gather.3 = bf16[4,32,128]{2,1,0:T(8,128)(2,1)S(1)} all-gather(bf16[2,32,128]{2,1,0:T(8,128)(2,1)S(1)} %level_3.1), channel_id=5, replica_groups={{0,1},{2,3},{4,5},{6,7},{8,9},{10,11},{12,13},{14,15},{16,17},{18,19},{..., dimensions={0}, use_global_device_ids=true | all-gather | bytes 49152 | tf_op jit(solution)/shard_map/cond/branch_0_fun/all_gather | solution.py:18
  26.5 0.1 level_4.1
  26.7 1.3 %collective-permute-start.5 = (bf16[3072,128]{1,0:T(8,128)(2,1)S(1)}, bf16[3072,128]{1,0:T(8,128)(2,1)S(1)}, u32[]{:S(2)}, u32[]{:S(2)}) collective-permute-start(bf16[3072,128]{1,0:T(8,128)(2,1)S(1)} %get-tuple-element.79), channel_id=1, source_target_pairs={{0,32},{64,96},{128,160},{192,224},{256,288},{320,352},{384,416},{... | collective-permute-start | bytes 2359304 | tf_op jit(solution)/shard_map/ppermute | solution.py:343
  28.0 9.8 %conditional.4 = (bf16[4,2,32,128]{3,2,1,0:T(8,128)(2,1)S(1)}) conditional(s32[]{:T(128)} %convert_element_type.2, bf16[4,2,32,128]{3,2,1,0:T(8,128)(2,1)S(1)} %get-tuple-element.78, bf16[4,2,32,128]{3,2,1,0:T(8,128)(2,1)S(1)} %get-tuple-element.78), branch_computations={%region_2.3_spmd, %region_3.4_spmd} | conditional | bytes 262152 | solution.py:344
  28.0 9.7 %all_to_all.4 = bf16[4,2,32,128]{3,2,1,0:T(8,128)(2,1)S(1)} all-to-all(bf16[4,2,32,128]{3,2,1,0:T(8,128)(2,1)S(1)} %copy.23), channel_id=1, replica_groups={{0,2,4,6},{1,3,5,7},{8,10,12,14},{9,11,13,15},{16,18,20,22},{17,19,21,2..., dimensions={0} | all-to-all | bytes 131072 | tf_op jit(solution)/shard_map/cond/branch_0_fun/all_to_all | solution.py:26
  37.7 7.2 %collective-permute-done.5 = bf16[3072,128]{1,0:T(8,128)(2,1)S(1)} collective-permute-done((bf16[3072,128]{1,0:T(8,128)(2,1)S(1)}, bf16[3072,128]{1,0:T(8,128)(2,1)S(1)}, u32[]{:S(2)}, u32[]{:S(2)}) %collective-permute-start.5) | collective-permute-done | bytes 786464 | tf_op jit(solution)/shard_map/ppermute | solution.py:343
  45.0 0.0 copy-done.2
  45.0 0.0 copy-start
  45.0 9.8 %conditional.5 = (f32[32,1024]{1,0:T(8,128)S(1)}, bf16[32,128]{1,0:T(8,128)(2,1)S(1)}, bf16[32,128]{1,0:T(8,128)(2,1)S(1)}) conditional(s32[]{:T(128)} %convert_element_type.2, (bf16[4,2,32,128]{3,2,1,0:T(8,128)(2,1)S(1)}, bf16[2,1824,128]{2,1,0:T(8,128)(2,1)S(1)}, bf16[3072,128]{1,0:T(8,128)(2,1)S(1)}, bf16[768,128]{1,0:T(8,128)(2,1)S(1)}, ...), branch_computations={%region_4.5_spmd, %region_5.6_spmd} | conditional | bytes 9535540 | solution.py:367
  45.0 0.0 copy-start.1
  45.0 0.4 two_levels.1
  45.4 3.4 %all-gather.4 = bf16[4,32,128]{2,1,0:T(8,128)(2,1)S(1)} all-gather(bf16[2,32,128]{2,1,0:T(8,128)(2,1)S(1)} %two_levels.1), channel_id=6, replica_groups={{0,8},{1,9},{2,10},{3,11},{4,12},{5,13},{6,14},{7,15},{16,24},{17,25},{..., dimensions={0}, use_global_device_ids=true | all-gather | bytes 49152 | tf_op jit(solution)/shard_map/cond/branch_0_fun/all_gather | solution.py:18
  48.8 0.1 level_7.1
  48.9 4.2 %all-gather.5 = bf16[4,32,128]{2,1,0:T(8,128)(2,1)S(1)} all-gather(bf16[2,32,128]{2,1,0:T(8,128)(2,1)S(1)} %level_7.1), channel_id=7, replica_groups={{0,16},{1,17},{2,18},{3,19},{4,20},{5,21},{6,22},{7,23},{8,24},{9,25},{..., dimensions={0}, use_global_device_ids=true | all-gather | bytes 49152 | tf_op jit(solution)/shard_map/cond/branch_0_fun/all_gather | solution.py:18
  53.1 0.1 level_8.1
  53.2 0.0 copy-done.1
  53.2 1.5 %near_1.1 = f32[32,1024]{1,0:T(8,128)S(1)} custom-call(bf16[3072,128]{1,0:T(8,128)(2,1)S(1)} %get-tuple-element.56.theirs.rest_0_.beside, bf16[2,1824,128]{2,1,0:T(8,128)(2,1)S(1)} %get-tuple-element.52.shared, bf16[9216,128]{1,0:T(8,128)(2,1)S(1)} %bitcast.42, s32[8,9]{1,0:T(8,128)S(1)} %get-tuple-element.58.rest_1_), custom_call_target="tpu_custom_call" | custom-call | tf_op jit(solution)/shard_map/cond/branch_0_fun/near_1/pallas_call | solution.py:258
  54.8 1.8 %all-gather.7 = bf16[64,128]{1,0:T(8,128)(2,1)S(1)} all-gather(bf16[32,128]{1,0:T(8,128)(2,1)S(1)} %get-tuple-element.82), channel_id=9, replica_groups={{0,32},{64,96},{128,160},{192,224},{256,288},{320,352},{384,416},{448,4..., dimensions={0}, use_global_device_ids=true | all-gather | bytes 24576 | tf_op jit(solution)/shard_map/all_gather | solution.py:18
  56.6 0.0 copy-done
  56.6 0.8 %respond.1 = f32[32,1,1,1024]{3,2,1,0:T(1,128)} custom-call(bf16[2,32,128]{2,1,0:T(8,128)(2,1)S(1)} %bitcast.41, bf16[32,128]{1,0:T(8,128)(2,1)S(1)} %get-tuple-element.83.own_final, f32[32,1024]{1,0:T(8,128)S(1)} %get-tuple-element.84.near, bf16[128,1024]{1,0:T(8,128)(2,1)S(1)} %bitcast.33), custom_call_target="tpu_custom_call" | custom-call | tf_op jit(solution)/shard_map/respond/pallas_call | solution.py:293
  (2 shorter events, 0.0 us)
Async XLA Ops:
  4.1 40.9 %copy-start.2 = (s32[1,1,8,9]{3,2,1,0:T(8,128)S(1)}, s32[1,1,8,9]{3,2,1,0:T(8,128)}, u32[]{:S(2)}) copy-start(s32[1,1,8,9]{3,2,1,0:T(8,128)} %param.14) | copy-start | bytes 868
  26.7 18.3 %collective-permute-start.5 = (bf16[3072,128]{1,0:T(8,128)(2,1)S(1)}, bf16[3072,128]{1,0:T(8,128)(2,1)S(1)}, u32[]{:S(2)}, u32[]{:S(2)}) collective-permute-start(bf16[3072,128]{1,0:T(8,128)(2,1)S(1)} %get-tuple-element.79), channel_id=1, source_target_pairs={{0,32},{64,96},{128,160},{192,224},{256,288},{320,352},{384,416},{... | collective-permute-start | bytes 2359304 | tf_op jit(solution)/shard_map/ppermute | solution.py:343
  45.0 11.6 %copy-start = (bf16[1,1,128,1024]{3,2,1,0:T(8,128)(2,1)S(1)}, bf16[1,1,128,1024]{3,2,1,0:T(8,128)(2,1)}, u32[]{:S(2)}) copy-start(bf16[1,1,128,1024]{3,2,1,0:T(8,128)(2,1)} %param.17) | copy-start | bytes 786436
  45.0 8.2 %copy-start.1 = (bf16[1,1,8,9,128,128]{5,4,3,2,1,0:T(8,128)(2,1)S(1)}, bf16[1,1,8,9,128,128]{5,4,3,2,1,0:T(8,128)(2,1)}, u32[]{:S(2)}) copy-start(bf16[1,1,8,9,128,128]{5,4,3,2,1,0:T(8,128)(2,1)} %get-tuple-element.57) | copy-start | bytes 7077892 | tf_op jit(solution)/shard_map/cond

commit v12 on v11

--- a/solution.py
+++ b/solution.py
@@ -6,6 +6,7 @@
 from jax.experimental import pallas as pl
 from jax.experimental.pallas import tpu as pltpu
 from jax.sharding import PartitionSpec as P
+
 
 BOTH = ("bx", "by")
 LANES = 128
@@ -203,11 +204,10 @@
     given[...], final[...] = mixed(packing, level, place, both, (theirs, own))
 
 
-def in_vmem(kernel, name, out_shape, operands):
+def in_vmem(kernel, out_shape, operands):
     vmem = pl.BlockSpec(memory_space=pltpu.VMEM)
     call = pl.pallas_call(
         kernel,
-        name=name,
         compiler_params=GRANT,
         out_shape=out_shape,
         in_specs=[vmem] * len(operands),
@@ -257,7 +257,6 @@
     operands += [near_blocks.reshape(-1, near_blocks.shape[3]), near_index]
     return pl.pallas_call(
         functools.partial(near_field, packing, offset),
-        name=f"near_{offset}",
         compiler_params=GRANT,
         out_shape=pltpu.VMEM((packing.excite, packing.blocks * LANES), jnp.float32),
         in_specs=[vmem] * len(operands),
@@ -329,14 +328,14 @@
         return jnp.zeros((4, 2, excite, rank), jnp.bfloat16), given, column
 
     def levels_early():
-        coeffs = in_vmem(functools.partial(first_level, packing), "level_0", coeffs_shape, (shared,))
+        coeffs = in_vmem(functools.partial(first_level, packing), coeffs_shape, (shared,))
         for level in range(1, merged):
             kernel, shape = next_level, coeffs_shape
             if level == merged - 1:
                 kernel, shape = spread_level, (four_shape, given_shape, column_shape)
             both = pair_gather(coeffs, *levels[level])
             kernel = functools.partial(kernel, packing, level, levels[level])
-            coeffs = in_vmem(kernel, f"level_{level}", shape, (both, shared))
+            coeffs = in_vmem(kernel, shape, (both, shared))
         return tuple(coeffs)
 
     copies, given, column = lax.cond(first_of_pair, gathering, levels_early)
@@ -351,7 +350,7 @@
 
     def levels_late():
         kernel = functools.partial(two_levels, packing, merged, levels[merged])
-        result = in_vmem(kernel, "two_levels", coeffs_shape, (four, shared, handed, later))
+        result = in_vmem(kernel, coeffs_shape, (four, shared, handed, later))
         for level in range(merged + 2, len(levels)):
             kernel = functools.partial(next_level, packing, level, levels[level])
             shape = coeffs_shape
@@ -359,7 +358,7 @@
                 kernel = functools.partial(last_level, packing, level, levels[level])
                 shape = (pltpu.VMEM((excite, rank), jnp.bfloat16),) * 2
             both = pair_gather(result, *levels[level])
-            result = in_vmem(kernel, f"level_{level}", shape, (both, handed, later))
+            result = in_vmem(kernel, shape, (both, handed, later))
         beside, result = lax.optimization_barrier((handed, tuple(result)))
         near = near_of(packing, 1, beside, shared, (), own_blocks, own_index)
         return near, *result

time: 57.7 us -> 57.7 us (level)
  no operation moved by 1% of the time
where the time goes in v12:
time: 57.7 us; the launch traced here: 57.4 us
  blocking collectives  43.8 us (76%)
  waiting for transfers between devices  7.24 us (13%)
  Pallas kernels  4.97 us (9%)
  starting transfers between devices  1.29 us (2%)
    all_gather x8, blocking collectives, pair_gather(): return lax.all_gather(values, axis, axis_index_groups=pairs)  34.1 us
    all_to_all x1, blocking collectives, four_exchange(): return lax.all_to_all(copies, axis, 0, 0, axis_index_groups=groups)  9.73 us
    ppermute x1, waiting for transfers between devices, per_device(): lax.ppermute(given, 'bx', [(i, i ^ 1) for i in range(0, lax.axis_size('bx...  7.24 us
    pallas_call x1, Pallas kernels, near_of(): pl.pallas_call(functools.partial(near_field, packing, offset), compiler_p...  1.54 us
    pallas_call x8, Pallas kernels, in_vmem(): call(*(pltpu.with_memory_space_constraint(x, pltpu.VMEM) for x in operands))  1.31 us
    ppermute x1, starting transfers between devices, per_device(): lax.ppermute(given, 'bx', [(i, i ^ 1) for i in range(0, lax.axis_size('bx...  1.29 us
    pallas_call x1, Pallas kernels, packed_own(): pl.pallas_call(functools.partial(pack, packing), name='pack', compiler_pa...  1.28 us
  transfers between devices with their start and end apart: 1, of which 1 were waited for; matrix products, arithmetic and copies ran while one was open for 0% of the time, Pallas kernels for 0%

profile of v12, /device:TPU:63, one launch (start us, length us, event | category | flops | bytes accessed | tf_op | source)
XLA Modules:
  0.0 57.4 jit_solution(2143507149577813128)
XLA Ops:
  0.0 1.3 %pack.1 = (bf16[1824,128]{1,0:T(8,128)(2,1)S(1)}, bf16[768,128]{1,0:T(8,128)(2,1)S(1)}) custom-call(bf16[2304,128]{1,0:T(8,128)(2,1)} %bitcast.45, bf16[32,1024]{1,0:T(8,128)(2,1)} %bitcast.49, bf16[1024,128]{1,0:T(8,128)(2,1)} %bitcast.47), custom_call_target="tpu_custom_call" | custom-call | tf_op jit(solution)/shard_map/pack/pallas_call | solution.py:120
  1.3 2.8 %all-gather.6 = bf16[3648,128]{1,0:T(8,128)(2,1)S(1)} all-gather(bf16[1824,128]{1,0:T(8,128)(2,1)S(1)} %get-tuple-element.76), channel_id=8, replica_groups={{0,32},{64,96},{128,160},{192,224},{256,288},{320,352},{384,416},{448,4..., dimensions={0}, use_global_device_ids=true | all-gather | bytes 1400832 | tf_op jit(solution)/shard_map/all_gather | solution.py:19
  4.1 0.0 copy-start.2
  4.1 22.6 %conditional.3 = (bf16[4,2,32,128]{3,2,1,0:T(8,128)(2,1)S(1)}, bf16[3072,128]{1,0:T(8,128)(2,1)S(1)}, bf16[768,128]{1,0:T(8,128)(2,1)S(1)}, bf16[4,2,32,128]{3,2,1,0:T(8,128)(2,1)S(1)}) conditional(s32[]{:T(128)} %convert_element_type.2, bf16[2,1824,128]{2,1,0:T(8,128)(2,1)S(1)} %bitcast.29, (bf16[2,1824,128]{2,1,0:T(8,128)(2,1)S(1)}, ...), branch_computations={%region_0.0_spmd, %region_1.2_spmd} | conditional | flops 3670026 | bytes 10092889 | solution.py:341
  4.1 0.1 branch_0_fun.9
  4.2 3.3 %all-gather = bf16[4,32,128]{2,1,0:T(8,128)(2,1)S(1)} all-gather(bf16[2,32,128]{2,1,0:T(8,128)(2,1)S(1)} %branch_0_fun.9), channel_id=2, replica_groups={{0,64},{32,96},{128,192},{160,224},{256,320},{288,352},{384,448},{416,4..., dimensions={0}, use_global_device_ids=true | all-gather | bytes 49152 | tf_op jit(solution)/shard_map/cond/branch_0_fun/all_gather | solution.py:19
  7.4 0.1 branch_0_fun.10
  7.6 4.8 %all-gather.1 = bf16[4,32,128]{2,1,0:T(8,128)(2,1)S(1)} all-gather(bf16[2,32,128]{2,1,0:T(8,128)(2,1)S(1)} %branch_0_fun.10), channel_id=3, replica_groups={{0,128},{32,160},{64,192},{96,224},{256,384},{288,416},{320,448},{352,4..., dimensions={0}, use_global_device_ids=true | all-gather | bytes 49152 | tf_op jit(solution)/shard_map/cond/branch_0_fun/all_gather | solution.py:19
  12.3 0.1 branch_0_fun.11
  12.5 10.5 %all-gather.2 = bf16[4,32,128]{2,1,0:T(8,128)(2,1)S(1)} all-gather(bf16[2,32,128]{2,1,0:T(8,128)(2,1)S(1)} %branch_0_fun.11), channel_id=4, replica_groups={{0,256},{32,288},{64,320},{96,352},{128,384},{160,416},{192,448},{224,4..., dimensions={0}, use_global_device_ids=true | all-gather | bytes 49152 | tf_op jit(solution)/shard_map/cond/branch_0_fun/all_gather | solution.py:19
  23.0 0.1 branch_0_fun.12
  23.1 3.4 %all-gather.3 = bf16[4,32,128]{2,1,0:T(8,128)(2,1)S(1)} all-gather(bf16[2,32,128]{2,1,0:T(8,128)(2,1)S(1)} %branch_0_fun.12), channel_id=5, replica_groups={{0,1},{2,3},{4,5},{6,7},{8,9},{10,11},{12,13},{14,15},{16,17},{18,19},{..., dimensions={0}, use_global_device_ids=true | all-gather | bytes 49152 | tf_op jit(solution)/shard_map/cond/branch_0_fun/all_gather | solution.py:19
  26.5 0.1 branch_0_fun.13
  26.7 1.3 %collective-permute-start.5 = (bf16[3072,128]{1,0:T(8,128)(2,1)S(1)}, bf16[3072,128]{1,0:T(8,128)(2,1)S(1)}, u32[]{:S(2)}, u32[]{:S(2)}) collective-permute-start(bf16[3072,128]{1,0:T(8,128)(2,1)S(1)} %get-tuple-element.79), channel_id=1, source_target_pairs={{0,32},{64,96},{128,160},{192,224},{256,288},{320,352},{384,416},{... | collective-permute-start | bytes 2359304 | tf_op jit(solution)/shard_map/ppermute | solution.py:342
  28.0 9.8 %conditional.4 = (bf16[4,2,32,128]{3,2,1,0:T(8,128)(2,1)S(1)}) conditional(s32[]{:T(128)} %convert_element_type.2, bf16[4,2,32,128]{3,2,1,0:T(8,128)(2,1)S(1)} %get-tuple-element.78, bf16[4,2,32,128]{3,2,1,0:T(8,128)(2,1)S(1)} %get-tuple-element.78), branch_computations={%region_2.3_spmd, %region_3.4_spmd} | conditional | bytes 262152 | solution.py:343
  28.0 9.7 %all_to_all.4 = bf16[4,2,32,128]{3,2,1,0:T(8,128)(2,1)S(1)} all-to-all(bf16[4,2,32,128]{3,2,1,0:T(8,128)(2,1)S(1)} %copy.23), channel_id=1, replica_groups={{0,2,4,6},{1,3,5,7},{8,10,12,14},{9,11,13,15},{16,18,20,22},{17,19,21,2..., dimensions={0} | all-to-all | bytes 131072 | tf_op jit(solution)/shard_map/cond/branch_0_fun/all_to_all | solution.py:27
  37.7 7.2 %collective-permute-done.5 = bf16[3072,128]{1,0:T(8,128)(2,1)S(1)} collective-permute-done((bf16[3072,128]{1,0:T(8,128)(2,1)S(1)}, bf16[3072,128]{1,0:T(8,128)(2,1)S(1)}, u32[]{:S(2)}, u32[]{:S(2)}) %collective-permute-start.5) | collective-permute-done | bytes 786464 | tf_op jit(solution)/shard_map/ppermute | solution.py:342
  45.0 0.0 copy-done.2
  45.0 0.0 copy-start
  45.0 9.8 %conditional.5 = (f32[32,1024]{1,0:T(8,128)S(1)}, bf16[32,128]{1,0:T(8,128)(2,1)S(1)}, bf16[32,128]{1,0:T(8,128)(2,1)S(1)}) conditional(s32[]{:T(128)} %convert_element_type.2, (bf16[4,2,32,128]{3,2,1,0:T(8,128)(2,1)S(1)}, bf16[2,1824,128]{2,1,0:T(8,128)(2,1)S(1)}, bf16[3072,128]{1,0:T(8,128)(2,1)S(1)}, bf16[768,128]{1,0:T(8,128)(2,1)S(1)}, ...), branch_computations={%region_4.5_spmd, %region_5.6_spmd} | conditional | bytes 9535540 | solution.py:366
  45.0 0.0 copy-start.1
  45.0 0.4 branch_0_fun.14
  45.4 3.4 %all-gather.4 = bf16[4,32,128]{2,1,0:T(8,128)(2,1)S(1)} all-gather(bf16[2,32,128]{2,1,0:T(8,128)(2,1)S(1)} %branch_0_fun.14), channel_id=6, replica_groups={{0,8},{1,9},{2,10},{3,11},{4,12},{5,13},{6,14},{7,15},{16,24},{17,25},{..., dimensions={0}, use_global_device_ids=true | all-gather | bytes 49152 | tf_op jit(solution)/shard_map/cond/branch_0_fun/all_gather | solution.py:19
  48.8 0.1 branch_0_fun.15
  48.9 4.2 %all-gather.5 = bf16[4,32,128]{2,1,0:T(8,128)(2,1)S(1)} all-gather(bf16[2,32,128]{2,1,0:T(8,128)(2,1)S(1)} %branch_0_fun.15), channel_id=7, replica_groups={{0,16},{1,17},{2,18},{3,19},{4,20},{5,21},{6,22},{7,23},{8,24},{9,25},{..., dimensions={0}, use_global_device_ids=true | all-gather | bytes 49152 | tf_op jit(solution)/shard_map/cond/branch_0_fun/all_gather | solution.py:19
  53.1 0.1 branch_0_fun.16
  53.2 0.0 copy-done.1
  53.2 1.5 %branch_0_fun.17 = f32[32,1024]{1,0:T(8,128)S(1)} custom-call(bf16[3072,128]{1,0:T(8,128)(2,1)S(1)} %get-tuple-element.56.theirs.rest_0_.beside, bf16[2,1824,128]{2,1,0:T(8,128)(2,1)S(1)} %get-tuple-element.52.shared, bf16[9216,128]{1,0:T(8,128)(2,1)S(1)} %bitcast.42, s32[8,9]{1,0:T(8,128)S(1)} %get-tuple-element.58.rest_1_), custom_call_target="tpu_custom_call" | custom-call | tf_op jit(solution)/shard_map/cond/branch_0_fun/pallas_call | solution.py:258
  54.8 1.8 %all-gather.7 = bf16[64,128]{1,0:T(8,128)(2,1)S(1)} all-gather(bf16[32,128]{1,0:T(8,128)(2,1)S(1)} %get-tuple-element.82), channel_id=9, replica_groups={{0,32},{64,96},{128,160},{192,224},{256,288},{320,352},{384,416},{448,4..., dimensions={0}, use_global_device_ids=true | all-gather | bytes 24576 | tf_op jit(solution)/shard_map/all_gather | solution.py:19
  56.6 0.0 copy-done
  56.6 0.8 %respond.1 = f32[32,1,1,1024]{3,2,1,0:T(1,128)} custom-call(bf16[2,32,128]{2,1,0:T(8,128)(2,1)S(1)} %bitcast.41, bf16[32,128]{1,0:T(8,128)(2,1)S(1)} %get-tuple-element.83.own_final, f32[32,1024]{1,0:T(8,128)S(1)} %get-tuple-element.84.near, bf16[128,1024]{1,0:T(8,128)(2,1)S(1)} %bitcast.33), custom_call_target="tpu_custom_call" | custom-call | tf_op jit(solution)/shard_map/respond/pallas_call | solution.py:292
  (2 shorter events, 0.0 us)
Async XLA Ops:
  4.1 40.9 %copy-start.2 = (s32[1,1,8,9]{3,2,1,0:T(8,128)S(1)}, s32[1,1,8,9]{3,2,1,0:T(8,128)}, u32[]{:S(2)}) copy-start(s32[1,1,8,9]{3,2,1,0:T(8,128)} %param.14) | copy-start | bytes 868
  26.7 18.3 %collective-permute-start.5 = (bf16[3072,128]{1,0:T(8,128)(2,1)S(1)}, bf16[3072,128]{1,0:T(8,128)(2,1)S(1)}, u32[]{:S(2)}, u32[]{:S(2)}) collective-permute-start(bf16[3072,128]{1,0:T(8,128)(2,1)S(1)} %get-tuple-element.79), channel_id=1, source_target_pairs={{0,32},{64,96},{128,160},{192,224},{256,288},{320,352},{384,416},{... | collective-permute-start | bytes 2359304 | tf_op jit(solution)/shard_map/ppermute | solution.py:342
  45.0 11.6 %copy-start = (bf16[1,1,128,1024]{3,2,1,0:T(8,128)(2,1)S(1)}, bf16[1,1,128,1024]{3,2,1,0:T(8,128)(2,1)}, u32[]{:S(2)}) copy-start(bf16[1,1,128,1024]{3,2,1,0:T(8,128)(2,1)} %param.17) | copy-start | bytes 786436
  45.0 8.2 %copy-start.1 = (bf16[1,1,8,9,128,128]{5,4,3,2,1,0:T(8,128)(2,1)S(1)}, bf16[1,1,8,9,128,128]{5,4,3,2,1,0:T(8,128)(2,1)}, u32[]{:S(2)}) copy-start(bf16[1,1,8,9,128,128]{5,4,3,2,1,0:T(8,128)(2,1)} %get-tuple-element.57) | copy-start | bytes 7077892 | tf_op jit(solution)/shard_map/cond

commit v13 on v8

--- a/solution.py
+++ b/solution.py
@@ -16,6 +16,12 @@
     count = lax.axis_size(axis)
     pairs = [[i, i ^ 1 << apart] for i in range(count) if not i >> apart & 1]
     return lax.all_gather(values, axis, axis_index_groups=pairs)
+
+
+def partners_of(values, apart):
+    count_x, count_y = lax.axis_size("bx"), lax.axis_size("by")
+    at = [x * count_y + y for x in range(1, count_x, 2) for y in range(count_y)]
+    return lax.ppermute(values, BOTH, [(i, i ^ 1 << apart) for i in at])
 
 
 def swapped(values, axis, phase):
@@ -151,8 +157,12 @@
         coeffs[box] = value
 
 
-def last_level(packing, level, place, both, theirs, own, given, final):
-    given[...], final[...] = mixed(packing, level, place, both, (theirs, own))
+def last_level(packing, level, place, coeffs, others, theirs, own, given, final):
+    starts = [packing.late + packing.place_of(level), packing.place_of(level)]
+    for box, (ref, out) in enumerate(((theirs, given), (own, final))):
+        pair = jnp.concatenate([coeffs[box], others[box]], axis=1)
+        weights = ref[pl.ds(starts[box], packing.level_rows)]
+        out[...] = jnp.dot(pair, weights, preferred_element_type=jnp.float32).astype(out.dtype)
 
 
 def in_vmem(kernel, name, out_shape, operands):
@@ -298,19 +308,19 @@
         return near, coeffs[0], coeffs[1]
 
     def levels_late():
-        gathered = both
-        for level in range(packing.split, len(levels)):
+        gathered, last = both, len(levels) - 1
+        for level in range(packing.split, last):
             kernel = functools.partial(next_level, packing, level, levels[level])
-            shape = coeffs_shape
-            if level == len(levels) - 1:
-                kernel = functools.partial(last_level, packing, level, levels[level])
-                shape = (pltpu.VMEM((excite, rank), jnp.bfloat16),) * 2
-            result = in_vmem(kernel, f"level_{level}", shape, (gathered, handed, later))
-            if level < len(levels) - 1:
+            result = in_vmem(kernel, f"level_{level}", coeffs_shape, (gathered, handed, later))
+            if level < last - 1:
                 gathered = pair_gather(result, *levels[level + 1])
-        beside, result = lax.optimization_barrier((handed, tuple(result)))
+        others = partners_of(result, levels[last][1])
+        beside, result = lax.optimization_barrier((handed, result))
         near = near_of(packing, 1, beside, shared, (), own_blocks, own_index)
-        return near, *result
+        near, others = lax.optimization_barrier((near, others))
+        kernel = functools.partial(last_level, packing, last, levels[last])
+        shape = (pltpu.VMEM((excite, rank), jnp.bfloat16),) * 2
+        return near, *in_vmem(kernel, f"level_{last}", shape, (result, others, handed, later))
 
     near, final_given, final = lax.cond(first_of_pair, near_only, levels_late)
     taken = pair_gather(final_given, "bx", 0)

time: 54.6 us -> 54.5 us (level)
  blocking collectives: 48 us -> 43.7 us
  starting transfers between devices: 1.29 us -> 3.64 us
  Pallas kernels: 4.85 us -> 6.51 us
    all_gather x10 -> x9, blocking collectives: 48 us -> 43.7 us  [pair_gather(): return lax.all_gather(values, axis, axis_index_groups=pairs)]
    ppermute x0 -> x1, starting transfers between devices: none -> 2.35 us  [partners_of(): return lax.ppermute(values, BOTH, [(i, i ^ 1 << apart) for i in at])]
    pallas_call x1, Pallas kernels: 1.54 us -> 3.2 us  [near_of(): pl.pallas_call(functools.partial(near_field, packing, offset), name=f'nea...]
  transfers between devices with their start and end apart: 1 -> 2, of which waited for: 0 -> 0; matrix products, arithmetic and copies ran while one was open for 0% -> 0% of each run, Pallas kernels for 0% -> 6%
where the time goes in v13:
time: 54.5 us; the launch traced here: 54 us
  blocking collectives  43.7 us (80%)
  Pallas kernels  6.51 us (12%)
  starting transfers between devices  3.64 us (7%)
    all_gather x9, blocking collectives, pair_gather(): return lax.all_gather(values, axis, axis_index_groups=pairs)  43.7 us
    pallas_call x1, Pallas kernels, near_of(): pl.pallas_call(functools.partial(near_field, packing, offset), name=f'nea...  3.2 us
    ppermute x1, starting transfers between devices, partners_of(): return lax.ppermute(values, BOTH, [(i, i ^ 1 << apart) for i in at])  2.35 us
    ppermute x1, starting transfers between devices, per_device(): lax.ppermute(given, 'bx', [(i, i ^ 1) for i in range(0, lax.axis_size('bx...  1.29 us
    pallas_call x1, Pallas kernels, packed_own(): pl.pallas_call(functools.partial(pack, packing), name='pack', compiler_pa...  1.28 us
    pallas_call x9, Pallas kernels, in_vmem(): call(*(pltpu.with_memory_space_constraint(x, pltpu.VMEM) for x in operands))  1.18 us
  transfers between devices with their start and end apart: 2, of which 0 were waited for; matrix products, arithmetic and copies ran while one was open for 0% of the time, Pallas kernels for 6%

profile of v13, /device:TPU:1, one launch (start us, length us, event | category | flops | bytes accessed | tf_op | source)
XLA Modules:
  0.0 54.0 jit_solution(15965018115786630869)
XLA Ops:
  0.0 1.3 %pack.1 = (bf16[1824,128]{1,0:T(8,128)(2,1)S(1)}, bf16[768,128]{1,0:T(8,128)(2,1)S(1)}) custom-call(bf16[2304,128]{1,0:T(8,128)(2,1)} %bitcast.47, bf16[32,1024]{1,0:T(8,128)(2,1)} %bitcast.51, bf16[1024,128]{1,0:T(8,128)(2,1)} %bitcast.49), custom_call_target="tpu_custom_call" | custom-call | tf_op jit(solution)/shard_map/pack/pallas_call | solution.py:108
  1.3 8.9 %all-gather.7 = bf16[3648,128]{1,0:T(8,128)(2,1)S(1)} all-gather(bf16[1824,128]{1,0:T(8,128)(2,1)S(1)} %get-tuple-element.75), channel_id=9, replica_groups={{0,32},{64,96},{128,160},{192,224},{256,288},{320,352},{384,416},{448,4..., dimensions={0}, use_global_device_ids=true | all-gather | bytes 1400832 | tf_op jit(solution)/shard_map/all_gather | solution.py:18
  10.2 0.0 copy-start.1
  10.2 23.4 %conditional.3 = (bf16[2,32,128]{2,1,0:T(8,128)(2,1)S(1)}, bf16[2560,128]{1,0:T(8,128)(2,1)S(1)}, bf16[768,128]{1,0:T(8,128)(2,1)S(1)}, bf16[2,32,128]{2,1,0:T(8,128)(2,1)S(1)}) conditional(s32[]{:T(128)} %convert_element_type.2, bf16[2,1824,128]{2,1,0:T(8,128)(2,1)S(1)} %bitcast.30, (bf16[2,1824,128]{2,1,0:T(8,128)(2,1)S(1)}, ...), branch_computations={%region_0.0_spmd, %region_1.2_spmd} | conditional | flops 2621450 | bytes 8683825 | solution.py:298
  10.2 0.1 level_0.1
  10.4 3.3 %all-gather = bf16[4,32,128]{2,1,0:T(8,128)(2,1)S(1)} all-gather(bf16[2,32,128]{2,1,0:T(8,128)(2,1)S(1)} %level_0.1), channel_id=2, replica_groups={{0,64},{32,96},{128,192},{160,224},{256,320},{288,352},{384,448},{416,4..., dimensions={0}, use_global_device_ids=true | all-gather | bytes 49152 | tf_op jit(solution)/shard_map/cond/branch_0_fun/all_gather | solution.py:18
  13.6 0.1 level_1.1
  13.7 4.8 %all-gather.1 = bf16[4,32,128]{2,1,0:T(8,128)(2,1)S(1)} all-gather(bf16[2,32,128]{2,1,0:T(8,128)(2,1)S(1)} %level_1.1), channel_id=3, replica_groups={{0,128},{32,160},{64,192},{96,224},{256,384},{288,416},{320,448},{352,4..., dimensions={0}, use_global_device_ids=true | all-gather | bytes 49152 | tf_op jit(solution)/shard_map/cond/branch_0_fun/all_gather | solution.py:18
  18.5 0.1 level_2.1
  18.6 7.2 %all-gather.2 = bf16[4,32,128]{2,1,0:T(8,128)(2,1)S(1)} all-gather(bf16[2,32,128]{2,1,0:T(8,128)(2,1)S(1)} %level_2.1), channel_id=4, replica_groups={{0,256},{32,288},{64,320},{96,352},{128,384},{160,416},{192,448},{224,4..., dimensions={0}, use_global_device_ids=true | all-gather | bytes 49152 | tf_op jit(solution)/shard_map/cond/branch_0_fun/all_gather | solution.py:18
  25.8 0.1 level_3.1
  25.9 3.3 %all-gather.3 = bf16[4,32,128]{2,1,0:T(8,128)(2,1)S(1)} all-gather(bf16[2,32,128]{2,1,0:T(8,128)(2,1)S(1)} %level_3.1), channel_id=5, replica_groups={{0,1},{2,3},{4,5},{6,7},{8,9},{10,11},{12,13},{14,15},{16,17},{18,19},{..., dimensions={0}, use_global_device_ids=true | all-gather | bytes 49152 | tf_op jit(solution)/shard_map/cond/branch_0_fun/all_gather | solution.py:18
  29.2 0.1 level_4.1
  29.3 4.2 %all-gather.4 = bf16[4,32,128]{2,1,0:T(8,128)(2,1)S(1)} all-gather(bf16[2,32,128]{2,1,0:T(8,128)(2,1)S(1)} %level_4.1), channel_id=6, replica_groups={{0,2},{1,3},{4,6},{5,7},{8,10},{9,11},{12,14},{13,15},{16,18},{17,19},{..., dimensions={0}, use_global_device_ids=true | all-gather | bytes 49152 | tf_op jit(solution)/shard_map/cond/branch_0_fun/all_gather | solution.py:18
  33.4 0.1 level_5.1
  33.6 1.3 %collective-permute-start.5 = (bf16[2560,128]{1,0:T(8,128)(2,1)S(1)}, bf16[2560,128]{1,0:T(8,128)(2,1)S(1)}, u32[]{:S(2)}, u32[]{:S(2)}) collective-permute-start(bf16[2560,128]{1,0:T(8,128)(2,1)S(1)} %get-tuple-element.78), channel_id=1, source_target_pairs={{0,32},{64,96},{128,160},{192,224},{256,288},{320,352},{384,416},{... | collective-permute-start | bytes 1966088 | tf_op jit(solution)/shard_map/ppermute | solution.py:299
  34.9 7.2 %conditional.4 = (bf16[2,2,32,128]{3,2,1,0:T(8,128)(2,1)S(1)}) conditional(s32[]{:T(128)} %convert_element_type.2, bf16[2,32,128]{2,1,0:T(8,128)(2,1)S(1)} %get-tuple-element.77, bf16[2,32,128]{2,1,0:T(8,128)(2,1)S(1)} %get-tuple-element.77), branch_computations={%region_2.3_spmd, %region_3.4_spmd} | conditional | flops 16384 | bytes 49160 | solution.py:300
  34.9 7.2 %all-gather.5 = bf16[4,32,128]{2,1,0:T(8,128)(2,1)S(1)} all-gather(bf16[2,32,128]{2,1,0:T(8,128)(2,1)S(1)} %param.2), channel_id=7, replica_groups={{0,4},{1,5},{2,6},{3,7},{8,12},{9,13},{10,14},{11,15},{16,20},{17,21},{..., dimensions={0}, use_global_device_ids=true | all-gather | bytes 49152 | tf_op jit(solution)/shard_map/cond/branch_0_fun/all_gather | solution.py:18
  42.1 0.0 collective-permute-done.5
  42.1 0.0 copy-done.1
  42.1 0.0 copy-start
  42.1 9.3 %conditional.5 = (f32[32,1024]{1,0:T(8,128)S(1)}, bf16[32,128]{1,0:T(8,128)(2,1)S(1)}, bf16[32,128]{1,0:T(8,128)(2,1)S(1)}) conditional(s32[]{:T(128)} %convert_element_type.2, (bf16[2,2,32,128]{3,2,1,0:T(8,128)(2,1)S(1)}, bf16[2560,128]{1,0:T(8,128)(2,1)S(1)}, bf16[768,128]{1,0:T(8,128)(2,1)S(1)}, bf16[1,1,8,9,128,128]{5,4,3,2,1,0:T(8,128)(2,1)}, ...), branch_computations={%region_4.5_spmd, %region_5.6_spmd} | conditional | bytes 114752 | solution.py:325
  42.1 0.1 level_6.1
  42.2 3.3 %all-gather.6 = bf16[4,32,128]{2,1,0:T(8,128)(2,1)S(1)} all-gather(bf16[2,32,128]{2,1,0:T(8,128)(2,1)S(1)} %level_6.1), channel_id=8, replica_groups={{0,8},{1,9},{2,10},{3,11},{4,12},{5,13},{6,14},{7,15},{16,24},{17,25},{..., dimensions={0}, use_global_device_ids=true | all-gather | bytes 49152 | tf_op jit(solution)/shard_map/cond/branch_0_fun/all_gather | solution.py:18
  45.5 0.1 level_7.1.coeffs
  45.6 2.3 %collective-permute-start = (bf16[2,32,128]{2,1,0:T(8,128)(2,1)S(1)}, bf16[2,32,128]{2,1,0:T(8,128)(2,1)S(1)}, u32[]{:S(2)}, u32[]{:S(2)}) collective-permute-start(bf16[2,32,128]{2,1,0:T(8,128)(2,1)S(1)} %level_7.1.coeffs), channel_id=1, source_target_pairs={{32,48},{33,49},{34,50},{35,51},{36,52},{37,53},{38,54},{39,55},{4... | collective-permute-start | bytes 49160 | tf_op jit(solution)/shard_map/cond/branch_0_fun/ppermute | solution.py:24
  48.0 3.2 %near_1.1 = f32[32,1024]{1,0:T(8,128)S(1)} custom-call(bf16[2560,128]{1,0:T(8,128)(2,1)S(1)} %get-tuple-element.51.rest_0_.beside.theirs, bf16[2,1824,128]{2,1,0:T(8,128)(2,1)S(1)} %get-tuple-element.52.shared, bf16[9216,128]{1,0:T(8,128)(2,1)} %bitcast.44, s32[8,9]{1,0:T(8,128)S(1)} %get-tuple-element.54.rest_1_), custom_call_target="tpu_custom_call" | custom-call | tf_op jit(solution)/shard_map/cond/branch_0_fun/near_1/pallas_call | solution.py:220
  51.2 0.0 collective-permute-done.others
  51.2 0.1 level_8.1
  51.3 1.8 %all-gather.8 = bf16[64,128]{1,0:T(8,128)(2,1)S(1)} all-gather(bf16[32,128]{1,0:T(8,128)(2,1)S(1)} %get-tuple-element.81), channel_id=10, replica_groups={{0,32},{64,96},{128,160},{192,224},{256,288},{320,352},{384,416},{448,4..., dimensions={0}, use_global_device_ids=true | all-gather | bytes 24576 | tf_op jit(solution)/shard_map/all_gather | solution.py:18
  53.2 0.0 copy-done
  53.2 0.8 %respond.1 = f32[32,1,1,1024]{3,2,1,0:T(1,128)} custom-call(bf16[2,32,128]{2,1,0:T(8,128)(2,1)S(1)} %bitcast.43, bf16[32,128]{1,0:T(8,128)(2,1)S(1)} %get-tuple-element.82.own_final, f32[32,1024]{1,0:T(8,128)S(1)} %get-tuple-element.83.near, bf16[128,1024]{1,0:T(8,128)(2,1)S(1)} %bitcast.34), custom_call_target="tpu_custom_call" | custom-call | tf_op jit(solution)/shard_map/respond/pallas_call | solution.py:255
  (1 shorter events, 0.0 us)
Async XLA Ops:
  10.2 31.8 %copy-start.1 = (s32[1,1,8,9]{3,2,1,0:T(8,128)S(1)}, s32[1,1,8,9]{3,2,1,0:T(8,128)}, u32[]{:S(2)}) copy-start(s32[1,1,8,9]{3,2,1,0:T(8,128)} %param.14) | copy-start | bytes 868
  33.6 8.5 %collective-permute-start.5 = (bf16[2560,128]{1,0:T(8,128)(2,1)S(1)}, bf16[2560,128]{1,0:T(8,128)(2,1)S(1)}, u32[]{:S(2)}, u32[]{:S(2)}) collective-permute-start(bf16[2560,128]{1,0:T(8,128)(2,1)S(1)} %get-tuple-element.78), channel_id=1, source_target_pairs={{0,32},{64,96},{128,160},{192,224},{256,288},{320,352},{384,416},{... | collective-permute-start | bytes 1966088 | tf_op jit(solution)/shard_map/ppermute | solution.py:299
  42.1 11.1 %copy-start = (bf16[1,1,128,1024]{3,2,1,0:T(8,128)(2,1)S(1)}, bf16[1,1,128,1024]{3,2,1,0:T(8,128)(2,1)}, u32[]{:S(2)}) copy-start(bf16[1,1,128,1024]{3,2,1,0:T(8,128)(2,1)} %param.17) | copy-start | bytes 786436
  45.6 5.6 %collective-permute-start = (bf16[2,32,128]{2,1,0:T(8,128)(2,1)S(1)}, bf16[2,32,128]{2,1,0:T(8,128)(2,1)S(1)}, u32[]{:S(2)}, u32[]{:S(2)}) collective-permute-start(bf16[2,32,128]{2,1,0:T(8,128)(2,1)S(1)} %level_7.1.coeffs), channel_id=1, source_target_pairs={{32,48},{33,49},{34,50},{35,51},{36,52},{37,53},{38,54},{39,55},{4... | collective-permute-start | bytes 49160 | tf_op jit(solution)/shard_map/cond/branch_0_fun/ppermute | solution.py:24

commit v14 on v13

--- a/solution.py
+++ b/solution.py
@@ -171,6 +171,9 @@
         kernel,
         name=name,
         compiler_params=GRANT,
+        cost_estimate=pl.CostEstimate(
+            flops=4 * 10**9, bytes_accessed=16 << 20, transcendentals=0
+        ),
         out_shape=out_shape,
         in_specs=[vmem] * len(operands),
         out_specs=jax.tree.map(lambda _: vmem, out_shape),

time: 54.5 us -> 54.2 us (level)
  Pallas kernels: 6.51 us -> 4.85 us
  waiting for transfers between devices: 0.01 us -> 1.47 us
    pallas_call x1, Pallas kernels: 3.2 us -> 1.54 us  [near_of(): pl.pallas_call(functools.partial(near_field, packing, offset), name=f'nea...]
    ppermute x1, waiting for transfers between devices: 0.01 us -> 1.47 us  [partners_of(): return lax.ppermute(values, BOTH, [(i, i ^ 1 << apart) for i in at])]
  transfers between devices with their start and end apart: 2 -> 2, of which waited for: 0 -> 1; matrix products, arithmetic and copies ran while one was open for 0% -> 0% of each run, Pallas kernels for 6% -> 3%
where the time goes in v14:
time: 54.2 us; the launch traced here: 53.9 us
  blocking collectives  43.7 us (81%)
  Pallas kernels  4.85 us (9%)
  starting transfers between devices  3.77 us (7%)
  waiting for transfers between devices  1.47 us (3%)
    all_gather x9, blocking collectives, pair_gather(): return lax.all_gather(values, axis, axis_index_groups=pairs)  43.7 us
    ppermute x1, starting transfers between devices, partners_of(): return lax.ppermute(values, BOTH, [(i, i ^ 1 << apart) for i in at])  2.48 us
    pallas_call x1, Pallas kernels, near_of(): pl.pallas_call(functools.partial(near_field, packing, offset), name=f'nea...  1.54 us
    ppermute x1, waiting for transfers between devices, partners_of(): return lax.ppermute(values, BOTH, [(i, i ^ 1 << apart) for i in at])  1.47 us
    ppermute x1, starting transfers between devices, per_device(): lax.ppermute(given, 'bx', [(i, i ^ 1) for i in range(0, lax.axis_size('bx...  1.29 us
    pallas_call x1, Pallas kernels, packed_own(): pl.pallas_call(functools.partial(pack, packing), name='pack', compiler_pa...  1.28 us
    pallas_call x9, Pallas kernels, in_vmem(): call(*(pltpu.with_memory_space_constraint(x, pltpu.VMEM) for x in operands))  1.18 us
  transfers between devices with their start and end apart: 2, of which 1 were waited for; matrix products, arithmetic and copies ran while one was open for 0% of the time, Pallas kernels for 3%

profile of v14, /device:TPU:1, one launch (start us, length us, event | category | flops | bytes accessed | tf_op | source)
XLA Modules:
  0.0 53.9 jit_solution(12497632687361076646)
XLA Ops:
  0.0 1.3 %pack.1 = (bf16[1824,128]{1,0:T(8,128)(2,1)S(1)}, bf16[768,128]{1,0:T(8,128)(2,1)S(1)}) custom-call(bf16[2304,128]{1,0:T(8,128)(2,1)} %bitcast.47, bf16[32,1024]{1,0:T(8,128)(2,1)} %bitcast.51, bf16[1024,128]{1,0:T(8,128)(2,1)} %bitcast.49), custom_call_target="tpu_custom_call" | custom-call | tf_op jit(solution)/shard_map/pack/pallas_call | solution.py:108
  1.3 8.9 %all-gather.7 = bf16[3648,128]{1,0:T(8,128)(2,1)S(1)} all-gather(bf16[1824,128]{1,0:T(8,128)(2,1)S(1)} %get-tuple-element.75), channel_id=9, replica_groups={{0,32},{64,96},{128,160},{192,224},{256,288},{320,352},{384,416},{448,4..., dimensions={0}, use_global_device_ids=true | all-gather | bytes 1400832 | tf_op jit(solution)/shard_map/all_gather | solution.py:18
  10.2 0.0 copy-start.2
  10.2 23.4 %conditional.3 = (bf16[2,32,128]{2,1,0:T(8,128)(2,1)S(1)}, bf16[2560,128]{1,0:T(8,128)(2,1)S(1)}, bf16[768,128]{1,0:T(8,128)(2,1)S(1)}, bf16[2,32,128]{2,1,0:T(8,128)(2,1)S(1)}) conditional(s32[]{:T(128)} %convert_element_type.2, bf16[2,1824,128]{2,1,0:T(8,128)(2,1)S(1)} %bitcast.30, (bf16[2,1824,128]{2,1,0:T(8,128)(2,1)S(1)}, ...), branch_computations={%region_0.0_spmd, %region_1.2_spmd} | conditional | flops 24000000000 | bytes 100941856 | solution.py:301
  10.2 0.1 level_0.1
  10.4 3.3 %all-gather = bf16[4,32,128]{2,1,0:T(8,128)(2,1)S(1)} all-gather(bf16[2,32,128]{2,1,0:T(8,128)(2,1)S(1)} %level_0.1), channel_id=2, replica_groups={{0,64},{32,96},{128,192},{160,224},{256,320},{288,352},{384,448},{416,4..., dimensions={0}, use_global_device_ids=true | all-gather | bytes 49152 | tf_op jit(solution)/shard_map/cond/branch_0_fun/all_gather | solution.py:18
  13.6 0.1 level_1.1
  13.7 4.8 %all-gather.1 = bf16[4,32,128]{2,1,0:T(8,128)(2,1)S(1)} all-gather(bf16[2,32,128]{2,1,0:T(8,128)(2,1)S(1)} %level_1.1), channel_id=3, replica_groups={{0,128},{32,160},{64,192},{96,224},{256,384},{288,416},{320,448},{352,4..., dimensions={0}, use_global_device_ids=true | all-gather | bytes 49152 | tf_op jit(solution)/shard_map/cond/branch_0_fun/all_gather | solution.py:18
  18.5 0.1 level_2.1
  18.6 7.2 %all-gather.2 = bf16[4,32,128]{2,1,0:T(8,128)(2,1)S(1)} all-gather(bf16[2,32,128]{2,1,0:T(8,128)(2,1)S(1)} %level_2.1), channel_id=4, replica_groups={{0,256},{32,288},{64,320},{96,352},{128,384},{160,416},{192,448},{224,4..., dimensions={0}, use_global_device_ids=true | all-gather | bytes 49152 | tf_op jit(solution)/shard_map/cond/branch_0_fun/all_gather | solution.py:18
  25.8 0.1 level_3.1
  25.9 3.3 %all-gather.3 = bf16[4,32,128]{2,1,0:T(8,128)(2,1)S(1)} all-gather(bf16[2,32,128]{2,1,0:T(8,128)(2,1)S(1)} %level_3.1), channel_id=5, replica_groups={{0,1},{2,3},{4,5},{6,7},{8,9},{10,11},{12,13},{14,15},{16,17},{18,19},{..., dimensions={0}, use_global_device_ids=true | all-gather | bytes 49152 | tf_op jit(solution)/shard_map/cond/branch_0_fun/all_gather | solution.py:18
  29.2 0.1 level_4.1
  29.3 4.2 %all-gather.4 = bf16[4,32,128]{2,1,0:T(8,128)(2,1)S(1)} all-gather(bf16[2,32,128]{2,1,0:T(8,128)(2,1)S(1)} %level_4.1), channel_id=6, replica_groups={{0,2},{1,3},{4,6},{5,7},{8,10},{9,11},{12,14},{13,15},{16,18},{17,19},{..., dimensions={0}, use_global_device_ids=true | all-gather | bytes 49152 | tf_op jit(solution)/shard_map/cond/branch_0_fun/all_gather | solution.py:18
  33.4 0.1 level_5.1
  33.6 1.3 %collective-permute-start.5 = (bf16[2560,128]{1,0:T(8,128)(2,1)S(1)}, bf16[2560,128]{1,0:T(8,128)(2,1)S(1)}, u32[]{:S(2)}, u32[]{:S(2)}) collective-permute-start(bf16[2560,128]{1,0:T(8,128)(2,1)S(1)} %get-tuple-element.78), channel_id=1, source_target_pairs={{0,32},{64,96},{128,160},{192,224},{256,288},{320,352},{384,416},{... | collective-permute-start | bytes 1966088 | tf_op jit(solution)/shard_map/ppermute | solution.py:302
  34.9 7.2 %conditional.4 = (bf16[2,2,32,128]{3,2,1,0:T(8,128)(2,1)S(1)}) conditional(s32[]{:T(128)} %convert_element_type.2, bf16[2,32,128]{2,1,0:T(8,128)(2,1)S(1)} %get-tuple-element.77, bf16[2,32,128]{2,1,0:T(8,128)(2,1)S(1)} %get-tuple-element.77), branch_computations={%region_2.3_spmd, %region_3.4_spmd} | conditional | flops 16384 | bytes 49160 | solution.py:303
  34.9 7.2 %all-gather.5 = bf16[4,32,128]{2,1,0:T(8,128)(2,1)S(1)} all-gather(bf16[2,32,128]{2,1,0:T(8,128)(2,1)S(1)} %param.2), channel_id=7, replica_groups={{0,4},{1,5},{2,6},{3,7},{8,12},{9,13},{10,14},{11,15},{16,20},{17,21},{..., dimensions={0}, use_global_device_ids=true | all-gather | bytes 49152 | tf_op jit(solution)/shard_map/cond/branch_0_fun/all_gather | solution.py:18
  42.1 0.0 collective-permute-done.5
  42.1 0.0 copy-done.2
  42.1 0.0 copy-start
  42.1 9.2 %conditional.5 = (f32[32,1024]{1,0:T(8,128)S(1)}, bf16[32,128]{1,0:T(8,128)(2,1)S(1)}, bf16[32,128]{1,0:T(8,128)(2,1)S(1)}) conditional(s32[]{:T(128)} %convert_element_type.2, (bf16[2,2,32,128]{3,2,1,0:T(8,128)(2,1)S(1)}, bf16[2560,128]{1,0:T(8,128)(2,1)S(1)}, bf16[768,128]{1,0:T(8,128)(2,1)S(1)}, bf16[1,1,8,9,128,128]{5,4,3,2,1,0:T(8,128)(2,1)}, ...), branch_computations={%region_4.5_spmd, %region_5.6_spmd} | conditional | flops 12000000000 | bytes 59883612 | solution.py:328
  42.1 0.1 level_6.1
  42.2 3.3 %all-gather.6 = bf16[4,32,128]{2,1,0:T(8,128)(2,1)S(1)} all-gather(bf16[2,32,128]{2,1,0:T(8,128)(2,1)S(1)} %level_6.1), channel_id=8, replica_groups={{0,8},{1,9},{2,10},{3,11},{4,12},{5,13},{6,14},{7,15},{16,24},{17,25},{..., dimensions={0}, use_global_device_ids=true | all-gather | bytes 49152 | tf_op jit(solution)/shard_map/cond/branch_0_fun/all_gather | solution.py:18
  45.5 0.0 copy-start.1
  45.5 0.1 level_7.1.coeffs
  45.6 2.5 %collective-permute-start = (bf16[2,32,128]{2,1,0:T(8,128)(2,1)S(1)}, bf16[2,32,128]{2,1,0:T(8,128)(2,1)S(1)}, u32[]{:S(2)}, u32[]{:S(2)}) collective-permute-start(bf16[2,32,128]{2,1,0:T(8,128)(2,1)S(1)} %level_7.1.coeffs), channel_id=1, source_target_pairs={{32,48},{33,49},{34,50},{35,51},{36,52},{37,53},{38,54},{39,55},{4... | collective-permute-start | bytes 49160 | tf_op jit(solution)/shard_map/cond/branch_0_fun/ppermute | solution.py:24
  48.1 0.0 copy-done.1
  48.1 1.5 %near_1.1 = f32[32,1024]{1,0:T(8,128)S(1)} custom-call(bf16[2560,128]{1,0:T(8,128)(2,1)S(1)} %get-tuple-element.51.rest_0_.beside.theirs, bf16[2,1824,128]{2,1,0:T(8,128)(2,1)S(1)} %get-tuple-element.52.shared, bf16[9216,128]{1,0:T(8,128)(2,1)S(1)} %bitcast.44, s32[8,9]{1,0:T(8,128)S(1)} %get-tuple-element.54.rest_1_), custom_call_target="tpu_custom_call" | custom-call | tf_op jit(solution)/shard_map/cond/branch_0_fun/near_1/pallas_call | solution.py:223
  49.7 1.5 %collective-permute-done.others = bf16[2,32,128]{2,1,0:T(8,128)(2,1)S(1)} collective-permute-done((bf16[2,32,128]{2,1,0:T(8,128)(2,1)S(1)}, bf16[2,32,128]{2,1,0:T(8,128)(2,1)S(1)}, u32[]{:S(2)}, u32[]{:S(2)}) %collective-permute-start) | collective-permute-done | bytes 16416 | tf_op jit(solution)/shard_map/cond/branch_0_fun/ppermute | solution.py:24
  51.1 0.1 level_8.1
  51.3 1.8 %all-gather.8 = bf16[64,128]{1,0:T(8,128)(2,1)S(1)} all-gather(bf16[32,128]{1,0:T(8,128)(2,1)S(1)} %get-tuple-element.81), channel_id=10, replica_groups={{0,32},{64,96},{128,160},{192,224},{256,288},{320,352},{384,416},{448,4..., dimensions={0}, use_global_device_ids=true | all-gather | bytes 24576 | tf_op jit(solution)/shard_map/all_gather | solution.py:18
  53.1 0.0 copy-done
  53.1 0.8 %respond.1 = f32[32,1,1,1024]{3,2,1,0:T(1,128)} custom-call(bf16[2,32,128]{2,1,0:T(8,128)(2,1)S(1)} %bitcast.36, bf16[32,128]{1,0:T(8,128)(2,1)S(1)} %get-tuple-element.82.own_final, f32[32,1024]{1,0:T(8,128)S(1)} %get-tuple-element.83.near, bf16[128,1024]{1,0:T(8,128)(2,1)S(1)} %bitcast.34), custom_call_target="tpu_custom_call" | custom-call | tf_op jit(solution)/shard_map/respond/pallas_call | solution.py:258
  (1 shorter events, 0.0 us)
Async XLA Ops:
  10.2 31.8 %copy-start.2 = (s32[1,1,8,9]{3,2,1,0:T(8,128)S(1)}, s32[1,1,8,9]{3,2,1,0:T(8,128)}, u32[]{:S(2)}) copy-start(s32[1,1,8,9]{3,2,1,0:T(8,128)} %param.14) | copy-start | bytes 868
  33.6 8.5 %collective-permute-start.5 = (bf16[2560,128]{1,0:T(8,128)(2,1)S(1)}, bf16[2560,128]{1,0:T(8,128)(2,1)S(1)}, u32[]{:S(2)}, u32[]{:S(2)}) collective-permute-start(bf16[2560,128]{1,0:T(8,128)(2,1)S(1)} %get-tuple-element.78), channel_id=1, source_target_pairs={{0,32},{64,96},{128,160},{192,224},{256,288},{320,352},{384,416},{... | collective-permute-start | bytes 1966088 | tf_op jit(solution)/shard_map/ppermute | solution.py:302
  42.1 11.0 %copy-start = (bf16[1,1,128,1024]{3,2,1,0:T(8,128)(2,1)S(1)}, bf16[1,1,128,1024]{3,2,1,0:T(8,128)(2,1)}, u32[]{:S(2)}) copy-start(bf16[1,1,128,1024]{3,2,1,0:T(8,128)(2,1)} %param.17) | copy-start | bytes 786436
  45.5 2.6 %copy-start.1 = (bf16[1,1,8,9,128,128]{5,4,3,2,1,0:T(8,128)(2,1)S(1)}, bf16[1,1,8,9,128,128]{5,4,3,2,1,0:T(8,128)(2,1)}, u32[]{:S(2)}) copy-start(bf16[1,1,8,9,128,128]{5,4,3,2,1,0:T(8,128)(2,1)} %get-tuple-element.53) | copy-start | bytes 7077892 | tf_op jit(solution)/shard_map/cond
  45.6 5.5 %collective-permute-start = (bf16[2,32,128]{2,1,0:T(8,128)(2,1)S(1)}, bf16[2,32,128]{2,1,0:T(8,128)(2,1)S(1)}, u32[]{:S(2)}, u32[]{:S(2)}) collective-permute-start(bf16[2,32,128]{2,1,0:T(8,128)(2,1)S(1)} %level_7.1.coeffs), channel_id=1, source_target_pairs={{32,48},{33,49},{34,50},{35,51},{36,52},{37,53},{38,54},{39,55},{4... | collective-permute-start | bytes 49160 | tf_op jit(solution)/shard_map/cond/branch_0_fun/ppermute | solution.py:24
